TPU v7x, 256 devices: a whole 4x4x8 slice. The times are simulated.
256 devices in a mesh: ply: 2 (over x_hi), gx: 8 (over y, core), gy: 16 (over z, x_lo).
Axes of the slice: x: 4 (x_hi: 2, x_lo: 2; x = x_hi * 2 + x_lo), y: 4, z: 8, core: 2. Of those that a mesh axis runs over, the one named last changes fastest.
Arguments:
- coords: float32 [3, 2, 48, 96, 128], P(None, 'ply', 'gx', 'gy'), may hold values from 0 to 1
- strain: float32 [2, 48, 96, 128], P('ply', 'gx', 'gy'), may hold values from 0.1 to 10.1
- kappa_old: float32 [2, 48, 96, 128], P('ply', 'gx', 'gy'), may hold values from 1 to 3
- counts: int32 [2, 48, 96], P('ply', 'gx', 'gy'), may hold values from 0 to 128, as said below
- pair_mask: int32 [2, 48, 96, 26], P('ply', 'gx', 'gy'), may hold values from 0 to 1, as said below
Outputs:
- kappa_new: float32 [2, 48, 96, 128], P('ply', 'gx', 'gy')
- damage: float32 [2, 48, 96, 128], P('ply', 'gx', 'gy')
Inputs may be any that keep to these rules, and one draw needn't show every extreme that they name: `counts`: blocks whose count is 0 form the plate's hole, the same through the thickness. pair_mask[a, k] equals pair_mask[a + o_k, 25 - k], o_k being the k-th offset, wherever both blocks lie in the grid.
All inputs are finite; a program needn't handle non-finite values.
Results may differ from a plain program's by a relative error of at most 0.0003.
Values sent between devices are 32-bit elements; how exact they have to be, the bound alone decides.
No kernel may reach another device: no remote copies, remote signals or barrier semaphores. Data moves between devices by JAX's collectives and lax.ppermute only.
A program may use at most 64 MiB of HBM per device.

v0:
```python
import jax
import jax.numpy as jnp
from jax import lax
from jax.sharding import PartitionSpec as P


def padded_2(block, sides, width):
    for axis, dim in sides:
        count = lax.axis_size(axis)
        forward = [(i, i + 1) for i in range(count - 1)]
        backward = [(target, source) for source, target in forward]
        low = lax.ppermute(
            lax.slice_in_dim(block, block.shape[dim] - width, None, axis=dim), axis, forward
        )
        high = lax.ppermute(lax.slice_in_dim(block, 0, width, axis=dim), axis, backward)
        block = jnp.concatenate([low, block, high], axis=dim)
    return block


def make_offsets():
    listed = []
    for first in (-1, 0, 1):
        for second in (-1, 0, 1):
            for third in (-1, 0, 1):
                listed.append((first, second, third))
    return listed


def bell_weights(center, beside, offset):
    squared = jnp.zeros((center.shape[1], center.shape[2], center.shape[2]), jnp.float32)
    for comp in range(3):
        gap = offset[comp] + beside[comp][:, None, :] - center[comp][:, :, None]
        squared = squared + gap * gap
    return jnp.square(jnp.maximum(0.0, 1.0 - squared))


def on_device(coords, strain, kappa_old, counts, pair_mask):
    every_offset = make_offsets()
    layer_count, strip_count, block_count, point_count = strain.shape
    slots = lax.broadcasted_iota(jnp.int32, strain.shape, 3)
    active = (slots < counts[..., None]).astype(jnp.float32)
    payload = jnp.concatenate([coords, (strain * active)[None], active[None]], 0)

    def locate(padded, row_at):
        zero = row_at * 0
        layer_at = row_at // strip_count
        strip_at = row_at % strip_count
        window = lax.dynamic_slice(
            padded, (zero, layer_at, strip_at, zero, zero), (5, 3, 3, block_count + 2, point_count)
        )
        pair_flags = lax.dynamic_slice(
            pair_mask, (layer_at, strip_at, zero, zero), (1, 1, block_count, 26)
        )[0, 0].astype(jnp.float32)
        return (zero, layer_at, strip_at, window, pair_flags)

    def neighbour(window, offset):
        return window[:, 1 + offset[0], 1 + offset[1], 1 + offset[2] : 1 + offset[2] + block_count]

    rows_all = jnp.arange(layer_count * strip_count, dtype=jnp.int32)
    padded = padded_2(payload, (("ply", 1), ("gx", 2), ("gy", 3)), 1)

    def one_row(row_at):
        zero, layer_at, strip_at, window, pair_flags = locate(padded, row_at)
        center = window[:, 1, 1, 1 : block_count + 1]
        totals = jnp.zeros((2, block_count, point_count), jnp.float32)
        for which, offset in enumerate(every_offset):
            beside = neighbour(window, offset)
            weights = bell_weights(center, beside, offset)
            term = jnp.einsum("bij,cbj->cbi", weights, beside[3:5], precision=lax.Precision.HIGHEST)
            if offset != (0, 0, 0):
                flag_at = which if which < 13 else which - 1
                term = term * pair_flags[:, flag_at][None, :, None]
            totals = totals + term
        return totals

    totals = lax.map(one_row, rows_all)
    totals = totals.reshape(layer_count, strip_count, 2, block_count, point_count).transpose(
        2, 0, 1, 3, 4
    )
    weighted, weight_sum = (totals[0], totals[1])
    averaged = active * weighted / (weight_sum + 1.0 - active)
    highest = lax.pmax(jnp.max(averaged), ("ply", "gx", "gy")) + 1e-06
    kappa_new = jnp.maximum(kappa_old, 4.0 * averaged / highest)
    damage = active * (1.0 - jnp.exp(-(kappa_new - 1.0) / 2.5) / kappa_new)
    return (kappa_new, damage)


def solution(mesh):
    placed = (
        P(None, "ply", "gx", "gy", None),
        P("ply", "gx", "gy", None),
        P("ply", "gx", "gy", None),
        P("ply", "gx", "gy"),
        P("ply", "gx", "gy", None),
    )
    return jax.shard_map(
        on_device,
        mesh=mesh,
        in_specs=placed,
        out_specs=(P("ply", "gx", "gy", None), P("ply", "gx", "gy", None)),
        check_vma=False,
    )
```

profile of v0, /device:TPU:1, one launch (start us, length us, event | category | flops | bytes accessed | tf_op | source)
XLA Modules:
  0.0 296.9 jit_solution(11097235214040952848)
XLA Ops:
  2.4 5.5 %collective-permute-start = (f32[5,1,6,6,128]{4,0,3,2,1:T(8,128)S(1)}, f32[5,1,6,6,128]{4,0,3,2,1:T(8,128)S(1)}, u32[]{:S(2)}, u32[]{:S(2)}) collective-permute-start(f32[5,1,6,6,128]{4,0,3,2,1:T(8,128)S(1)} %pad_maximum_fusion.1), channel_id=1, source_target_pairs={{0,128},{1,129},{2,130},{3,131},{4,132},{5,133},{6,134},{7,135},{8... | collective-permute-start | bytes 276488 | tf_op jit(solution)/shard_map/ppermute | solution.py:12
  7.9 1.3 collective-permute-start.1
  9.2 1.2 collective-permute-done
  10.4 5.3 %collective-permute-done.1 = f32[5,1,6,6,128]{4,0,3,2,1:T(8,128)S(1)} collective-permute-done((f32[5,1,6,6,128]{4,0,3,2,1:T(8,128)S(1)}, f32[5,1,6,6,128]{4,0,3,2,1:T(8,128)S(1)}, u32[]{:S(2)}, u32[]{:S(2)}) %collective-permute-start.1) | collective-permute-done | bytes 92192 | tf_op jit(solution)/shard_map/ppermute | solution.py:15
  15.8 4.9 %collective-permute-start.2 = (f32[5,3,1,6,128]{4,0,3,2,1:T(8,128)S(1)}, f32[5,3,1,6,128]{4,0,3,2,1:T(8,128)S(1)}, u32[]{:S(2)}, u32[]{:S(2)}) collective-permute-start(f32[5,3,1,6,128]{4,0,3,2,1:T(8,128)S(1)} %get-tuple-element.277), channel_id=1, source_target_pairs={{0,16},{16,32},{32,48},{48,64},{64,80},{80,96},{96,112},{1,17},{17... | collective-permute-start | bytes 138248 | tf_op jit(solution)/shard_map/ppermute | solution.py:12
  20.7 1.9 collective-permute-start.3
  22.6 3.7 %collective-permute-done.3 = f32[5,3,1,6,128]{4,0,3,2,1:T(8,128)S(1)} collective-permute-done((f32[5,3,1,6,128]{4,0,3,2,1:T(8,128)S(1)}, f32[5,3,1,6,128]{4,0,3,2,1:T(8,128)S(1)}, u32[]{:S(2)}, u32[]{:S(2)}) %collective-permute-start.3) | collective-permute-done | bytes 46112 | tf_op jit(solution)/shard_map/ppermute | solution.py:15
  26.4 2.2 collective-permute-start.4
  28.6 1.3 collective-permute-start.5
  30.2 4.8 %collective-permute-done.5 = f32[5,3,8,1,128]{4,0,3,2,1:T(8,128)S(1)} collective-permute-done((f32[5,3,8,1,128]{4,0,3,2,1:T(8,128)S(1)}, f32[5,3,8,1,128]{4,0,3,2,1:T(8,128)S(1)}, u32[]{:S(2)}, u32[]{:S(2)}) %collective-permute-start.5) | collective-permute-done | bytes 61472 | tf_op jit(solution)/shard_map/ppermute | solution.py:15
  35.1 179.9 %while.12 = (s32[]{:T(128)}, f32[6,2,6,128]{3,1,2,0:T(2,128)S(1)}, s32[6]{0:T(128)S(1)}, f32[5,3,8,8,128]{4,0,3,2,1:T(8,128)S(1)}, s32[1,6,6,26]{3,0,2,1:T(1,128...) while((s32[]{:T(128)}, f32[6,2,6,128]{3,1,2,0:T(2,128)S(1)}, ...), condition=%wide.region_1.2_spmd, body=%wide.region_0.1_spmd.sunk | while | flops 93018800 | bytes 2169382 | solution.py:76
  39.9 1.0 convolution_multiply_fusion.51
  43.9 1.0 convolution_multiply_fusion.47
  45.9 1.0 convolution_multiply_fusion.45
  47.9 1.0 convolution_multiply_fusion.43
  50.0 1.0 fusion.854
  53.0 1.0 fusion.853
  57.0 1.0 fusion.849
  59.1 1.0 fusion.847
  61.1 1.0 fusion.845
  63.1 1.0 fusion.843
  64.1 1.0 fusion.855
  69.8 1.0 convolution_multiply_fusion.51
  71.9 1.0 convolution_multiply_fusion.49
  73.9 1.0 convolution_multiply_fusion.47
  75.9 1.0 convolution_multiply_fusion.45
  77.9 1.0 convolution_multiply_fusion.43
  80.0 1.0 fusion.854
  83.0 1.0 fusion.853
  85.0 1.0 fusion.851
  89.0 1.0 fusion.847
  91.1 1.0 fusion.845
  93.1 1.0 fusion.843
  94.1 1.0 fusion.855
  99.8 1.0 convolution_multiply_fusion.51
  101.9 1.0 convolution_multiply_fusion.49
  105.9 1.0 convolution_multiply_fusion.45
  109.9 1.0 fusion.854
  113.0 1.0 fusion.853
  115.0 1.0 fusion.851
  117.0 1.0 fusion.849
  119.0 1.0 fusion.847
  121.1 1.0 fusion.845
  124.1 1.0 fusion.855
  129.8 1.0 convolution_multiply_fusion.51
  133.9 1.0 convolution_multiply_fusion.47
  137.9 1.0 convolution_multiply_fusion.43
  139.9 1.0 fusion.854
  143.0 1.0 fusion.853
  147.0 1.0 fusion.849
  149.0 1.0 fusion.847
  151.0 1.0 fusion.845
  153.1 1.0 fusion.843
  154.1 1.0 fusion.855
  161.8 1.0 convolution_multiply_fusion.49
  163.9 1.0 convolution_multiply_fusion.47
  165.9 1.0 convolution_multiply_fusion.45
  167.9 1.0 convolution_multiply_fusion.43
  169.9 1.0 fusion.854
  173.0 1.0 fusion.853
  184.1 1.0 fusion.855
  199.9 1.0 fusion.854
  214.0 1.0 fusion.855
  215.8 79.7 %pmax.7 = f32[]{:T(128)} all-reduce(f32[]{:T(128)} %get-tuple-element.86), channel_id=1, replica_groups=mesh['ply'=2,'gx'=8,'gy'=16] {'ply','gx','gy'}, use_global_device_ids=true, to_apply=%region_3.4 | all-reduce | flops 1 | bytes 8 | tf_op jit(solution)/shard_map/pmax | solution.py:82
  (416 shorter events, 126.3 us)
Async XLA Ops:
  0.6 1.7 copy-start
  2.4 8.0 %collective-permute-start = (f32[5,1,6,6,128]{4,0,3,2,1:T(8,128)S(1)}, f32[5,1,6,6,128]{4,0,3,2,1:T(8,128)S(1)}, u32[]{:S(2)}, u32[]{:S(2)}) collective-permute-start(f32[5,1,6,6,128]{4,0,3,2,1:T(8,128)S(1)} %pad_maximum_fusion.1), channel_id=1, source_target_pairs={{0,128},{1,129},{2,130},{3,131},{4,132},{5,133},{6,134},{7,135},{8... | collective-permute-start | bytes 276488 | tf_op jit(solution)/shard_map/ppermute | solution.py:12
  7.9 7.9 %collective-permute-start.1 = (f32[5,1,6,6,128]{4,0,3,2,1:T(8,128)S(1)}, f32[5,1,6,6,128]{4,0,3,2,1:T(8,128)S(1)}, u32[]{:S(2)}, u32[]{:S(2)}) collective-permute-start(f32[5,1,6,6,128]{4,0,3,2,1:T(8,128)S(1)} %pad_maximum_fusion.1), channel_id=1, source_target_pairs={{128,0},{129,1},{130,2},{131,3},{132,4},{133,5},{134,6},{135,7},{1... | collective-permute-start | bytes 276488 | tf_op jit(solution)/shard_map/ppermute | solution.py:15
  15.8 6.8 %collective-permute-start.2 = (f32[5,3,1,6,128]{4,0,3,2,1:T(8,128)S(1)}, f32[5,3,1,6,128]{4,0,3,2,1:T(8,128)S(1)}, u32[]{:S(2)}, u32[]{:S(2)}) collective-permute-start(f32[5,3,1,6,128]{4,0,3,2,1:T(8,128)S(1)} %get-tuple-element.277), channel_id=1, source_target_pairs={{0,16},{16,32},{32,48},{48,64},{64,80},{80,96},{96,112},{1,17},{17... | collective-permute-start | bytes 138248 | tf_op jit(solution)/shard_map/ppermute | solution.py:12
  20.7 5.7 %collective-permute-start.3 = (f32[5,3,1,6,128]{4,0,3,2,1:T(8,128)S(1)}, f32[5,3,1,6,128]{4,0,3,2,1:T(8,128)S(1)}, u32[]{:S(2)}, u32[]{:S(2)}) collective-permute-start(f32[5,3,1,6,128]{4,0,3,2,1:T(8,128)S(1)} %get-tuple-element.278), channel_id=1, source_target_pairs={{16,0},{32,16},{48,32},{64,48},{80,64},{96,80},{112,96},{17,1},{33... | collective-permute-start | bytes 138248 | tf_op jit(solution)/shard_map/ppermute | solution.py:15
  26.4 3.8 %collective-permute-start.4 = (f32[5,3,8,1,128]{4,0,3,2,1:T(8,128)S(1)}, f32[5,3,8,1,128]{4,0,3,2,1:T(8,128)S(1)}, u32[]{:S(2)}, u32[]{:S(2)}) collective-permute-start(f32[5,3,8,1,128]{4,0,3,2,1:T(8,128)S(1)} %get-tuple-element.275), channel_id=1, source_target_pairs={{0,1},{1,2},{2,3},{3,4},{4,5},{5,6},{6,7},{7,8},{8,9},{9,10},{10,1... | collective-permute-start | bytes 184328 | tf_op jit(solution)/shard_map/ppermute | solution.py:12
  28.6 6.4 %collective-permute-start.5 = (f32[5,3,8,1,128]{4,0,3,2,1:T(8,128)S(1)}, f32[5,3,8,1,128]{4,0,3,2,1:T(8,128)S(1)}, u32[]{:S(2)}, u32[]{:S(2)}) collective-permute-start(f32[5,3,8,1,128]{4,0,3,2,1:T(8,128)S(1)} %get-tuple-element.276), channel_id=1, source_target_pairs={{1,0},{2,1},{3,2},{4,3},{5,4},{6,5},{7,6},{8,7},{9,8},{10,9},{11,1... | collective-permute-start | bytes 184328 | tf_op jit(solution)/shard_map/ppermute | solution.py:15
  215.1 81.1 %copy-start.1 = (f32[1,6,6,128]{3,0,2,1:T(1,128)S(1)}, f32[1,6,6,128]{3,0,2,1:T(1,128)}, u32[]{:S(2)}) copy-start(f32[1,6,6,128]{3,0,2,1:T(1,128)} %param.9) | copy-start | bytes 55300
where the time goes:
time: 298 us; the launch traced here: 297 us
  matrix products  163 us (55%)
  blocking collectives  79.7 us (27%)
  starting transfers between devices  17.1 us (6%)
  waiting for transfers between devices  15.4 us (5%)
  local copies, waits for them, and re-layouts  9.74 us (3%)
  other arithmetic  6.04 us (2%)
  loops' own time  4.77 us (2%)
    dot_general x162, matrix products, one_row(): jnp.einsum('bij,cbj->cbi', weights, beside[3:5], precision=lax.Precision....  163 us
    pmax x1, blocking collectives, on_device(): highest = lax.pmax(jnp.max(averaged), ('ply', 'gx', 'gy')) + 1e-06  79.7 us
    ppermute x3, waiting for transfers between devices, padded_2(): lax.ppermute(lax.slice_in_dim(block, 0, width, axis=dim), axis, backward)  13.9 us
    ppermute x3, starting transfers between devices, padded_2(): lax.ppermute(lax.slice_in_dim(block, block.shape[dim] - width, None, axis...  12.6 us
  transfers between devices with their start and end apart: 6, of which 5 were waited for; matrix products, arithmetic and copies ran while one was open for 0% of the time, Pallas kernels for 0%

commit v1 on v0

v1 whole, which is shorter than its diff:
```python
import jax
import jax.numpy as jnp
from jax import lax
from jax.experimental import pallas as pl
from jax.experimental.pallas import tpu as pltpu
from jax.sharding import Mesh
from jax.sharding import PartitionSpec as P

BX = 6
BY = 6
PTS = 128
K = 32
WX = BX + 2
WY = BY + 2
AXES = ("ply", "y", "core", "z", "xlo")
F32 = jnp.float32
BF16 = jnp.bfloat16


def split2(v):
    high = v.astype(BF16).astype(F32)
    return high, (v - high).astype(BF16).astype(F32)


def split3(v):
    high, rest = v.astype(BF16).astype(F32), None
    rest = v - high
    mid = rest.astype(BF16).astype(F32)
    return high, mid, rest - mid


def window_kernel(
    shift_ref, flag_ref, own_ref, other_ref, xlo_ref, xhi_ref, ylo_ref, yhi_ref, avg_ref, top_ref, feat, cent, rows, bfeat, bcent, acc
):
    feat[...] = jnp.zeros_like(feat)
    cent[...] = jnp.zeros_like(cent)
    rows[...] = jnp.zeros_like(rows)
    shift = shift_ref[0]

    def emit(parts, strain, layer, x_at, y_at, base, stride, own_base):
        count = strain.shape[0]
        z_at = shift if layer else 0.0
        pos = (parts[0] + (z_at - 0.5), parts[1] + x_at, parts[2] + y_at)
        pieces = [split2(p) for p in pos]
        norm = jnp.zeros_like(strain)
        for high, low in pieces:
            p = high + low
            norm = norm + p * p
        highs = [p[0] for p in pieces]
        lows = [p[1] for p in pieces]
        one = jnp.ones_like(strain)
        listed = highs + lows + highs + lows + list(split3(1.0 - norm)) + [one] * 3
        for k, v in enumerate(listed):
            feat[pl.ds(base * K + k, count, stride=stride * K), :] = v
        live = jnp.where(strain > 0.0, 1.0, 0.0)
        for k, v in enumerate(list(split3(strain)) + [live]):
            rows[pl.ds(base * 8 + k, count, stride=stride * 8), :] = v
        if own_base is not None:
            highs = [2.0 * v for v in highs]
            lows = [2.0 * v for v in lows]
            listed = highs + highs + lows + lows + [one] * 3 + list(split3(-norm))
            for k, v in enumerate(listed):
                cent[pl.ds(own_base * K + k, count, stride=K), :] = v

    y_in = lax.broadcasted_iota(jnp.int32, (BY, PTS), 0).astype(F32) - (BY // 2)
    x_in = lax.broadcasted_iota(jnp.int32, (WX, PTS), 0).astype(F32) - (WX // 2)
    for layer, ref in enumerate((own_ref, other_ref)):
        for x in range(BX):
            emit(
                [ref[c, x] for c in range(3)], ref[3, x], layer, float(x - BX // 2), y_in,
                layer * WX * WY + (x + 1) * WY + 1, 1, x * BY if layer == 0 else None,
            )
        for ref2, x in ((xlo_ref, -1), (xhi_ref, BX)):
            emit(
                [ref2[layer * 4 + c] for c in range(3)], ref2[layer * 4 + 3], layer, float(x - BX // 2), y_in,
                layer * WX * WY + (x + 1) * WY + 1, 1, None,
            )
        for ref2, y in ((ylo_ref, -1), (yhi_ref, BY)):
            emit(
                [ref2[layer * 4 + c] for c in range(3)], ref2[layer * 4 + 3], layer, x_in, float(y - BY // 2),
                layer * WX * WY + y + 1, WY, None,
            )

    def to_bf16(b, carry):
        bfeat[b] = feat[pl.ds(pl.multiple_of(b * K, K), K), :].astype(BF16)
        return carry

    lax.fori_loop(0, 2 * WX * WY, to_bf16, 0, unroll=8)

    def turn(a, carry):
        bcent[a] = cent[pl.ds(pl.multiple_of(a * K, K), K), :].T.astype(BF16)
        return carry

    lax.fori_loop(0, BX * BY, turn, 0, unroll=4)

    window = [(layer, dx, dy) for layer in (0, 1) for dx in (0, 1, 2) for dy in (0, 1, 2)]

    def block(a, carry):
        base = (a // BY) * WY + a % BY
        center = bcent[a]
        total = jnp.zeros((8, PTS), F32)
        for t in range(0, 18, 2):
            at = [layer * WX * WY + dx * WY + dy + base for layer, dx, dy in window[t : t + 2]]
            rhs = jnp.concatenate([bfeat[b] for b in at], axis=1)
            gap = jnp.dot(center, rhs, preferred_element_type=F32)
            w = jnp.maximum(gap, 0.0)
            w = w * w
            high = w.astype(BF16)
            low = (w - high.astype(F32)).astype(BF16)
            lhs = jnp.concatenate(
                [rows[pl.ds(pl.multiple_of(b * 8, 8), 8), :] * flag_ref[a * 18 + t + n] for n, b in enumerate(at)], axis=1
            ).astype(BF16)
            for piece in (high, low):
                total = total + lax.dot_general(lhs, piece, (((1,), (1,)), ((), ())), preferred_element_type=F32)
        acc[pl.ds(pl.multiple_of(a * 8, 8), 8), :] = total
        return carry

    lax.fori_loop(0, BX * BY, block, 0)

    top = jnp.zeros((BY, PTS), F32)
    for x in range(BX):
        s = [acc[pl.ds(x * BY * 8 + k, BY, stride=8), :] for k in range(4)]
        live = jnp.where(own_ref[3, x] > 0.0, 1.0, 0.0)
        averaged = live * (s[0] + s[1] + s[2]) / (s[3] + 1.0 - live)
        avg_ref[x] = averaged
        top = jnp.maximum(top, averaged)
    top_ref[...] = jnp.max(top, axis=0, keepdims=True)


def window_sums(shift, flags, own, other, xlo, xhi, ylo, yhi, interpret=False):
    vm = pl.BlockSpec(memory_space=pltpu.VMEM)
    sm = pl.BlockSpec(memory_space=pltpu.SMEM)
    return pl.pallas_call(
        window_kernel,
        out_shape=(jax.ShapeDtypeStruct((BX, BY, PTS), F32), jax.ShapeDtypeStruct((1, PTS), F32)),
        in_specs=[sm, sm] + [vm] * 6,
        out_specs=(vm, vm),
        scratch_shapes=[
            pltpu.VMEM((2 * WX * WY * K, PTS), F32),
            pltpu.VMEM((BX * BY * K, PTS), F32),
            pltpu.VMEM((2 * WX * WY * 8, PTS), F32),
            pltpu.VMEM((2 * WX * WY, K, PTS), BF16),
            pltpu.VMEM((BX * BY, PTS, K), BF16),
            pltpu.VMEM((BX * BY * 8, PTS), F32),
        ],
        name="window_sums",
        interpret=interpret,
    )(shift, flags, own, other, xlo, xhi, ylo, yhi)


def on_device(coords, strain, kappa_old, counts, pair_mask):
    ply = lax.axis_index("ply")
    slots = lax.broadcasted_iota(jnp.int32, (BX, BY, PTS), 2)
    active = slots < counts[0][..., None]
    own = jnp.concatenate([coords[:, 0], jnp.where(active, strain[0], 0.0)[None]], 0)
    other = lax.ppermute(own, "ply", [(0, 1), (1, 0)])

    gx = ("y", "core")
    gy = ("z", "xlo")
    up = lambda n: [(i, i + 1) for i in range(n - 1)]
    down = lambda n: [(i + 1, i) for i in range(n - 1)]
    xlo = lax.ppermute(jnp.concatenate([own[:, BX - 1], other[:, BX - 1]], 0), gx, up(8))
    xhi = lax.ppermute(jnp.concatenate([own[:, 0], other[:, 0]], 0), gx, down(8))

    def column(y):
        inner = jnp.concatenate([own[:, :, y], other[:, :, y]], 0)
        return jnp.concatenate([xlo[:, y][:, None], inner, xhi[:, y][:, None]], 1)

    ylo = lax.ppermute(column(BY - 1), gy, up(16))
    yhi = lax.ppermute(column(0), gy, down(16))

    flags = pair_mask[0]
    flags = jnp.concatenate(
        [flags[..., 9:13], jnp.ones_like(flags[..., :1]), flags[..., 13:17], jnp.where(ply == 0, flags[..., 17:26], flags[..., 0:9])],
        -1,
    ).astype(F32)
    shift = (1.0 - 2.0 * ply.astype(F32)).reshape(1)
    averaged, top = window_sums(shift, flags.reshape(-1), own, other, xlo, xhi, ylo, yhi)

    spread = lax.all_to_all(
        jnp.broadcast_to(top, (128, PTS)), ("ply", "y", "z", "xlo"), 0, 0, tiled=True
    )
    top = jnp.max(spread, axis=0, keepdims=True)
    top = jnp.maximum(top, lax.ppermute(top, "core", [(0, 1), (1, 0)]))
    highest = jnp.max(top) + 1e-06
    kappa_new = jnp.maximum(kappa_old, 4.0 * averaged[None] / highest)
    damage = active[None].astype(F32) * (1.0 - jnp.exp(-(kappa_new - 1.0) / 2.5) / kappa_new)
    return (kappa_new, damage)


def solution(mesh):
    fine = Mesh(mesh.devices.reshape(2, 4, 2, 8, 2), AXES)
    gx, gy = ("y", "core"), ("z", "xlo")
    placed = (
        P(None, "ply", gx, gy, None),
        P("ply", gx, gy, None),
        P("ply", gx, gy, None),
        P("ply", gx, gy),
        P("ply", gx, gy, None),
    )
    return jax.shard_map(
        on_device,
        mesh=fine,
        in_specs=placed,
        out_specs=(P("ply", gx, gy, None), P("ply", gx, gy, None)),
        check_vma=False,
    )
```

time: 298 us -> 119 us (0.40)
  matrix products: 163 us -> 0 us
  Pallas kernels: 0 us -> 56.2 us
  blocking collectives: 79.7 us -> 28.4 us
  waiting for transfers between devices: 15.4 us -> 5.4 us
  other arithmetic: 6.04 us -> 1.13 us
  loops' own time: 4.77 us -> 0 us
    dot_general x162 -> x0, matrix products: 163 us -> none  [one_row(): jnp.einsum('bij,cbj->cbi', weights, beside[3:5], precision=lax.Precision....]
    pmax x1 -> x0, blocking collectives: 79.7 us -> none  [on_device(): highest = lax.pmax(jnp.max(averaged), ('ply', 'gx', 'gy')) + 1e-06]
    pallas_call x0 -> x1, Pallas kernels: none -> 56.2 us  [window_sums(): pl.pallas_call(window_kernel, out_shape=(jax.ShapeDtypeStruct((BX, BY, PT...]
    all_to_all x0 -> x1, blocking collectives: none -> 28.4 us  [on_device(): lax.all_to_all(jnp.broadcast_to(top, (128, PTS)), ('ply', 'y', 'z', 'xlo'...]
    ppermute x6, waiting for transfers between devices: 15.4 us -> 5.4 us  [the longest x1 3.28 us: on_device(): lax.ppermute(jnp.concatenate([own[:, 0], other[:, 0]], 0), gx, down(8))]
    dynamic_slice x18 -> x0, local copies, waits for them, and re-layouts: 8.27 us -> none  [the longest x12 4.75 us: locate(): lax.dynamic_slice(pair_mask, (layer_at, strip_at, zero, zero), (1, 1, blo...]
    another operation x1 -> x0, loops' own time: 4.77 us -> none  [on_device(): totals = lax.map(one_row, rows_all)]
    unnamed x6 -> x19, local copies, waits for them, and re-layouts: 0.73 us -> 5.2 us
  transfers between devices with their start and end apart: 6 -> 6, of which waited for: 5 -> 4; matrix products, arithmetic and copies ran while one was open for 0% -> 3% of each run, Pallas kernels for 0% -> 0%
where the time goes in v1:
time: 119 us
  Pallas kernels  56.2 us (47%)
  blocking collectives  28.4 us (24%)
  starting transfers between devices  16.5 us (14%)
  local copies, waits for them, and re-layouts  9.46 us (8%)
  waiting for transfers between devices  5.4 us (5%)
  between operations  1.49 us (1%)
    pallas_call x1, Pallas kernels, window_sums(): pl.pallas_call(window_kernel, out_shape=(jax.ShapeDtypeStruct((BX, BY, PT...  56.2 us
    all_to_all x1, blocking collectives, on_device(): lax.all_to_all(jnp.broadcast_to(top, (128, PTS)), ('ply', 'y', 'z', 'xlo'...  28.4 us
    unnamed x19, local copies, waits for them, and re-layouts  5.2 us
    ppermute x1, starting transfers between devices, on_device(): lax.ppermute(jnp.concatenate([own[:, BX - 1], other[:, BX - 1]], 0), gx,...  5.14 us
    ppermute x1, starting transfers between devices, on_device(): other = lax.ppermute(own, 'ply', [(0, 1), (1, 0)])  3.65 us
    ppermute x1, waiting for transfers between devices, on_device(): lax.ppermute(jnp.concatenate([own[:, 0], other[:, 0]], 0), gx, down(8))  3.28 us
    ppermute x1, starting transfers between devices, on_device(): ylo = lax.ppermute(column(BY - 1), gy, up(16))  3.1 us
  transfers between devices with their start and end apart: 6, of which 4 were waited for; matrix products, arithmetic and copies ran while one was open for 3% of the time, Pallas kernels for 0%

profile of v1, /device:TPU:1, one launch (start us, length us, event | category | flops | bytes accessed | tf_op | source)
XLA Modules:
  0.0 118.6 jit_solution(9944808494363263603)
XLA Ops:
  0.6 0.8 copy.65
  1.4 0.0 copy-start.3
  1.4 0.8 copy.79
  2.2 0.0 copy-done.3
  2.3 0.1 compare_select_fusion.1
  2.4 3.6 %collective-permute-start = (f32[4,6,6,128]{3,2,0,1:T(8,128)S(1)}, f32[4,6,6,128]{3,2,0,1:T(8,128)S(1)}, u32[]{:S(2)}, u32[]{:S(2)}) collective-permute-start(f32[4,6,6,128]{3,2,0,1:T(8,128)S(1)} %copy.48), channel_id=1, source_target_pairs={{0,128},{128,0},{1,129},{129,1},{2,130},{130,2},{3,131},{131,3},{4... | collective-permute-start | bytes 221192 | tf_op jit(solution)/shard_map/ppermute | solution.py:156
  6.1 0.0 copy-start.4
  6.1 0.1 pad.16.clone
  6.2 0.6 copy-done.4
  6.8 0.1 fusion.12
  6.9 0.1 slice_select_fusion
  7.0 1.1 collective-permute-done
  8.1 5.1 %collective-permute-start.1 = (f32[8,6,128]{2,0,1:T(8,128)S(1)}, f32[8,6,128]{2,0,1:T(8,128)S(1)}, u32[]{:S(2)}, u32[]{:S(2)}) collective-permute-start(f32[8,6,128]{2,0,1:T(8,128)S(1)} %pad_maximum_fusion.4), channel_id=1, source_target_pairs={{0,16},{16,32},{32,48},{48,64},{64,80},{80,96},{96,112},{1,17},{17... | collective-permute-start | bytes 73736 | tf_op jit(solution)/shard_map/ppermute | solution.py:162
  13.3 1.9 %collective-permute-start.2 = (f32[8,6,128]{2,1,0:T(8,128)S(1)}, f32[8,6,128]{2,1,0:T(8,128)S(1)}, u32[]{:S(2)}, u32[]{:S(2)}) collective-permute-start(f32[8,6,128]{2,1,0:T(8,128)S(1)} %pad_maximum_fusion.1), channel_id=1, source_target_pairs={{16,0},{32,16},{48,32},{64,48},{80,64},{96,80},{112,96},{17,1},{33... | collective-permute-start | bytes 73736 | tf_op jit(solution)/shard_map/ppermute | solution.py:163
  15.3 0.0 collective-permute-done.1
  15.3 3.3 %collective-permute-done.2.xhi_ref = f32[8,6,128]{2,1,0:T(8,128)S(1)} collective-permute-done((f32[8,6,128]{2,1,0:T(8,128)S(1)}, f32[8,6,128]{2,1,0:T(8,128)S(1)}, u32[]{:S(2)}, u32[]{:S(2)}) %collective-permute-start.2) | collective-permute-done | bytes 24608 | tf_op jit(solution)/shard_map/ppermute | solution.py:163
  18.6 0.0 copy-start
  18.6 0.6 copy-done
  19.2 3.1 %collective-permute-start.3 = (f32[8,8,128]{2,0,1:T(8,128)S(1)}, f32[8,8,128]{2,0,1:T(8,128)S(1)}, u32[]{:S(2)}, u32[]{:S(2)}) collective-permute-start(f32[8,8,128]{2,0,1:T(8,128)S(1)} %pad_maximum_fusion.2), channel_id=1, source_target_pairs={{0,1},{1,2},{2,3},{3,4},{4,5},{5,6},{6,7},{7,8},{8,9},{9,10},{10,1... | collective-permute-start | bytes 98312 | tf_op jit(solution)/shard_map/ppermute | solution.py:169
  22.3 1.3 %collective-permute-start.4 = (f32[8,8,128]{2,1,0:T(8,128)S(1)}, f32[8,8,128]{2,1,0:T(8,128)S(1)}, u32[]{:S(2)}, u32[]{:S(2)}) collective-permute-start(f32[8,8,128]{2,1,0:T(8,128)S(1)} %pad_maximum_fusion.3), channel_id=1, source_target_pairs={{1,0},{2,1},{3,2},{4,3},{5,4},{6,5},{7,6},{8,7},{9,8},{10,9},{11,1... | collective-permute-start | bytes 98312 | tf_op jit(solution)/shard_map/ppermute | solution.py:170
  23.6 0.1 add_convert_fusion
  23.7 0.7 copy.56.own_ref
  24.4 0.7 convert_element_type.13.flag_ref
  25.1 0.6 copy.57.other_ref
  25.7 0.6 copy.58.xlo_ref
  26.3 0.0 collective-permute-done.3
  26.3 0.6 copy.59.ylo_ref
  27.0 0.2 collective-permute-done.4.yhi_ref
  27.1 0.0 copy-start.1
  27.1 0.6 copy-done.1
  27.8 56.2 %window_sums.1 = (f32[6,6,128]{2,1,0:T(8,128)}, f32[1,128]{1,0:T(1,128)}) custom-call(f32[1]{0:T(128)} %bitcast.shift_ref, f32[648]{0:T(1024)} %convert_element_type.13.flag_ref, f32[4,6,6,128]{3,2,1,0:T(8,128)} %copy.56.own_ref, f32[4,6,6,128]{3,2,1,0:T(8,128)} %copy.57.other_ref, f32[8,6,128]{2,1,0:T(8,128)} %copy.58.xlo_ref, f32[8,6,128]{2,1,0:T(8,128)} %copy-done, ...), custom_call_target="tpu_custom_call" | custom-call | tf_op jit(solution)/shard_map/window_sums/pallas_call | solution.py:133
  84.0 0.0 copy-start.6
  84.0 0.6 copy-done.6
  84.6 28.4 %all_to_all.6 = f32[128,1,128]{2,1,0:T(1,128)S(1)} all-to-all(f32[128,1,128]{2,1,0:T(1,128)S(1)} %broadcast_in_dim.20), channel_id=1, replica_groups=mesh['ply'=2,'y'=4,'core'=2,'z'=8,'xlo'=2] {'ply','y','z','xlo'}, dimensions={0} | all-to-all | bytes 131072 | tf_op jit(solution)/shard_map/all_to_all | solution.py:180
  113.1 0.0 copy-start.2
  113.1 1.4 %collective-permute-start.5 = (f32[1,128]{1,0:T(1,128)S(1)}, f32[1,128]{1,0:T(1,128)S(1)}, u32[]{:S(2)}, u32[]{:S(2)}) collective-permute-start(f32[1,128]{1,0:T(1,128)S(1)} %bitcast.49), channel_id=1, source_target_pairs={{0,16},{16,0},{1,17},{17,1},{2,18},{18,2},{3,19},{19,3},{4,20},{20... | collective-permute-start | bytes 1544 | tf_op jit(solution)/shard_map/ppermute | solution.py:184
  114.4 0.8 collective-permute-done.5
  115.3 0.6 maximum_reduce_fusion
  116.5 0.0 copy-done.2
  116.5 0.0 copy-start.5
  116.6 0.7 copy-done.5
  117.3 0.1 compare_select_fusion
  117.4 0.6 copy.64
  118.0 0.6 copy.63
  (20 shorter events, 0.3 us)
Async XLA Ops:
  1.4 0.8 copy-start.3
  2.4 5.7 %collective-permute-start = (f32[4,6,6,128]{3,2,0,1:T(8,128)S(1)}, f32[4,6,6,128]{3,2,0,1:T(8,128)S(1)}, u32[]{:S(2)}, u32[]{:S(2)}) collective-permute-start(f32[4,6,6,128]{3,2,0,1:T(8,128)S(1)} %copy.48), channel_id=1, source_target_pairs={{0,128},{128,0},{1,129},{129,1},{2,130},{130,2},{3,131},{131,3},{4... | collective-permute-start | bytes 221192 | tf_op jit(solution)/shard_map/ppermute | solution.py:156
  6.1 0.7 copy-start.4
  8.1 7.2 %collective-permute-start.1 = (f32[8,6,128]{2,0,1:T(8,128)S(1)}, f32[8,6,128]{2,0,1:T(8,128)S(1)}, u32[]{:S(2)}, u32[]{:S(2)}) collective-permute-start(f32[8,6,128]{2,0,1:T(8,128)S(1)} %pad_maximum_fusion.4), channel_id=1, source_target_pairs={{0,16},{16,32},{32,48},{48,64},{64,80},{80,96},{96,112},{1,17},{17... | collective-permute-start | bytes 73736 | tf_op jit(solution)/shard_map/ppermute | solution.py:162
  13.3 5.2 %collective-permute-start.2 = (f32[8,6,128]{2,1,0:T(8,128)S(1)}, f32[8,6,128]{2,1,0:T(8,128)S(1)}, u32[]{:S(2)}, u32[]{:S(2)}) collective-permute-start(f32[8,6,128]{2,1,0:T(8,128)S(1)} %pad_maximum_fusion.1), channel_id=1, source_target_pairs={{16,0},{32,16},{48,32},{64,48},{80,64},{96,80},{112,96},{17,1},{33... | collective-permute-start | bytes 73736 | tf_op jit(solution)/shard_map/ppermute | solution.py:163
  18.6 0.6 copy-start
  19.2 7.1 %collective-permute-start.3 = (f32[8,8,128]{2,0,1:T(8,128)S(1)}, f32[8,8,128]{2,0,1:T(8,128)S(1)}, u32[]{:S(2)}, u32[]{:S(2)}) collective-permute-start(f32[8,8,128]{2,0,1:T(8,128)S(1)} %pad_maximum_fusion.2), channel_id=1, source_target_pairs={{0,1},{1,2},{2,3},{3,4},{4,5},{5,6},{6,7},{7,8},{8,9},{9,10},{10,1... | collective-permute-start | bytes 98312 | tf_op jit(solution)/shard_map/ppermute | solution.py:169
  22.3 4.8 %collective-permute-start.4 = (f32[8,8,128]{2,1,0:T(8,128)S(1)}, f32[8,8,128]{2,1,0:T(8,128)S(1)}, u32[]{:S(2)}, u32[]{:S(2)}) collective-permute-start(f32[8,8,128]{2,1,0:T(8,128)S(1)} %pad_maximum_fusion.3), channel_id=1, source_target_pairs={{1,0},{2,1},{3,2},{4,3},{5,4},{6,5},{7,6},{8,7},{9,8},{10,9},{11,1... | collective-permute-start | bytes 98312 | tf_op jit(solution)/shard_map/ppermute | solution.py:170
  27.1 0.6 copy-start.1
  84.0 0.6 copy-start.6
  113.1 3.5 %copy-start.2 = (f32[6,6,128]{2,1,0:T(8,128)S(1)}, f32[6,6,128]{2,1,0:T(8,128)}, u32[]{:S(2)}) copy-start(f32[6,6,128]{2,1,0:T(8,128)} %get-tuple-element.4) | copy-start | bytes 55300
  113.1 2.2 %collective-permute-start.5 = (f32[1,128]{1,0:T(1,128)S(1)}, f32[1,128]{1,0:T(1,128)S(1)}, u32[]{:S(2)}, u32[]{:S(2)}) collective-permute-start(f32[1,128]{1,0:T(1,128)S(1)} %bitcast.49), channel_id=1, source_target_pairs={{0,16},{16,0},{1,17},{17,1},{2,18},{18,2},{3,19},{19,3},{4,20},{20... | collective-permute-start | bytes 1544 | tf_op jit(solution)/shard_map/ppermute | solution.py:184
  116.5 0.7 copy-start.5

commit v2 on v0

v2 whole, which is shorter than its diff:
```python
import functools

import jax
import jax.numpy as jnp
from jax import lax
from jax.experimental import pallas as pl
from jax.experimental.pallas import tpu as pltpu
from jax.sharding import Mesh
from jax.sharding import PartitionSpec as P

BX = 6
BY = 6
NB = BX * BY
WX = BX + 2
PTS = 128
K = 16
AXES = ("ply", "y", "core", "z", "xlo")
F32 = jnp.float32
BF16 = jnp.bfloat16
VMEM = pl.BlockSpec(memory_space=pltpu.VMEM)
SMEM = pl.BlockSpec(memory_space=pltpu.SMEM)


def pieces_of(v, count):
    out = []
    for n in range(count):
        high = v.astype(BF16).astype(F32)
        out.append(high)
        v = v - high
    return out


def positions(ref, row, count, stride, step, x_at, y_at, z_at):
    load = lambda c: ref[pl.ds(row + c * step, count, stride=stride), :]
    shifts = (z_at - 0.5, x_at, y_at)
    pieces = [pieces_of(load(c) + shifts[c], 2) for c in range(3)]
    norm = None
    for high, low in pieces:
        p = high + low
        norm = p * p if norm is None else norm + p * p
    return [p[0] for p in pieces], [p[1] for p in pieces], norm, load(3)


def put_neighbour(feat, rows, base, highs, lows, norm, strain):
    count = strain.shape[0]
    one = jnp.ones_like(strain)
    live = jnp.where(strain > 0.0, 1.0, -256.0)
    listed = highs + lows + highs + pieces_of(live - norm, 3) + [one] * 3 + [jnp.zeros_like(strain)]
    for k, v in enumerate(listed):
        feat[pl.ds(base * K + k, count, stride=K), :] = v
    rows[pl.ds(base, count), :] = strain


def put_center(cent, base, highs, lows, norm):
    count = norm.shape[0]
    one = jnp.ones_like(norm)
    twice = [2.0 * v for v in highs]
    listed = twice + twice + [2.0 * v for v in lows] + [one] * 3 + pieces_of(-norm, 3) + [jnp.zeros_like(norm)]
    for k, v in enumerate(listed):
        cent[pl.ds(base * K + k, count, stride=K), :] = v


def round_tiles(feat, bfeat, count, unroll):
    def one(b, carry):
        bfeat[b] = feat[pl.ds(pl.multiple_of(b * K, K), K), :].astype(BF16)
        return carry

    lax.fori_loop(0, count, one, 0, unroll=unroll)


def pair_sums(center, pairs, bfeat, rows, mask):
    spot = jnp.where(lax.broadcasted_iota(jnp.int32, (K, PTS), 0) == 9, 1.0, 0.0)
    sums = [[None] * 16, [None] * 16]
    for t in range(0, len(pairs), 2):
        some = pairs[t : t + 2]
        tiles = []
        for b, flag in some:
            tile = bfeat[b]
            if flag is not None:
                tile = tile + (spot * mask(*flag)).astype(BF16)
            tiles.append(tile)
        rhs = jnp.concatenate(tiles, axis=1) if len(tiles) > 1 else tiles[0]
        gap = jnp.dot(center, rhs, preferred_element_type=F32)
        for n, (b, flag) in enumerate(some):
            strain = jnp.broadcast_to(rows[pl.ds(b, 1), :], (8, PTS))
            for r in range(16):
                w = jnp.maximum(gap[r * 8 : r * 8 + 8, n * PTS : (n + 1) * PTS], 0.0)
                w = w * w
                v = w * strain
                sums[0][r] = v if sums[0][r] is None else sums[0][r] + v
                sums[1][r] = w if sums[1][r] is None else sums[1][r] + w
    return [jnp.sum(jnp.concatenate(s, axis=0).T, axis=0, keepdims=True) for s in sums]


def y_in():
    return lax.broadcasted_iota(jnp.int32, (BY, PTS), 0).astype(F32) - (BY // 2)


def mask_reader(mask_ref, place_ref):
    def read(a, layer, dx, dy):
        t = dx * 3 + dy
        if layer:
            k = jnp.where(place_ref[0] == 0, 17, 0) + t
        else:
            k = 9 + t - jnp.where(t > 4, 1, 0)
        return (mask_ref[a, 0, k] * 256 - 256).astype(F32)

    return read


def inner_sums(layer, bcent, bfeat, rows, mask, acc):
    def strip(x, first, dxs):
        for y in range(BY):
            a = x * BY + y
            pairs = []
            for n in range(dxs):
                for dy in range(3):
                    if 0 <= y + dy - 1 < BY:
                        flag = (a, layer, first + n - x + 1, dy)
                        if layer == 0 and dy == 1 and dxs == 3 and n == 1:
                            flag = None
                        pairs.append(((first + n) * BY + y + dy - 1, flag))
            for c, s in enumerate(pair_sums(bcent[a], pairs, bfeat, rows, mask)):
                acc[pl.ds(a * 2 + c, 1), :] = s

    def edge(e, carry):
        strip(e * (BX - 1), e * (BX - 2), 2)
        return carry

    def middle(x, carry):
        strip(x, x - 1, 3)
        return carry

    lax.fori_loop(0, 2, edge, 0)
    lax.fori_loop(1, BX - 1, middle, 0)


def own_kernel(place_ref, mask_ref, own_ref, acc, bcent, cent, feat, rows, bfeat):
    read = mask_reader(mask_ref, place_ref)

    def mask(a, layer, dx, dy):
        at_self = (dx == 1) if dy == 1 else False
        return read(a, layer, dx, dy) if dy != 1 else jnp.where(at_self, 0.0, read(a, layer, dx, dy))

    for x in range(BX):
        highs, lows, norm, strain = positions(own_ref, x * BY, BY, 1, NB, float(x - BX // 2), y_in(), 0.0)
        put_neighbour(feat, rows, x * BY, highs, lows, norm, strain)
        put_center(cent, x * BY, highs, lows, norm)
    round_tiles(feat, bfeat, NB, 6)

    def turn(a, carry):
        bcent[a] = cent[pl.ds(pl.multiple_of(a * K, K), K), :].T.astype(BF16)
        return carry

    lax.fori_loop(0, NB, turn, 0, unroll=6)
    inner_sums(0, bcent, bfeat, rows, mask, acc)


def other_kernel(place_ref, mask_ref, other_ref, bcent, acc, feat, rows, bfeat):
    shift = (1 - 2 * place_ref[0]).astype(F32)
    for x in range(BX):
        highs, lows, norm, strain = positions(other_ref, x * BY, BY, 1, NB, float(x - BX // 2), y_in(), shift)
        put_neighbour(feat, rows, x * BY, highs, lows, norm, strain)
    round_tiles(feat, bfeat, NB, 6)
    inner_sums(1, bcent, bfeat, rows, mask_reader(mask_ref, place_ref), acc)


def x_kernel(place_ref, mask_ref, core_ref, far_ref, bcent, acc, feat, rows, bfeat):
    shift = (1 - 2 * place_ref[0]).astype(F32)
    mask = mask_reader(mask_ref, place_ref)
    acc[...] = jnp.zeros_like(acc)
    for slot, ref in enumerate((core_ref, far_ref)):
        above = (1 - place_ref[1]) if slot == 0 else place_ref[1]
        x_at = (above * (BX + 1) - 1 - BX // 2).astype(F32)
        for layer in range(2):
            highs, lows, norm, strain = positions(ref, layer * 4 * BY, BY, 1, BY, x_at, y_in(), shift if layer else 0.0)
            put_neighbour(feat, rows, (slot * 2 + layer) * BY, highs, lows, norm, strain)
    round_tiles(feat, bfeat, 4 * BY, 6)

    def side(slot, carry):
        above = jnp.where(slot == 0, 1 - place_ref[1], place_ref[1])
        for y in range(BY):
            a = above * (BX - 1) * BY + y
            pairs = [
                ((slot * 2 + layer) * BY + y + dy - 1, (a, layer, above * 2, dy))
                for layer in range(2)
                for dy in range(3)
                if 0 <= y + dy - 1 < BY
            ]
            for c, s in enumerate(pair_sums(bcent[a], pairs, bfeat, rows, mask)):
                acc[pl.ds(a * 2 + c, 1), :] = s
        return carry

    lax.fori_loop(0, 2, side, 0)


def y_kernel(
    place_ref, mask_ref, near_ref, far_ref, bcent, own_ref, acc1, acc2, acc3, avg_ref, top_ref, feat, rows, bfeat, acc
):
    shift = (1 - 2 * place_ref[0]).astype(F32)
    mask = mask_reader(mask_ref, place_ref)
    acc[...] = acc1[...] + acc2[...] + acc3[...]
    x_in = lax.broadcasted_iota(jnp.int32, (WX, PTS), 0).astype(F32) - (WX // 2)
    for slot, ref in enumerate((near_ref, far_ref)):
        above = (1 - place_ref[2]) if slot == 0 else place_ref[2]
        y_at = (above * (BY + 1) - 1 - BY // 2).astype(F32)
        for layer in range(2):
            highs, lows, norm, strain = positions(ref, layer * 4 * WX, WX, 1, WX, x_in, y_at, shift if layer else 0.0)
            put_neighbour(feat, rows, (slot * 2 + layer) * WX, highs, lows, norm, strain)
    round_tiles(feat, bfeat, 4 * WX, 8)

    def side(slot, carry):
        above = jnp.where(slot == 0, 1 - place_ref[2], place_ref[2])
        for x in range(BX):
            a = above * (BY - 1) + x * BY
            pairs = [
                ((slot * 2 + layer) * WX + x + dx, (a, layer, dx, above * 2)) for layer in range(2) for dx in range(3)
            ]
            for c, s in enumerate(pair_sums(bcent[a], pairs, bfeat, rows, mask)):
                acc[pl.ds(a * 2 + c, 1), :] += s
        return carry

    lax.fori_loop(0, 2, side, 0)
    top = None
    for r in range(0, NB, 12):
        s = [acc[pl.ds(r * 2 + k, 12, stride=2), :] for k in range(2)]
        live = jnp.where(own_ref[pl.ds(3 * NB + r, 12), :] > 0.0, 1.0, 0.0)
        averaged = live * s[0] / (s[1] + 1.0 - live)
        avg_ref[pl.ds(r, 12), :] = averaged
        top = averaged if top is None else jnp.maximum(top, averaged)
    top_ref[...] = jnp.broadcast_to(jnp.max(top, axis=0, keepdims=True), (8, PTS))


def pack_kernel(counts_ref, coords_ref, strain_ref, own_ref):
    slots = lax.broadcasted_iota(jnp.int32, (1, PTS), 1)
    for c in range(3):
        own_ref[pl.ds(c * NB, NB), :] = coords_ref[pl.ds(c * NB, NB), 0, :]
    for b in range(NB):
        live = slots < counts_ref[b // BY, 0, b % BY]
        own_ref[pl.ds(3 * NB + b, 1), :] = jnp.where(live, strain_ref[b], 0.0)


def strips_kernel(place_ref, own_ref, other_ref, core_ref, far_ref):
    for slot, out in enumerate((core_ref, far_ref)):
        above = (1 - place_ref[1]) if slot == 0 else place_ref[1]
        for layer, ref in enumerate((own_ref, other_ref)):
            for c in range(4):
                out[pl.ds((layer * 4 + c) * BY, BY), :] = ref[pl.ds(c * NB + above * (BX - 1) * BY, BY), :]


def columns_kernel(place_ref, own_ref, other_ref, core_ref, far_ref, near_out, far_out):
    for slot, out in enumerate((near_out, far_out)):
        y = ((1 - place_ref[2]) if slot == 0 else place_ref[2]) * (BY - 1)
        for layer, ref in enumerate((own_ref, other_ref)):
            for c in range(4):
                row, halo = (layer * 4 + c) * WX, (layer * 4 + c) * BY
                out[pl.ds(row + 1, BX), :] = ref[pl.ds(c * NB + y, BX, stride=BY), :]
                out[pl.ds(row + (1 - place_ref[1]) * (WX - 1), 1), :] = core_ref[pl.ds(halo + y, 1), :]
                out[pl.ds(row + place_ref[1] * (WX - 1), 1), :] = far_ref[pl.ds(halo + y, 1), :]


def final_kernel(top_ref, avg_ref, old_ref, own_ref, new_ref, damage_ref):
    highest = jnp.max(top_ref[...], keepdims=True) + 1e-06
    for b in range(0, NB, 12):
        averaged = avg_ref[pl.ds(b, 12), :]
        live = jnp.where(own_ref[pl.ds(3 * NB + b, 12), :] > 0.0, 1.0, 0.0)
        new = jnp.maximum(old_ref[pl.ds(b, 12), 0, :], 4.0 * averaged / highest)
        new_ref[pl.ds(b, 12), 0, :] = new
        damage_ref[pl.ds(b, 12), 0, :] = live * (1.0 - jnp.exp(-(new - 1.0) / 2.5) / new)


def call(kernel, outs, in_specs, scratch=(), us=1):
    return pl.pallas_call(
        kernel,
        out_shape=tuple(jax.ShapeDtypeStruct(s, d) for s, d in outs),
        in_specs=in_specs,
        out_specs=tuple(VMEM for _ in outs),
        scratch_shapes=[pltpu.VMEM(s, d) for s, d in scratch],
        compiler_params=pltpu.CompilerParams(vmem_limit_bytes=16 << 20),
        cost_estimate=pl.CostEstimate(flops=us * 400_000_000, bytes_accessed=1 << 16, transcendentals=0),
        name=kernel.__name__,
    )


def feature_scratch(count):
    return [((count * K, PTS), F32), ((count, PTS), F32), ((count, K, PTS), BF16)]


SUMS = ((2 * NB, PTS), F32)


def on_device(coords, strain, kappa_old, counts, pair_mask):
    place = jnp.stack([lax.axis_index(a) for a in ("ply", "core", "xlo")]).astype(jnp.int32)
    mask = pair_mask.reshape(NB, 1, 26)
    (own,) = call(pack_kernel, [((4 * NB, PTS), F32)], [SMEM, VMEM, VMEM])(
        counts.reshape(BX, 1, BY), coords.reshape(3 * NB, 1, PTS), strain.reshape(NB, 1, PTS)
    )
    swap = [(0, 1), (1, 0)]
    beside = lambda n: [p for i in range(1, n - 1, 2) for p in ((i, i + 1), (i + 1, i))]
    other = lax.ppermute(own, "ply", swap)
    acc1, bcent = call(
        own_kernel, [SUMS, ((NB, PTS, K), BF16)], [SMEM, SMEM, VMEM], [((NB * K, PTS), F32)] + feature_scratch(NB), 5
    )(place, mask, own)

    strip = ((8 * BY, PTS), F32)
    core, far = call(strips_kernel, [strip, strip], [SMEM, VMEM, VMEM])(place, own, other)
    core = lax.ppermute(core, "core", swap)
    far = lax.ppermute(far, ("y", "core"), beside(8))
    (acc2,) = call(other_kernel, [SUMS], [SMEM, SMEM, VMEM, VMEM], feature_scratch(NB), 5)(place, mask, other, bcent)

    column = ((8 * WX, PTS), F32)
    ynear, yfar = call(columns_kernel, [column, column], [SMEM] + [VMEM] * 4)(place, own, other, core, far)
    ynear = lax.ppermute(ynear, "xlo", swap)
    yfar = lax.ppermute(yfar, ("z", "xlo"), beside(16))
    (acc3,) = call(x_kernel, [SUMS], [SMEM, SMEM] + [VMEM] * 3, feature_scratch(4 * BY), 2)(place, mask, core, far, bcent)
    averaged, top = call(
        y_kernel, [((NB, PTS), F32), ((8, PTS), F32)], [SMEM, SMEM] + [VMEM] * 7, feature_scratch(4 * WX) + [SUMS], 2
    )(place, mask, ynear, yfar, bcent, own, acc1, acc2, acc3)

    top = jnp.maximum(top, lax.ppermute(top, "core", swap))
    tops = lax.all_to_all(jnp.broadcast_to(top[:1], (128, PTS)), ("ply", "y", "z", "xlo"), 0, 0, tiled=True)
    new, damage = call(final_kernel, [((NB, 1, PTS), F32)] * 2, [VMEM] * 4)(tops, averaged, kappa_old.reshape(NB, 1, PTS), own)
    return (new.reshape(1, BX, BY, PTS), damage.reshape(1, BX, BY, PTS))


def solution(mesh):
    fine = Mesh(mesh.devices.reshape(2, 4, 2, 8, 2), AXES)
    gx, gy = ("y", "core"), ("z", "xlo")
    placed = (
        P(None, "ply", gx, gy, None),
        P("ply", gx, gy, None),
        P("ply", gx, gy, None),
        P("ply", gx, gy),
        P("ply", gx, gy, None),
    )
    return jax.shard_map(
        on_device,
        mesh=fine,
        in_specs=placed,
        out_specs=(P("ply", gx, gy, None), P("ply", gx, gy, None)),
        check_vma=False,
    )
```

time: 298 us -> 61.4 us (0.21)
  matrix products: 163 us -> 0 us
  blocking collectives: 79.7 us -> 29.4 us
  Pallas kernels: 0 us -> 18.5 us
  waiting for transfers between devices: 15.4 us -> 1.17 us
  starting transfers between devices: 17.1 us -> 8.94 us
  local copies, waits for them, and re-layouts: 9.74 us -> 2.27 us
  other arithmetic: 6.04 us -> 0.08 us
  loops' own time: 4.77 us -> 0 us
    dot_general x162 -> x0, matrix products: 163 us -> none  [one_row(): jnp.einsum('bij,cbj->cbi', weights, beside[3:5], precision=lax.Precision....]
    pmax x1 -> x0, blocking collectives: 79.7 us -> none  [on_device(): highest = lax.pmax(jnp.max(averaged), ('ply', 'gx', 'gy')) + 1e-06]
    all_to_all x0 -> x1, blocking collectives: none -> 29.4 us  [on_device(): lax.all_to_all(jnp.broadcast_to(top[:1], (128, PTS)), ('ply', 'y', 'z', '...]
    pallas_call x0 -> x8, Pallas kernels: none -> 18.5 us  [the longest x1 6.24 us: on_device(): call(own_kernel, [SUMS, ((NB, PTS, K), BF16)], [SMEM, SMEM, VMEM], [((NB...]
    ppermute x6, waiting for transfers between devices: 15.4 us -> 1.17 us  [the longest x1 1.15 us: on_device(): top = jnp.maximum(top, lax.ppermute(top, 'core', swap))]
    dynamic_slice x18 -> x0, local copies, waits for them, and re-layouts: 8.27 us -> none  [the longest x12 4.75 us: locate(): lax.dynamic_slice(pair_mask, (layer_at, strip_at, zero, zero), (1, 1, blo...]
    ppermute x6, starting transfers between devices: 17.1 us -> 8.94 us  [the longest x1 3.65 us: on_device(): other = lax.ppermute(own, 'ply', swap)]
    another operation x1 -> x0, loops' own time: 4.77 us -> none  [on_device(): totals = lax.map(one_row, rows_all)]
  transfers between devices with their start and end apart: 6 -> 6, of which waited for: 5 -> 1; matrix products, arithmetic and copies ran while one was open for 0% -> 0% of each run, Pallas kernels for 0% -> 23%
where the time goes in v2:
time: 61.4 us; the launch traced here: 61.1 us
  blocking collectives  29.4 us (48%)
  Pallas kernels  18.5 us (30%)
  starting transfers between devices  8.94 us (15%)
  local copies, waits for them, and re-layouts  2.27 us (4%)
  waiting for transfers between devices  1.17 us (2%)
  between operations  0.75 us (1%)
    all_to_all x1, blocking collectives, on_device(): lax.all_to_all(jnp.broadcast_to(top[:1], (128, PTS)), ('ply', 'y', 'z', '...  29.4 us
    pallas_call x1, Pallas kernels, on_device(): call(own_kernel, [SUMS, ((NB, PTS, K), BF16)], [SMEM, SMEM, VMEM], [((NB...  6.24 us
    pallas_call x1, Pallas kernels, on_device(): call(other_kernel, [SUMS], [SMEM, SMEM, VMEM, VMEM], feature_scratch(NB), 5)  5.39 us
    ppermute x1, starting transfers between devices, on_device(): other = lax.ppermute(own, 'ply', swap)  3.65 us
    ppermute x1, starting transfers between devices, on_device(): far = lax.ppermute(far, ('y', 'core'), beside(8))  3.1 us
    pallas_call x1, Pallas kernels, on_device(): call(y_kernel, [((NB, PTS), F32), ((8, PTS), F32)], [SMEM, SMEM] + [VMEM]...  2.26 us
    unnamed x10, local copies, waits for them, and re-layouts  2.22 us
    pallas_call x1, Pallas kernels, on_device(): call(x_kernel, [SUMS], [SMEM, SMEM] + [VMEM] * 3, feature_scratch(4 * BY)...  2.12 us
  transfers between devices with their start and end apart: 6, of which 1 were waited for; matrix products, arithmetic and copies ran while one was open for 0% of the time, Pallas kernels for 23%

profile of v2, /device:TPU:1, one launch (start us, length us, event | category | flops | bytes accessed | tf_op | source)
XLA Modules:
  0.0 61.1 jit_solution(5053553998865864098)
XLA Ops:
  0.6 0.0 copy-start
  0.6 0.8 %copy-done = f32[3,1,6,6,128]{4,1,3,2,0:T(1,128)S(1)} copy-done((f32[3,1,6,6,128]{4,1,3,2,0:T(1,128)S(1)}, f32[3,1,6,6,128]{4,1,3,2,0:T(1,128)}, u32[]{:S(2)}) %copy-start) | copy-done | bytes 55320
  1.4 0.0 copy-start.1
  1.4 0.7 %copy-done.1 = f32[1,6,6,128]{3,0,2,1:T(1,128)S(1)} copy-done((f32[1,6,6,128]{3,0,2,1:T(1,128)S(1)}, f32[1,6,6,128]{3,0,2,1:T(1,128)}, u32[]{:S(2)}) %copy-start.1) | copy-done | bytes 18456
  2.2 0.0 copy-start.4
  2.2 0.7 %copy-done.4 = s32[1,6,6]{2,0,1:T(1,128)S(1)} copy-done((s32[1,6,6]{2,0,1:T(1,128)S(1)}, s32[1,6,6]{2,0,1:T(1,128)}, u32[]{:S(2)}) %copy-start.4) | copy-done | bytes 168
  2.9 0.0 copy-start.2
  2.9 0.6 %pack_kernel.1.own_ref = f32[144,128]{1,0:T(8,128)S(1)} custom-call(s32[6,1,6]{2,1,0:T(1,128)S(1)} %bitcast.21, f32[108,1,128]{2,1,0:T(1,128)S(1)} %bitcast.14, f32[36,1,128]{2,1,0:T(1,128)S(1)} %bitcast.15), custom_call_target="tpu_custom_call" | custom-call | flops 400000000 | bytes 65536 | tf_op jit(solution)/shard_map/pack_kernel/pallas_call | solution.py:295
  3.5 3.6 %collective-permute-start = (f32[144,128]{1,0:T(8,128)S(1)}, f32[144,128]{1,0:T(8,128)S(1)}, u32[]{:S(2)}, u32[]{:S(2)}) collective-permute-start(f32[144,128]{1,0:T(8,128)S(1)} %pack_kernel.1.own_ref), channel_id=1, source_target_pairs={{0,128},{128,0},{1,129},{129,1},{2,130},{130,2},{3,131},{131,3},{4... | collective-permute-start | bytes 221192 | tf_op jit(solution)/shard_map/ppermute | solution.py:300
  7.1 0.1 pad_add_fusion.place_ref
  7.2 0.0 copy-done.2
  7.2 6.2 %own_kernel.1 = (f32[72,128]{1,0:T(8,128)S(1)}, bf16[36,128,16]{2,1,0:T(8,128)(2,1)S(1)}) custom-call(s32[3]{0:T(128)S(1)} %pad_add_fusion.place_ref, s32[36,1,26]{2,1,0:T(1,128)S(1)} %bitcast.16, f32[144,128]{1,0:T(8,128)S(1)} %pack_kernel.1.own_ref), custom_call_target="tpu_custom_call" | custom-call | flops 2000000000 | bytes 65536 | tf_op jit(solution)/shard_map/own_kernel/pallas_call | solution.py:301
  13.5 0.0 collective-permute-done.other_ref
  13.5 0.6 strips_kernel.1
  14.0 1.0 %collective-permute-start.1 = (f32[48,128]{1,0:T(8,128)S(1)}, f32[48,128]{1,0:T(8,128)S(1)}, u32[]{:S(2)}, u32[]{:S(2)}) collective-permute-start(f32[48,128]{1,0:T(8,128)S(1)} %get-tuple-element.12), channel_id=1, source_target_pairs={{0,16},{16,0},{1,17},{17,1},{2,18},{18,2},{3,19},{19,3},{4,20},{20... | collective-permute-start | bytes 73736 | tf_op jit(solution)/shard_map/ppermute | solution.py:307
  15.1 3.1 %collective-permute-start.2 = (f32[48,128]{1,0:T(8,128)S(1)}, f32[48,128]{1,0:T(8,128)S(1)}, u32[]{:S(2)}, u32[]{:S(2)}) collective-permute-start(f32[48,128]{1,0:T(8,128)S(1)} %get-tuple-element.13), channel_id=1, source_target_pairs={{16,32},{32,16},{48,64},{64,48},{80,96},{96,80},{17,33},{33,17},{4... | collective-permute-start | bytes 73736 | tf_op jit(solution)/shard_map/ppermute | solution.py:308
  18.2 5.4 %other_kernel.1.acc2 = f32[72,128]{1,0:T(8,128)S(1)} custom-call(s32[3]{0:T(128)S(1)} %pad_add_fusion.place_ref, s32[36,1,26]{2,1,0:T(1,128)S(1)} %bitcast.17, f32[144,128]{1,0:T(8,128)S(1)} %collective-permute-done.other_ref, bf16[36,128,16]{2,1,0:T(8,128)(2,1)S(1)} %get-tuple-element.16.bcent), custom_call_target="tpu_custom_call" | custom-call | flops 2000000000 | bytes 65536 | tf_op jit(solution)/shard_map/other_kernel/pallas_call | solution.py:309
  23.6 0.0 collective-permute-done.1.core_ref
  23.6 0.0 collective-permute-done.2.far_ref
  23.6 0.6 columns_kernel.1
  24.2 0.4 collective-permute-start.3
  24.6 0.7 %collective-permute-start.4 = (f32[64,128]{1,0:T(8,128)S(1)}, f32[64,128]{1,0:T(8,128)S(1)}, u32[]{:S(2)}, u32[]{:S(2)}) collective-permute-start(f32[64,128]{1,0:T(8,128)S(1)} %get-tuple-element.15), channel_id=1, source_target_pairs={{1,2},{2,1},{3,4},{4,3},{5,6},{6,5},{7,8},{8,7},{9,10},{10,9},{11,... | collective-permute-start | bytes 98312 | tf_op jit(solution)/shard_map/ppermute | solution.py:314
  25.2 2.1 %x_kernel.1.acc3 = f32[72,128]{1,0:T(8,128)S(1)} custom-call(s32[3]{0:T(128)S(1)} %pad_add_fusion.place_ref, s32[36,1,26]{2,1,0:T(1,128)S(1)} %bitcast.18, f32[48,128]{1,0:T(8,128)S(1)} %collective-permute-done.1.core_ref, f32[48,128]{1,0:T(8,128)S(1)} %collective-permute-done.2.far_ref, bf16[36,128,16]{2,1,0:T(8,128)(2,1)S(1)} %get-tuple-element.16.bcent), custom_call_target="tpu_custom_call" | custom-call | flops 800000000 | bytes 65536 | tf_op jit(solution)/shard_map/x_kernel/pallas_call | solution.py:315
  27.4 0.0 collective-permute-done.3.near_ref
  27.4 0.0 collective-permute-done.4.far_ref
  27.4 0.0 copy-start.3
  27.4 2.3 %y_kernel.1 = (f32[36,128]{1,0:T(8,128)S(1)}, f32[8,128]{1,0:T(8,128)S(1)}) custom-call(s32[3]{0:T(128)S(1)} %pad_add_fusion.place_ref, s32[36,1,26]{2,1,0:T(1,128)S(1)} %bitcast.19, f32[64,128]{1,0:T(8,128)S(1)} %collective-permute-done.3.near_ref, f32[64,128]{1,0:T(8,128)S(1)} %collective-permute-done.4.far_ref, ...), custom_call_target="tpu_custom_call" | custom-call | flops 800000000 | bytes 65536 | tf_op jit(solution)/shard_map/y_kernel/pallas_call | solution.py:316
  29.7 0.1 collective-permute-start.5
  29.8 1.2 %collective-permute-done.5 = f32[8,128]{1,0:T(8,128)S(1)} collective-permute-done((f32[8,128]{1,0:T(8,128)S(1)}, f32[8,128]{1,0:T(8,128)S(1)}, u32[]{:S(2)}, u32[]{:S(2)}) %collective-permute-start.5) | collective-permute-done | bytes 4128 | tf_op jit(solution)/shard_map/ppermute | solution.py:320
  31.0 29.4 %all_to_all.8 = f32[128,1,128]{2,1,0:T(1,128)S(1)} all-to-all(f32[128,1,128]{2,1,0:T(1,128)S(1)} %broadcast_in_dim.2), channel_id=1, replica_groups=mesh['ply'=2,'y'=4,'core'=2,'z'=8,'xlo'=2] {'ply','y','z','xlo'}, dimensions={0} | all-to-all | bytes 131072 | tf_op jit(solution)/shard_map/all_to_all | solution.py:321
  60.4 0.0 copy-done.3
  60.4 0.8 %final_kernel.1 = (f32[36,1,128]{2,1,0:T(1,128)}, f32[36,1,128]{2,1,0:T(1,128)}) custom-call(f32[128,128]{1,0:T(8,128)S(1)} %bitcast.13, f32[36,128]{1,0:T(8,128)S(1)} %get-tuple-element.19.avg_ref, f32[36,1,128]{2,1,0:T(1,128)S(1)} %bitcast.20, f32[144,128]{1,0:T(8,128)S(1)} %pack_kernel.1.own_ref), custom_call_target="tpu_custom_call" | custom-call | flops 400000000 | bytes 65536 | tf_op jit(solution)/shard_map/final_kernel/pallas_call | solution.py:322
  (3 shorter events, 0.0 us)
Async XLA Ops:
  0.6 0.8 %copy-start = (f32[3,1,6,6,128]{4,1,3,2,0:T(1,128)S(1)}, f32[3,1,6,6,128]{4,1,3,2,0:T(1,128)}, u32[]{:S(2)}) copy-start(f32[3,1,6,6,128]{4,1,3,2,0:T(1,128)} %param.5) | copy-start | bytes 165892
  1.4 0.7 %copy-start.1 = (f32[1,6,6,128]{3,0,2,1:T(1,128)S(1)}, f32[1,6,6,128]{3,0,2,1:T(1,128)}, u32[]{:S(2)}) copy-start(f32[1,6,6,128]{3,0,2,1:T(1,128)} %param.6) | copy-start | bytes 55300
  2.2 0.7 %copy-start.4 = (s32[1,6,6]{2,0,1:T(1,128)S(1)}, s32[1,6,6]{2,0,1:T(1,128)}, u32[]{:S(2)}) copy-start(s32[1,6,6]{2,0,1:T(1,128)} %param.8) | copy-start | bytes 436
  2.9 4.4 %copy-start.2 = (s32[1,6,6,26]{3,0,2,1:T(1,128)S(1)}, s32[1,6,6,26]{3,0,2,1:T(1,128)}, u32[]{:S(2)}) copy-start(s32[1,6,6,26]{3,0,2,1:T(1,128)} %param.9) | copy-start | bytes 11236
  3.5 10.0 %collective-permute-start = (f32[144,128]{1,0:T(8,128)S(1)}, f32[144,128]{1,0:T(8,128)S(1)}, u32[]{:S(2)}, u32[]{:S(2)}) collective-permute-start(f32[144,128]{1,0:T(8,128)S(1)} %pack_kernel.1.own_ref), channel_id=1, source_target_pairs={{0,128},{128,0},{1,129},{129,1},{2,130},{130,2},{3,131},{131,3},{4... | collective-permute-start | bytes 221192 | tf_op jit(solution)/shard_map/ppermute | solution.py:300
  14.0 9.6 %collective-permute-start.1 = (f32[48,128]{1,0:T(8,128)S(1)}, f32[48,128]{1,0:T(8,128)S(1)}, u32[]{:S(2)}, u32[]{:S(2)}) collective-permute-start(f32[48,128]{1,0:T(8,128)S(1)} %get-tuple-element.12), channel_id=1, source_target_pairs={{0,16},{16,0},{1,17},{17,1},{2,18},{18,2},{3,19},{19,3},{4,20},{20... | collective-permute-start | bytes 73736 | tf_op jit(solution)/shard_map/ppermute | solution.py:307
  15.1 8.5 %collective-permute-start.2 = (f32[48,128]{1,0:T(8,128)S(1)}, f32[48,128]{1,0:T(8,128)S(1)}, u32[]{:S(2)}, u32[]{:S(2)}) collective-permute-start(f32[48,128]{1,0:T(8,128)S(1)} %get-tuple-element.13), channel_id=1, source_target_pairs={{16,32},{32,16},{48,64},{64,48},{80,96},{96,80},{17,33},{33,17},{4... | collective-permute-start | bytes 73736 | tf_op jit(solution)/shard_map/ppermute | solution.py:308
  24.2 3.2 %collective-permute-start.3 = (f32[64,128]{1,0:T(8,128)S(1)}, f32[64,128]{1,0:T(8,128)S(1)}, u32[]{:S(2)}, u32[]{:S(2)}) collective-permute-start(f32[64,128]{1,0:T(8,128)S(1)} %get-tuple-element.14), channel_id=1, source_target_pairs={{0,1},{1,0},{2,3},{3,2},{4,5},{5,4},{6,7},{7,6},{8,9},{9,8},{10,11... | collective-permute-start | bytes 98312 | tf_op jit(solution)/shard_map/ppermute | solution.py:313
  24.6 2.8 %collective-permute-start.4 = (f32[64,128]{1,0:T(8,128)S(1)}, f32[64,128]{1,0:T(8,128)S(1)}, u32[]{:S(2)}, u32[]{:S(2)}) collective-permute-start(f32[64,128]{1,0:T(8,128)S(1)} %get-tuple-element.15), channel_id=1, source_target_pairs={{1,2},{2,1},{3,4},{4,3},{5,6},{6,5},{7,8},{8,7},{9,10},{10,9},{11,... | collective-permute-start | bytes 98312 | tf_op jit(solution)/shard_map/ppermute | solution.py:314
  27.4 33.0 %copy-start.3 = (f32[1,6,6,128]{3,0,2,1:T(1,128)S(1)}, f32[1,6,6,128]{3,0,2,1:T(1,128)}, u32[]{:S(2)}) copy-start(f32[1,6,6,128]{3,0,2,1:T(1,128)} %param.7) | copy-start | bytes 55300
  29.7 1.3 %collective-permute-start.5 = (f32[8,128]{1,0:T(8,128)S(1)}, f32[8,128]{1,0:T(8,128)S(1)}, u32[]{:S(2)}, u32[]{:S(2)}) collective-permute-start(f32[8,128]{1,0:T(8,128)S(1)} %get-tuple-element.18), channel_id=1, source_target_pairs={{0,16},{16,0},{1,17},{17,1},{2,18},{18,2},{3,19},{19,3},{4,20},{20... | collective-permute-start | bytes 12296 | tf_op jit(solution)/shard_map/ppermute | solution.py:320

commit v3 on v2

v3 whole, which is shorter than its diff:
```python
import jax
import jax.numpy as jnp
from jax import lax
from jax.experimental import pallas as pl
from jax.experimental.pallas import tpu as pltpu
from jax.sharding import Mesh
from jax.sharding import PartitionSpec as P

BX = 6
BY = 6
NB = BX * BY
WX = BX + 2
PTS = 128
K = 16
FLAGS = 32
AXES = ("ply", "y", "core", "z", "xlo")
F32 = jnp.float32
BF16 = jnp.bfloat16
VMEM = pl.BlockSpec(memory_space=pltpu.VMEM)


def pieces_of(v, count):
    out = []
    for n in range(count):
        high = v.astype(BF16).astype(F32)
        out.append(high)
        v = v - high
    return out


def positions(ref, row, count, stride, step, x_at, y_at, z_at):
    load = lambda c: ref[pl.ds(row + c * step, count, stride=stride), :]
    shifts = (z_at - 0.5, x_at, y_at)
    pieces = [pieces_of(load(c) + shifts[c], 2) for c in range(3)]
    norm = None
    for high, low in pieces:
        p = high + low
        norm = p * p if norm is None else norm + p * p
    return [p[0] for p in pieces], [p[1] for p in pieces], norm, load(3)


def put_neighbour(feat, rows, base, highs, lows, norm, strain):
    count = strain.shape[0]
    one = jnp.ones_like(strain)
    live = jnp.where(strain > 0.0, 1.0, -256.0)
    listed = highs + lows + highs + pieces_of(live - norm, 3) + [one] * 3 + [jnp.zeros_like(strain)]
    for k, v in enumerate(listed):
        feat[pl.ds(base * K + k, count, stride=K), :] = v
    rows[pl.ds(base, count), :] = strain


def put_center(cent, base, highs, lows, norm):
    count = norm.shape[0]
    one = jnp.ones_like(norm)
    twice = [2.0 * v for v in highs]
    listed = twice + twice + [2.0 * v for v in lows] + [one] * 3 + pieces_of(-norm, 3) + [jnp.zeros_like(norm)]
    for k, v in enumerate(listed):
        cent[pl.ds(base * K + k, count, stride=K), :] = v


def round_tiles(feat, bfeat, count, unroll):
    def one(b, carry):
        bfeat[b] = feat[pl.ds(pl.multiple_of(b * K, K), K), :].astype(BF16)
        return carry

    lax.fori_loop(0, count, one, 0, unroll=unroll)


def pair_sums(center, pairs, bfeat, rows, mask):
    spot = jnp.where(lax.broadcasted_iota(jnp.int32, (K, PTS), 0) == 9, 1.0, 0.0)
    sums = [[None] * 16, [None] * 16]
    for t in range(0, len(pairs), 2):
        some = pairs[t : t + 2]
        tiles = []
        for b, flag in some:
            tile = bfeat[b]
            if flag is not None:
                tile = tile + (spot * jnp.broadcast_to(mask[pl.ds(flag, 1), :], (K, PTS))).astype(BF16)
            tiles.append(tile)
        rhs = jnp.concatenate(tiles, axis=1) if len(tiles) > 1 else tiles[0]
        gap = jnp.dot(center, rhs, preferred_element_type=F32)
        for n, (b, flag) in enumerate(some):
            strain = jnp.broadcast_to(rows[pl.ds(b, 1), :], (8, PTS))
            for r in range(16):
                w = jnp.maximum(gap[r * 8 : r * 8 + 8, n * PTS : (n + 1) * PTS], 0.0)
                w = w * w
                v = w * strain
                sums[0][r] = v if sums[0][r] is None else sums[0][r] + v
                sums[1][r] = w if sums[1][r] is None else sums[1][r] + w
    return [jnp.sum(jnp.concatenate(s, axis=0).T, axis=0, keepdims=True) for s in sums]


def y_in():
    return lax.broadcasted_iota(jnp.int32, (BY, PTS), 0).astype(F32) - (BY // 2)


def flag_row(a, layer, dx, dy):
    t = dx * 3 + dy
    if layer:
        return a * FLAGS + t + jnp.where(lax.axis_index("ply") == 0, 17, 0)
    return a * FLAGS + jnp.where(t == 4, FLAGS - 1, 9 + t - jnp.where(t > 4, 1, 0))


def fill_flags(mask_ref, turned, flags):
    turned[...] = jnp.zeros_like(turned)
    turned[0:NB, 0:26] = (mask_ref[:, 0, :] * 256 - 256).astype(F32)
    across = turned[...].T
    for a in range(NB):
        flags[a * FLAGS : (a + 1) * FLAGS, :] = jnp.broadcast_to(across[0:FLAGS, a : a + 1], (FLAGS, PTS))


def strip_sums(layer, x, first, dxs, bcent, bfeat, rows, flags, acc, add):
    for y in range(BY):
        a = x * BY + y
        pairs = []
        for n in range(dxs):
            for dy in range(3):
                if 0 <= y + dy - 1 < BY:
                    at_self = layer == 0 and dy == 1 and dxs == 3 and n == 1
                    flag = None if at_self else flag_row(a, layer, first + n - x + 1, dy)
                    pairs.append(((first + n) * BY + y + dy - 1, flag))
        for c, s in enumerate(pair_sums(bcent[a], pairs, bfeat, rows, flags)):
            if add:
                s = s + acc[pl.ds(a * 2 + c, 1), :]
            acc[pl.ds(a * 2 + c, 1), :] = s


def edges(layer, add, *refs):
    def edge(e, carry):
        strip_sums(layer, e * (BX - 1), e * (BX - 2), 2, *refs, add)
        return carry

    lax.fori_loop(0, 2, edge, 0)


def middles(layer, low, high, add, *refs):
    def middle(x, carry):
        strip_sums(layer, x, x - 1, 3, *refs, add)
        return carry

    lax.fori_loop(low, high, middle, 0)


def other_shift():
    return (1 - 2 * lax.axis_index("ply")).astype(F32)


def own_kernel(mask_ref, own_ref, acc, bcent, flags, turned, cent, feat, rows, bfeat):
    fill_flags(mask_ref, turned, flags)
    for x in range(BX):
        highs, lows, norm, strain = positions(own_ref, x * BY, BY, 1, NB, float(x - BX // 2), y_in(), 0.0)
        put_neighbour(feat, rows, x * BY, highs, lows, norm, strain)
        put_center(cent, x * BY, highs, lows, norm)
    round_tiles(feat, bfeat, NB, 6)

    def turn(a, carry):
        bcent[a] = cent[pl.ds(pl.multiple_of(a * K, K), K), :].T.astype(BF16)
        return carry

    lax.fori_loop(0, NB, turn, 0, unroll=6)
    refs = (bcent, bfeat, rows, flags, acc)
    edges(0, False, *refs)
    middles(0, 1, BX - 1, False, *refs)


def other_kernel(other_ref, bcent, flags, before, acc, rows, bfeat, feat):
    for x in range(BX):
        highs, lows, norm, strain = positions(other_ref, x * BY, BY, 1, NB, float(x - BX // 2), y_in(), other_shift())
        put_neighbour(feat, rows, x * BY, highs, lows, norm, strain)
    round_tiles(feat, bfeat, NB, 6)
    acc[...] = before[...]
    refs = (bcent, bfeat, rows, flags, acc)
    edges(1, True, *refs)
    middles(1, 1, 2, True, *refs)


def x_kernel(core_ref, far_ref, bcent, flags, other_rows, other_bfeat, before, acc, feat, rows, bfeat):
    core = lax.axis_index("core")
    for slot, ref in enumerate((core_ref, far_ref)):
        above = (1 - core) if slot == 0 else core
        x_at = (above * (BX + 1) - 1 - BX // 2).astype(F32)
        for layer in range(2):
            highs, lows, norm, strain = positions(
                ref, layer * 4 * BY, BY, 1, BY, x_at, y_in(), other_shift() if layer else 0.0
            )
            put_neighbour(feat, rows, (slot * 2 + layer) * BY, highs, lows, norm, strain)
    round_tiles(feat, bfeat, 4 * BY, 6)
    acc[...] = before[...]

    def side(slot, carry):
        above = jnp.where(slot == 0, 1 - core, core)
        for y in range(BY):
            a = above * (BX - 1) * BY + y
            pairs = [
                ((slot * 2 + layer) * BY + y + dy - 1, flag_row(a, layer, above * 2, dy))
                for layer in range(2)
                for dy in range(3)
                if 0 <= y + dy - 1 < BY
            ]
            for c, s in enumerate(pair_sums(bcent[a], pairs, bfeat, rows, flags)):
                acc[pl.ds(a * 2 + c, 1), :] += s
        return carry

    lax.fori_loop(0, 2, side, 0)
    middles(1, 2, BX - 1, True, bcent, other_bfeat, other_rows, flags, acc)


def y_kernel(near_ref, far_ref, bcent, flags, own_ref, before, avg_ref, top_ref, feat, rows, bfeat, acc):
    xlo = lax.axis_index("xlo")
    acc[...] = before[...]
    x_in = lax.broadcasted_iota(jnp.int32, (WX, PTS), 0).astype(F32) - (WX // 2)
    for slot, ref in enumerate((near_ref, far_ref)):
        above = (1 - xlo) if slot == 0 else xlo
        y_at = (above * (BY + 1) - 1 - BY // 2).astype(F32)
        for layer in range(2):
            highs, lows, norm, strain = positions(
                ref, layer * 4 * WX, WX, 1, WX, x_in, y_at, other_shift() if layer else 0.0
            )
            put_neighbour(feat, rows, (slot * 2 + layer) * WX, highs, lows, norm, strain)
    round_tiles(feat, bfeat, 4 * WX, 8)

    def side(slot, carry):
        above = jnp.where(slot == 0, 1 - xlo, xlo)
        for x in range(BX):
            a = above * (BY - 1) + x * BY
            pairs = [
                ((slot * 2 + layer) * WX + x + dx, flag_row(a, layer, dx, above * 2))
                for layer in range(2)
                for dx in range(3)
            ]
            for c, s in enumerate(pair_sums(bcent[a], pairs, bfeat, rows, flags)):
                acc[pl.ds(a * 2 + c, 1), :] += s
        return carry

    lax.fori_loop(0, 2, side, 0)
    top = None
    for r in range(0, NB, 12):
        s = [acc[pl.ds(r * 2 + k, 12, stride=2), :] for k in range(2)]
        live = jnp.where(own_ref[pl.ds(3 * NB + r, 12), :] > 0.0, 1.0, 0.0)
        averaged = live * s[0] / (s[1] + 1.0 - live)
        avg_ref[pl.ds(r, 12), :] = averaged
        top = averaged if top is None else jnp.maximum(top, averaged)
    top_ref[...] = jnp.broadcast_to(jnp.max(top, axis=0, keepdims=True), (8, PTS))


def pack_kernel(counts_hbm, coords_hbm, strain_hbm, own_ref, counts_ref, coords_ref, strain_ref, sems):
    copies = [
        pltpu.make_async_copy(source, target, sems.at[n])
        for n, (source, target) in enumerate(
            ((counts_hbm, counts_ref), (strain_hbm, strain_ref), (coords_hbm, coords_ref))
        )
    ]
    for copy in copies:
        copy.start()
    for copy in copies:
        copy.wait()
    slots = lax.broadcasted_iota(jnp.int32, (1, PTS), 1)
    for c in range(3):
        own_ref[pl.ds(c * NB, NB), :] = coords_ref[pl.ds(c * NB, NB), 0, :]
    for b in range(NB):
        live = slots < counts_ref[b // BY, 0, b % BY]
        own_ref[pl.ds(3 * NB + b, 1), :] = jnp.where(live, strain_ref[b], 0.0)


def strips_kernel(own_ref, other_ref, core_ref, far_ref):
    core = lax.axis_index("core")
    for slot, out in enumerate((core_ref, far_ref)):
        above = (1 - core) if slot == 0 else core
        for layer, ref in enumerate((own_ref, other_ref)):
            for c in range(4):
                out[pl.ds((layer * 4 + c) * BY, BY), :] = ref[pl.ds(c * NB + above * (BX - 1) * BY, BY), :]


def columns_kernel(own_ref, other_ref, core_ref, far_ref, near_out, far_out):
    core, xlo = lax.axis_index("core"), lax.axis_index("xlo")
    for slot, out in enumerate((near_out, far_out)):
        y = ((1 - xlo) if slot == 0 else xlo) * (BY - 1)
        for layer, ref in enumerate((own_ref, other_ref)):
            for c in range(4):
                row, halo = (layer * 4 + c) * WX, (layer * 4 + c) * BY
                out[pl.ds(row + 1, BX), :] = ref[pl.ds(c * NB + y, BX, stride=BY), :]
                out[pl.ds(row + (1 - core) * (WX - 1), 1), :] = core_ref[pl.ds(halo + y, 1), :]
                out[pl.ds(row + core * (WX - 1), 1), :] = far_ref[pl.ds(halo + y, 1), :]


def final_kernel(top_ref, avg_ref, old_ref, own_ref, new_ref, damage_ref):
    highest = jnp.max(top_ref[...], keepdims=True) + 1e-06
    for b in range(0, NB, 12):
        averaged = avg_ref[pl.ds(b, 12), :]
        live = jnp.where(own_ref[pl.ds(3 * NB + b, 12), :] > 0.0, 1.0, 0.0)
        new = jnp.maximum(old_ref[pl.ds(b, 12), 0, :], 4.0 * averaged / highest)
        new_ref[pl.ds(b, 12), 0, :] = new
        damage_ref[pl.ds(b, 12), 0, :] = live * (1.0 - jnp.exp(-(new - 1.0) / 2.5) / new)


def call(kernel, outs, ins, scratch=(), us=1, space=VMEM, extra=()):
    return pl.pallas_call(
        kernel,
        out_shape=tuple(jax.ShapeDtypeStruct(s, d) for s, d in outs),
        in_specs=[space] * ins,
        out_specs=tuple(VMEM for _ in outs),
        scratch_shapes=[pltpu.VMEM(s, d) for s, d in scratch] + list(extra),
        compiler_params=pltpu.CompilerParams(vmem_limit_bytes=16 << 20),
        cost_estimate=pl.CostEstimate(flops=us * 400_000_000, bytes_accessed=1 << 16, transcendentals=0),
        name=kernel.__name__,
    )


def feature_scratch(count):
    return [((count * K, PTS), F32), ((count, PTS), F32), ((count, K, PTS), BF16)]


SUMS = ((2 * NB, PTS), F32)


def on_device(coords, strain, kappa_old, counts, pair_mask):
    (own,) = call(
        pack_kernel,
        [((4 * NB, PTS), F32)],
        3,
        space=pl.BlockSpec(memory_space=pltpu.HBM),
        extra=[
            pltpu.SMEM((BX, 1, BY), jnp.int32),
            pltpu.VMEM((3 * NB, 1, PTS), F32),
            pltpu.VMEM((NB, 1, PTS), F32),
            pltpu.SemaphoreType.DMA((3,)),
        ],
    )(counts.reshape(BX, 1, BY), coords.reshape(3 * NB, 1, PTS), strain.reshape(NB, 1, PTS))
    swap = [(0, 1), (1, 0)]
    beside = lambda n: [p for i in range(1, n - 1, 2) for p in ((i, i + 1), (i + 1, i))]
    other = lax.ppermute(own, "ply", swap)
    acc, bcent, flags = call(
        own_kernel,
        [SUMS, ((NB, PTS, K), BF16), ((NB * FLAGS, PTS), F32)],
        2,
        [((PTS, PTS), F32), ((NB * K, PTS), F32)] + feature_scratch(NB),
        6,
    )(pair_mask.reshape(NB, 1, 26), own)

    strip = ((8 * BY, PTS), F32)
    core, far = call(strips_kernel, [strip, strip], 2)(own, other)
    core = lax.ppermute(core, "core", swap)
    far = lax.ppermute(far, ("y", "core"), beside(8))
    tile = feature_scratch(NB)
    acc, rows, bfeat = call(other_kernel, [SUMS] + tile[1:], 4, tile[:1], 3)(other, bcent, flags, acc)

    column = ((8 * WX, PTS), F32)
    ynear, yfar = call(columns_kernel, [column, column], 4)(own, other, core, far)
    ynear = lax.ppermute(ynear, "xlo", swap)
    yfar = lax.ppermute(yfar, ("z", "xlo"), beside(16))
    (acc,) = call(x_kernel, [SUMS], 7, feature_scratch(4 * BY), 4)(core, far, bcent, flags, rows, bfeat, acc)
    averaged, top = call(y_kernel, [((NB, PTS), F32), ((8, PTS), F32)], 6, feature_scratch(4 * WX) + [SUMS], 2)(
        ynear, yfar, bcent, flags, own, acc
    )

    top = jnp.maximum(top, lax.ppermute(top, "core", swap))
    tops = lax.all_to_all(jnp.broadcast_to(top[:1], (128, PTS)), ("ply", "y", "z", "xlo"), 0, 0, tiled=True)
    new, damage = call(final_kernel, [((NB, 1, PTS), F32)] * 2, 4)(tops, averaged, kappa_old.reshape(NB, 1, PTS), own)
    return (new.reshape(1, BX, BY, PTS), damage.reshape(1, BX, BY, PTS))


def solution(mesh):
    fine = Mesh(mesh.devices.reshape(2, 4, 2, 8, 2), AXES)
    gx, gy = ("y", "core"), ("z", "xlo")
    placed = (
        P(None, "ply", gx, gy, None),
        P("ply", gx, gy, None),
        P("ply", gx, gy, None),
        P("ply", gx, gy),
        P("ply", gx, gy, None),
    )
    return jax.shard_map(
        on_device,
        mesh=fine,
        in_specs=placed,
        out_specs=(P("ply", gx, gy, None), P("ply", gx, gy, None)),
        check_vma=False,
    )
```

time: 61.4 us -> 56 us (0.912)
  Pallas kernels: 18.5 us -> 14.3 us
  blocking collectives: 29.4 us -> 28.4 us
    pallas_call x8, Pallas kernels: 18.5 us -> 14.3 us  [the longest x1 5.69 us: on_device(): call(own_kernel, [SUMS, ((NB, PTS, K), BF16), ((NB * FLAGS, PTS), F32)],...]
    all_to_all x1, blocking collectives: 29.4 us -> 28.4 us  [on_device(): lax.all_to_all(jnp.broadcast_to(top[:1], (128, PTS)), ('ply', 'y', 'z', '...]
  transfers between devices with their start and end apart: 6 -> 6, of which waited for: 1 -> 1; matrix products, arithmetic and copies ran while one was open for 0% -> 0% of each run, Pallas kernels for 23% -> 20%
where the time goes in v3:
time: 56 us; the launch traced here: 55.7 us
  blocking collectives  28.4 us (51%)
  Pallas kernels  14.3 us (26%)
  starting transfers between devices  8.94 us (16%)
  local copies, waits for them, and re-layouts  2.27 us (4%)
  waiting for transfers between devices  1.17 us (2%)
  between operations  0.76 us (1%)
    all_to_all x1, blocking collectives, on_device(): lax.all_to_all(jnp.broadcast_to(top[:1], (128, PTS)), ('ply', 'y', 'z', '...  28.4 us
    pallas_call x1, Pallas kernels, on_device(): call(own_kernel, [SUMS, ((NB, PTS, K), BF16), ((NB * FLAGS, PTS), F32)],...  5.69 us
    pallas_call x1, Pallas kernels, on_device(): call(x_kernel, [SUMS], 7, feature_scratch(4 * BY), 4)  3.65 us
    ppermute x1, starting transfers between devices, on_device(): other = lax.ppermute(own, 'ply', swap)  3.65 us
    ppermute x1, starting transfers between devices, on_device(): far = lax.ppermute(far, ('y', 'core'), beside(8))  3.1 us
    unnamed x10, local copies, waits for them, and re-layouts  2.22 us
    pallas_call x1, Pallas kernels, on_device(): call(other_kernel, [SUMS] + tile[1:], 4, tile[:1], 3)  2.06 us
    pallas_call x1, Pallas kernels, on_device(): call(y_kernel, [((NB, PTS), F32), ((8, PTS), F32)], 6, feature_scratch(4...  1.39 us
  transfers between devices with their start and end apart: 6, of which 1 were waited for; matrix products, arithmetic and copies ran while one was open for 0% of the time, Pallas kernels for 20%

profile of v3, /device:TPU:1, one launch (start us, length us, event | category | flops | bytes accessed | tf_op | source)
XLA Modules:
  0.0 55.7 jit_solution(13683931915991485942)
XLA Ops:
  0.6 0.0 copy-start
  0.6 0.8 %copy-done = f32[3,1,6,6,128]{4,1,3,2,0:T(1,128)S(1)} copy-done((f32[3,1,6,6,128]{4,1,3,2,0:T(1,128)S(1)}, f32[3,1,6,6,128]{4,1,3,2,0:T(1,128)}, u32[]{:S(2)}) %copy-start) | copy-done | bytes 55320
  1.4 0.0 copy-start.1
  1.4 0.7 %copy-done.1 = f32[1,6,6,128]{3,0,2,1:T(1,128)S(1)} copy-done((f32[1,6,6,128]{3,0,2,1:T(1,128)S(1)}, f32[1,6,6,128]{3,0,2,1:T(1,128)}, u32[]{:S(2)}) %copy-start.1) | copy-done | bytes 18456
  2.2 0.0 copy-start.4
  2.2 0.7 %copy-done.4 = s32[1,6,6]{2,0,1:T(1,128)S(1)} copy-done((s32[1,6,6]{2,0,1:T(1,128)S(1)}, s32[1,6,6]{2,0,1:T(1,128)}, u32[]{:S(2)}) %copy-start.4) | copy-done | bytes 168
  2.9 0.0 copy-start.2
  2.9 0.7 %pack_kernel.1.own_ref = f32[144,128]{1,0:T(8,128)S(1)} custom-call(s32[6,1,6]{2,1,0:T(1,128)S(1)} %bitcast.15, f32[108,1,128]{2,1,0:T(1,128)S(1)} %bitcast.11, f32[36,1,128]{2,1,0:T(1,128)S(1)} %bitcast.12), custom_call_target="tpu_custom_call" | custom-call | flops 400000000 | bytes 65536 | tf_op jit(solution)/shard_map/pack_kernel/pallas_call | solution.py:317
  3.5 3.6 %collective-permute-start = (f32[144,128]{1,0:T(8,128)S(1)}, f32[144,128]{1,0:T(8,128)S(1)}, u32[]{:S(2)}, u32[]{:S(2)}) collective-permute-start(f32[144,128]{1,0:T(8,128)S(1)} %pack_kernel.1.own_ref), channel_id=1, source_target_pairs={{0,128},{128,0},{1,129},{129,1},{2,130},{130,2},{3,131},{131,3},{4... | collective-permute-start | bytes 221192 | tf_op jit(solution)/shard_map/ppermute | solution.py:331
  7.2 0.0 copy-done.2
  7.2 5.7 %own_kernel.1 = (f32[72,128]{1,0:T(8,128)S(1)}, bf16[36,128,16]{2,1,0:T(8,128)(2,1)S(1)}, f32[1152,128]{1,0:T(8,128)S(1)}) custom-call(s32[36,1,26]{2,1,0:T(1,128)S(1)} %bitcast.13, f32[144,128]{1,0:T(8,128)S(1)} %pack_kernel.1.own_ref), custom_call_target="tpu_custom_call" | custom-call | flops 2400000000 | bytes 65536 | tf_op jit(solution)/shard_map/own_kernel/pallas_call | solution.py:332
  12.9 0.0 collective-permute-done.other_ref
  12.9 1.0 %collective-permute-start.1 = (f32[48,128]{1,0:T(8,128)S(1)}, f32[48,128]{1,0:T(8,128)S(1)}, u32[]{:S(2)}, u32[]{:S(2)}) collective-permute-start(f32[48,128]{1,0:T(8,128)S(1)} %get-tuple-element.16), channel_id=1, source_target_pairs={{0,16},{16,0},{1,17},{17,1},{2,18},{18,2},{3,19},{19,3},{4,20},{20... | collective-permute-start | bytes 73736 | tf_op jit(solution)/shard_map/ppermute | solution.py:342
  13.9 3.1 %collective-permute-start.2 = (f32[48,128]{1,0:T(8,128)S(1)}, f32[48,128]{1,0:T(8,128)S(1)}, u32[]{:S(2)}, u32[]{:S(2)}) collective-permute-start(f32[48,128]{1,0:T(8,128)S(1)} %get-tuple-element.17), channel_id=1, source_target_pairs={{16,32},{32,16},{48,64},{64,48},{80,96},{96,80},{17,33},{33,17},{4... | collective-permute-start | bytes 73736 | tf_op jit(solution)/shard_map/ppermute | solution.py:343
  17.1 2.1 %other_kernel.1 = (f32[72,128]{1,0:T(8,128)S(1)}, f32[36,128]{1,0:T(8,128)S(1)}, bf16[36,16,128]{2,1,0:T(8,128)(2,1)S(1)}) custom-call(f32[144,128]{1,0:T(8,128)S(1)} %collective-permute-done.other_ref, bf16[36,128,16]{2,1,0:T(8,128)(2,1)S(1)} %get-tuple-element.20.bcent, f32[1152,128]{1,0:T(8,128)S(1)} %get-tuple-element.21.flags, ...), custom_call_target="tpu_custom_call" | custom-call | flops 1200000000 | bytes 65536 | tf_op jit(solution)/shard_map/other_kernel/pallas_call | solution.py:345
  19.1 0.0 collective-permute-done.1.core_ref
  19.1 0.0 collective-permute-done.2.far_ref
  19.2 0.4 collective-permute-start.3
  19.6 0.7 %collective-permute-start.4 = (f32[64,128]{1,0:T(8,128)S(1)}, f32[64,128]{1,0:T(8,128)S(1)}, u32[]{:S(2)}, u32[]{:S(2)}) collective-permute-start(f32[64,128]{1,0:T(8,128)S(1)} %get-tuple-element.19), channel_id=1, source_target_pairs={{1,2},{2,1},{3,4},{4,3},{5,6},{6,5},{7,8},{8,7},{9,10},{10,9},{11,... | collective-permute-start | bytes 98312 | tf_op jit(solution)/shard_map/ppermute | solution.py:350
  20.2 3.7 %x_kernel.1.before = f32[72,128]{1,0:T(8,128)S(1)} custom-call(f32[48,128]{1,0:T(8,128)S(1)} %collective-permute-done.1.core_ref, f32[48,128]{1,0:T(8,128)S(1)} %collective-permute-done.2.far_ref, bf16[36,128,16]{2,1,0:T(8,128)(2,1)S(1)} %get-tuple-element.20.bcent, f32[1152,128]{1,0:T(8,128)S(1)} %get-tuple-element.21.flags, ...), custom_call_target="tpu_custom_call" | custom-call | flops 1600000000 | bytes 65536 | tf_op jit(solution)/shard_map/x_kernel/pallas_call | solution.py:351
  23.9 0.0 copy-start.3
  23.9 0.0 collective-permute-done.3.near_ref
  23.9 0.0 collective-permute-done.4.far_ref
  23.9 1.4 %y_kernel.1 = (f32[36,128]{1,0:T(8,128)S(1)}, f32[8,128]{1,0:T(8,128)S(1)}) custom-call(f32[64,128]{1,0:T(8,128)S(1)} %collective-permute-done.3.near_ref, f32[64,128]{1,0:T(8,128)S(1)} %collective-permute-done.4.far_ref, bf16[36,128,16]{2,1,0:T(8,128)(2,1)S(1)} %get-tuple-element.20.bcent, f32[1152,128]{1,0:T(8,128)S(1)} %get-tuple-element.21.flags, ...), custom_call_target="tpu_custom_call" | custom-call | flops 800000000 | bytes 65536 | tf_op jit(solution)/shard_map/y_kernel/pallas_call | solution.py:352
  25.3 0.1 collective-permute-start.5
  25.4 1.2 %collective-permute-done.5 = f32[8,128]{1,0:T(8,128)S(1)} collective-permute-done((f32[8,128]{1,0:T(8,128)S(1)}, f32[8,128]{1,0:T(8,128)S(1)}, u32[]{:S(2)}, u32[]{:S(2)}) %collective-permute-start.5) | collective-permute-done | bytes 4128 | tf_op jit(solution)/shard_map/ppermute | solution.py:356
  26.6 28.4 %all_to_all.8 = f32[128,1,128]{2,1,0:T(1,128)S(1)} all-to-all(f32[128,1,128]{2,1,0:T(1,128)S(1)} %broadcast_in_dim.2), channel_id=1, replica_groups=mesh['ply'=2,'y'=4,'core'=2,'z'=8,'xlo'=2] {'ply','y','z','xlo'}, dimensions={0} | all-to-all | bytes 131072 | tf_op jit(solution)/shard_map/all_to_all | solution.py:357
  55.0 0.0 copy-done.3
  55.0 0.8 %final_kernel.1 = (f32[36,1,128]{2,1,0:T(1,128)}, f32[36,1,128]{2,1,0:T(1,128)}) custom-call(f32[128,128]{1,0:T(8,128)S(1)} %bitcast.10, f32[36,128]{1,0:T(8,128)S(1)} %get-tuple-element.27.avg_ref, f32[36,1,128]{2,1,0:T(1,128)S(1)} %bitcast.14, f32[144,128]{1,0:T(8,128)S(1)} %pack_kernel.1.own_ref), custom_call_target="tpu_custom_call" | custom-call | flops 400000000 | bytes 65536 | tf_op jit(solution)/shard_map/final_kernel/pallas_call | solution.py:358
  (5 shorter events, 0.1 us)
Async XLA Ops:
  0.6 0.8 %copy-start = (f32[3,1,6,6,128]{4,1,3,2,0:T(1,128)S(1)}, f32[3,1,6,6,128]{4,1,3,2,0:T(1,128)}, u32[]{:S(2)}) copy-start(f32[3,1,6,6,128]{4,1,3,2,0:T(1,128)} %param.5) | copy-start | bytes 165892
  1.4 0.7 %copy-start.1 = (f32[1,6,6,128]{3,0,2,1:T(1,128)S(1)}, f32[1,6,6,128]{3,0,2,1:T(1,128)}, u32[]{:S(2)}) copy-start(f32[1,6,6,128]{3,0,2,1:T(1,128)} %param.6) | copy-start | bytes 55300
  2.2 0.7 %copy-start.4 = (s32[1,6,6]{2,0,1:T(1,128)S(1)}, s32[1,6,6]{2,0,1:T(1,128)}, u32[]{:S(2)}) copy-start(s32[1,6,6]{2,0,1:T(1,128)} %param.8) | copy-start | bytes 436
  2.9 4.3 %copy-start.2 = (s32[1,6,6,26]{3,0,2,1:T(1,128)S(1)}, s32[1,6,6,26]{3,0,2,1:T(1,128)}, u32[]{:S(2)}) copy-start(s32[1,6,6,26]{3,0,2,1:T(1,128)} %param.9) | copy-start | bytes 11236
  3.5 9.4 %collective-permute-start = (f32[144,128]{1,0:T(8,128)S(1)}, f32[144,128]{1,0:T(8,128)S(1)}, u32[]{:S(2)}, u32[]{:S(2)}) collective-permute-start(f32[144,128]{1,0:T(8,128)S(1)} %pack_kernel.1.own_ref), channel_id=1, source_target_pairs={{0,128},{128,0},{1,129},{129,1},{2,130},{130,2},{3,131},{131,3},{4... | collective-permute-start | bytes 221192 | tf_op jit(solution)/shard_map/ppermute | solution.py:331
  12.9 6.2 %collective-permute-start.1 = (f32[48,128]{1,0:T(8,128)S(1)}, f32[48,128]{1,0:T(8,128)S(1)}, u32[]{:S(2)}, u32[]{:S(2)}) collective-permute-start(f32[48,128]{1,0:T(8,128)S(1)} %get-tuple-element.16), channel_id=1, source_target_pairs={{0,16},{16,0},{1,17},{17,1},{2,18},{18,2},{3,19},{19,3},{4,20},{20... | collective-permute-start | bytes 73736 | tf_op jit(solution)/shard_map/ppermute | solution.py:342
  13.9 5.2 %collective-permute-start.2 = (f32[48,128]{1,0:T(8,128)S(1)}, f32[48,128]{1,0:T(8,128)S(1)}, u32[]{:S(2)}, u32[]{:S(2)}) collective-permute-start(f32[48,128]{1,0:T(8,128)S(1)} %get-tuple-element.17), channel_id=1, source_target_pairs={{16,32},{32,16},{48,64},{64,48},{80,96},{96,80},{17,33},{33,17},{4... | collective-permute-start | bytes 73736 | tf_op jit(solution)/shard_map/ppermute | solution.py:343
  19.2 4.7 %collective-permute-start.3 = (f32[64,128]{1,0:T(8,128)S(1)}, f32[64,128]{1,0:T(8,128)S(1)}, u32[]{:S(2)}, u32[]{:S(2)}) collective-permute-start(f32[64,128]{1,0:T(8,128)S(1)} %get-tuple-element.18), channel_id=1, source_target_pairs={{0,1},{1,0},{2,3},{3,2},{4,5},{5,4},{6,7},{7,6},{8,9},{9,8},{10,11... | collective-permute-start | bytes 98312 | tf_op jit(solution)/shard_map/ppermute | solution.py:349
  19.6 4.3 %collective-permute-start.4 = (f32[64,128]{1,0:T(8,128)S(1)}, f32[64,128]{1,0:T(8,128)S(1)}, u32[]{:S(2)}, u32[]{:S(2)}) collective-permute-start(f32[64,128]{1,0:T(8,128)S(1)} %get-tuple-element.19), channel_id=1, source_target_pairs={{1,2},{2,1},{3,4},{4,3},{5,6},{6,5},{7,8},{8,7},{9,10},{10,9},{11,... | collective-permute-start | bytes 98312 | tf_op jit(solution)/shard_map/ppermute | solution.py:350
  23.9 31.1 %copy-start.3 = (f32[1,6,6,128]{3,0,2,1:T(1,128)S(1)}, f32[1,6,6,128]{3,0,2,1:T(1,128)}, u32[]{:S(2)}) copy-start(f32[1,6,6,128]{3,0,2,1:T(1,128)} %param.7) | copy-start | bytes 55300
  25.3 1.3 %collective-permute-start.5 = (f32[8,128]{1,0:T(8,128)S(1)}, f32[8,128]{1,0:T(8,128)S(1)}, u32[]{:S(2)}, u32[]{:S(2)}) collective-permute-start(f32[8,128]{1,0:T(8,128)S(1)} %get-tuple-element.26), channel_id=1, source_target_pairs={{0,16},{16,0},{1,17},{17,1},{2,18},{18,2},{3,19},{19,3},{4,20},{20... | collective-permute-start | bytes 12296 | tf_op jit(solution)/shard_map/ppermute | solution.py:356

commit v4 on v3

--- a/solution.py
+++ b/solution.py
@@ -130,22 +130,22 @@
         strip_sums(layer, e * (BX - 1), e * (BX - 2), 2, *refs, add)
         return carry
 
-    lax.fori_loop(0, 2, edge, 0)
-
-
-def middles(layer, low, high, add, *refs):
+    lax.fori_loop(0, 2, edge, 0, unroll=2)
+
+
+def middles(layer, low, high, add, unroll, *refs):
     def middle(x, carry):
         strip_sums(layer, x, x - 1, 3, *refs, add)
         return carry
 
-    lax.fori_loop(low, high, middle, 0)
+    lax.fori_loop(low, high, middle, 0, unroll=unroll)
 
 
 def other_shift():
     return (1 - 2 * lax.axis_index("ply")).astype(F32)
 
 
-def own_kernel(mask_ref, own_ref, acc, bcent, flags, turned, cent, feat, rows, bfeat):
+def own_kernel(mask_ref, own_ref, acc, bcent, flags, rows, bfeat, turned, cent, feat):
     fill_flags(mask_ref, turned, flags)
     for x in range(BX):
         highs, lows, norm, strain = positions(own_ref, x * BY, BY, 1, NB, float(x - BX // 2), y_in(), 0.0)
@@ -160,7 +160,8 @@
     lax.fori_loop(0, NB, turn, 0, unroll=6)
     refs = (bcent, bfeat, rows, flags, acc)
     edges(0, False, *refs)
-    middles(0, 1, BX - 1, False, *refs)
+    middles(0, 1, BX - 2, False, 3, *refs)
+    acc[pl.ds(2 * (BX - 2) * BY, 2 * BY), :] = jnp.zeros((2 * BY, PTS), F32)
 
 
 def other_kernel(other_ref, bcent, flags, before, acc, rows, bfeat, feat):
@@ -171,10 +172,12 @@
     acc[...] = before[...]
     refs = (bcent, bfeat, rows, flags, acc)
     edges(1, True, *refs)
-    middles(1, 1, 2, True, *refs)
-
-
-def x_kernel(core_ref, far_ref, bcent, flags, other_rows, other_bfeat, before, acc, feat, rows, bfeat):
+    middles(1, 1, 2, True, 1, *refs)
+
+
+def x_kernel(
+    core_ref, far_ref, bcent, flags, own_rows, own_bfeat, other_rows, other_bfeat, before, acc, feat, rows, bfeat
+):
     core = lax.axis_index("core")
     for slot, ref in enumerate((core_ref, far_ref)):
         above = (1 - core) if slot == 0 else core
@@ -201,8 +204,9 @@
                 acc[pl.ds(a * 2 + c, 1), :] += s
         return carry
 
-    lax.fori_loop(0, 2, side, 0)
-    middles(1, 2, BX - 1, True, bcent, other_bfeat, other_rows, flags, acc)
+    lax.fori_loop(0, 2, side, 0, unroll=2)
+    middles(0, BX - 2, BX - 1, True, 1, bcent, own_bfeat, own_rows, flags, acc)
+    middles(1, 2, BX - 1, True, 3, bcent, other_bfeat, other_rows, flags, acc)
 
 
 def y_kernel(near_ref, far_ref, bcent, flags, own_ref, before, avg_ref, top_ref, feat, rows, bfeat, acc):
@@ -232,7 +236,7 @@
                 acc[pl.ds(a * 2 + c, 1), :] += s
         return carry
 
-    lax.fori_loop(0, 2, side, 0)
+    lax.fori_loop(0, 2, side, 0, unroll=2)
     top = None
     for r in range(0, NB, 12):
         s = [acc[pl.ds(r * 2 + k, 12, stride=2), :] for k in range(2)]
@@ -314,6 +318,7 @@
 
 
 def on_device(coords, strain, kappa_old, counts, pair_mask):
+    raw = (counts.reshape(BX, 1, BY), coords.reshape(3 * NB, 1, PTS), strain.reshape(NB, 1, PTS))
     (own,) = call(
         pack_kernel,
         [((4 * NB, PTS), F32)],
@@ -325,30 +330,32 @@
             pltpu.VMEM((NB, 1, PTS), F32),
             pltpu.SemaphoreType.DMA((3,)),
         ],
-    )(counts.reshape(BX, 1, BY), coords.reshape(3 * NB, 1, PTS), strain.reshape(NB, 1, PTS))
+    )(*(pltpu.with_memory_space_constraint(v, pltpu.HBM) for v in raw))
     swap = [(0, 1), (1, 0)]
     beside = lambda n: [p for i in range(1, n - 1, 2) for p in ((i, i + 1), (i + 1, i))]
     other = lax.ppermute(own, "ply", swap)
-    acc, bcent, flags = call(
+    tile = feature_scratch(NB)
+    acc, bcent, flags, own_rows, own_bfeat = call(
         own_kernel,
-        [SUMS, ((NB, PTS, K), BF16), ((NB * FLAGS, PTS), F32)],
+        [SUMS, ((NB, PTS, K), BF16), ((NB * FLAGS, PTS), F32)] + tile[1:],
         2,
-        [((PTS, PTS), F32), ((NB * K, PTS), F32)] + feature_scratch(NB),
+        [((PTS, PTS), F32), ((NB * K, PTS), F32)] + tile[:1],
         6,
     )(pair_mask.reshape(NB, 1, 26), own)
 
     strip = ((8 * BY, PTS), F32)
     core, far = call(strips_kernel, [strip, strip], 2)(own, other)
+    far = lax.ppermute(far, ("y", "core"), beside(8))
     core = lax.ppermute(core, "core", swap)
-    far = lax.ppermute(far, ("y", "core"), beside(8))
-    tile = feature_scratch(NB)
     acc, rows, bfeat = call(other_kernel, [SUMS] + tile[1:], 4, tile[:1], 3)(other, bcent, flags, acc)
 
     column = ((8 * WX, PTS), F32)
     ynear, yfar = call(columns_kernel, [column, column], 4)(own, other, core, far)
+    yfar = lax.ppermute(yfar, ("z", "xlo"), beside(16))
     ynear = lax.ppermute(ynear, "xlo", swap)
-    yfar = lax.ppermute(yfar, ("z", "xlo"), beside(16))
-    (acc,) = call(x_kernel, [SUMS], 7, feature_scratch(4 * BY), 4)(core, far, bcent, flags, rows, bfeat, acc)
+    (acc,) = call(x_kernel, [SUMS], 9, feature_scratch(4 * BY), 4)(
+        core, far, bcent, flags, own_rows, own_bfeat, rows, bfeat, acc
+    )
     averaged, top = call(y_kernel, [((NB, PTS), F32), ((8, PTS), F32)], 6, feature_scratch(4 * WX) + [SUMS], 2)(
         ynear, yfar, bcent, flags, own, acc
     )

time: 56 us -> 52.6 us (0.939)
  local copies, waits for them, and re-layouts: 2.27 us -> 0.05 us
  Pallas kernels: 14.3 us -> 12.6 us
    unnamed x10 -> x4, local copies, waits for them, and re-layouts: 2.22 us -> 0.01 us
    pallas_call x2, Pallas kernels: 9.34 us -> 7.92 us  [the longest x1 4.26 us: on_device(): call(own_kernel, [SUMS, ((NB, PTS, K), BF16), ((NB * FLAGS, PTS), F32)] +...]
  transfers between devices with their start and end apart: 6 -> 6, of which waited for: 1 -> 2; matrix products, arithmetic and copies ran while one was open for 0% -> 0% of each run, Pallas kernels for 20% -> 18%
where the time goes in v4:
time: 52.6 us; the launch traced here: 52.4 us
  blocking collectives  28.6 us (54%)
  Pallas kernels  12.6 us (24%)
  starting transfers between devices  8.69 us (17%)
  waiting for transfers between devices  1.7 us (3%)
  between operations  0.73 us (1%)
    all_to_all x1, blocking collectives, on_device(): lax.all_to_all(jnp.broadcast_to(top[:1], (128, PTS)), ('ply', 'y', 'z', '...  28.6 us
    pallas_call x1, Pallas kernels, on_device(): call(own_kernel, [SUMS, ((NB, PTS, K), BF16), ((NB * FLAGS, PTS), F32)] +...  4.26 us
    pallas_call x1, Pallas kernels, on_device(): call(x_kernel, [SUMS], 9, feature_scratch(4 * BY), 4)  3.66 us
    ppermute x1, starting transfers between devices, on_device(): other = lax.ppermute(own, 'ply', swap)  3.65 us
    ppermute x1, starting transfers between devices, on_device(): far = lax.ppermute(far, ('y', 'core'), beside(8))  2.85 us
    pallas_call x1, Pallas kernels, on_device(): call(other_kernel, [SUMS] + tile[1:], 4, tile[:1], 3)  1.73 us
    ppermute x1, starting transfers between devices, on_device(): core = lax.ppermute(core, 'core', swap)  1.29 us
    pallas_call x1, Pallas kernels, on_device(): call(y_kernel, [((NB, PTS), F32), ((8, PTS), F32)], 6, feature_scratch(4...  1.28 us
  transfers between devices with their start and end apart: 6, of which 2 were waited for; matrix products, arithmetic and copies ran while one was open for 0% of the time, Pallas kernels for 18%

profile of v4, /device:TPU:1, one launch (start us, length us, event | category | flops | bytes accessed | tf_op | source)
XLA Modules:
  0.0 52.4 jit_solution(5102757213626671100)
XLA Ops:
  0.6 0.0 copy-start
  0.6 0.9 %pack_kernel.1.own_ref = f32[144,128]{1,0:T(8,128)S(1)} custom-call(s32[6,1,6]{2,1,0:T(1,128)} %bitcast.15, f32[108,1,128]{2,1,0:T(1,128)} %bitcast.13, f32[36,1,128]{2,1,0:T(1,128)} %bitcast.14), custom_call_target="tpu_custom_call" | custom-call | flops 400000000 | bytes 65536 | tf_op jit(solution)/shard_map/pack_kernel/pallas_call | solution.py:322
  1.6 3.6 %collective-permute-start = (f32[144,128]{1,0:T(8,128)S(1)}, f32[144,128]{1,0:T(8,128)S(1)}, u32[]{:S(2)}, u32[]{:S(2)}) collective-permute-start(f32[144,128]{1,0:T(8,128)S(1)} %pack_kernel.1.own_ref), channel_id=1, source_target_pairs={{0,128},{128,0},{1,129},{129,1},{2,130},{130,2},{3,131},{131,3},{4... | collective-permute-start | bytes 221192 | tf_op jit(solution)/shard_map/ppermute | solution.py:336
  5.2 0.0 copy-done
  5.2 4.3 %own_kernel.1 = (f32[72,128]{1,0:T(8,128)S(1)}, bf16[36,128,16]{2,1,0:T(8,128)(2,1)S(1)}, f32[1152,128]{1,0:T(8,128)S(1)}, f32[36,128]{1,0:T(8,128)S(1)}, bf16[36,16,128]{2,1,0:T(8,128)(2,1)S(1)}) custom-call(s32[36,1,26]{2,1,0:T(1,128)S(1)} %bitcast.11, f32[144,128]{1,0:T(8,128)S(1)} %pack_kernel.1.own_ref), custom_call_target="tpu_custom_call" | custom-call | flops 2400000000 | bytes 65536 | tf_op jit(solution)/shard_map/own_kernel/pallas_call | solution.py:338
  9.5 0.0 collective-permute-done.other_ref
  9.5 1.3 %collective-permute-start.1 = (f32[48,128]{1,0:T(8,128)S(1)}, f32[48,128]{1,0:T(8,128)S(1)}, u32[]{:S(2)}, u32[]{:S(2)}) collective-permute-start(f32[48,128]{1,0:T(8,128)S(1)} %get-tuple-element.18), channel_id=1, source_target_pairs={{0,16},{16,0},{1,17},{17,1},{2,18},{18,2},{3,19},{19,3},{4,20},{20... | collective-permute-start | bytes 73736 | tf_op jit(solution)/shard_map/ppermute | solution.py:349
  10.8 2.9 %collective-permute-start.2 = (f32[48,128]{1,0:T(8,128)S(1)}, f32[48,128]{1,0:T(8,128)S(1)}, u32[]{:S(2)}, u32[]{:S(2)}) collective-permute-start(f32[48,128]{1,0:T(8,128)S(1)} %get-tuple-element.19), channel_id=1, source_target_pairs={{16,32},{32,16},{48,64},{64,48},{80,96},{96,80},{17,33},{33,17},{4... | collective-permute-start | bytes 73736 | tf_op jit(solution)/shard_map/ppermute | solution.py:348
  13.6 1.7 %other_kernel.1 = (f32[72,128]{1,0:T(8,128)S(1)}, f32[36,128]{1,0:T(8,128)S(1)}, bf16[36,16,128]{2,1,0:T(8,128)(2,1)S(1)}) custom-call(f32[144,128]{1,0:T(8,128)S(1)} %collective-permute-done.other_ref, bf16[36,128,16]{2,1,0:T(8,128)(2,1)S(1)} %get-tuple-element.22.bcent, f32[1152,128]{1,0:T(8,128)S(1)} %get-tuple-element.23.flags, ...), custom_call_target="tpu_custom_call" | custom-call | flops 1200000000 | bytes 65536 | tf_op jit(solution)/shard_map/other_kernel/pallas_call | solution.py:350
  15.4 0.0 collective-permute-done.1.core_ref
  15.4 0.5 %collective-permute-done.2.far_ref = f32[48,128]{1,0:T(8,128)S(1)} collective-permute-done((f32[48,128]{1,0:T(8,128)S(1)}, f32[48,128]{1,0:T(8,128)S(1)}, u32[]{:S(2)}, u32[]{:S(2)}) %collective-permute-start.2) | collective-permute-done | bytes 24608 | tf_op jit(solution)/shard_map/ppermute | solution.py:348
  15.9 0.2 collective-permute-start.3
  16.1 0.7 %collective-permute-start.4 = (f32[64,128]{1,0:T(8,128)S(1)}, f32[64,128]{1,0:T(8,128)S(1)}, u32[]{:S(2)}, u32[]{:S(2)}) collective-permute-start(f32[64,128]{1,0:T(8,128)S(1)} %get-tuple-element.21), channel_id=1, source_target_pairs={{1,2},{2,1},{3,4},{4,3},{5,6},{6,5},{7,8},{8,7},{9,10},{10,9},{11,... | collective-permute-start | bytes 98312 | tf_op jit(solution)/shard_map/ppermute | solution.py:354
  16.8 3.7 %x_kernel.1.before = f32[72,128]{1,0:T(8,128)S(1)} custom-call(f32[48,128]{1,0:T(8,128)S(1)} %collective-permute-done.1.core_ref, f32[48,128]{1,0:T(8,128)S(1)} %collective-permute-done.2.far_ref, bf16[36,128,16]{2,1,0:T(8,128)(2,1)S(1)} %get-tuple-element.22.bcent, f32[1152,128]{1,0:T(8,128)S(1)} %get-tuple-element.23.flags, ...), custom_call_target="tpu_custom_call" | custom-call | flops 1600000000 | bytes 65536 | tf_op jit(solution)/shard_map/x_kernel/pallas_call | solution.py:356
  20.4 0.0 copy-start.1
  20.4 0.0 collective-permute-done.3.near_ref
  20.4 0.0 collective-permute-done.4.far_ref
  20.5 1.3 %y_kernel.1 = (f32[36,128]{1,0:T(8,128)S(1)}, f32[8,128]{1,0:T(8,128)S(1)}) custom-call(f32[64,128]{1,0:T(8,128)S(1)} %collective-permute-done.3.near_ref, f32[64,128]{1,0:T(8,128)S(1)} %collective-permute-done.4.far_ref, bf16[36,128,16]{2,1,0:T(8,128)(2,1)S(1)} %get-tuple-element.22.bcent, f32[1152,128]{1,0:T(8,128)S(1)} %get-tuple-element.23.flags, ...), custom_call_target="tpu_custom_call" | custom-call | flops 800000000 | bytes 65536 | tf_op jit(solution)/shard_map/y_kernel/pallas_call | solution.py:359
  21.7 0.1 collective-permute-start.5
  21.8 1.2 %collective-permute-done.5 = f32[8,128]{1,0:T(8,128)S(1)} collective-permute-done((f32[8,128]{1,0:T(8,128)S(1)}, f32[8,128]{1,0:T(8,128)S(1)}, u32[]{:S(2)}, u32[]{:S(2)}) %collective-permute-start.5) | collective-permute-done | bytes 4128 | tf_op jit(solution)/shard_map/ppermute | solution.py:363
  23.0 28.6 %all_to_all.8 = f32[128,1,128]{2,1,0:T(1,128)S(1)} all-to-all(f32[128,1,128]{2,1,0:T(1,128)S(1)} %broadcast_in_dim.2), channel_id=1, replica_groups=mesh['ply'=2,'y'=4,'core'=2,'z'=8,'xlo'=2] {'ply','y','z','xlo'}, dimensions={0} | all-to-all | bytes 131072 | tf_op jit(solution)/shard_map/all_to_all | solution.py:364
  51.6 0.0 copy-done.1
  51.6 0.8 %final_kernel.1 = (f32[36,1,128]{2,1,0:T(1,128)}, f32[36,1,128]{2,1,0:T(1,128)}) custom-call(f32[128,128]{1,0:T(8,128)S(1)} %bitcast.10, f32[36,128]{1,0:T(8,128)S(1)} %get-tuple-element.31.avg_ref, f32[36,1,128]{2,1,0:T(1,128)S(1)} %bitcast.12, f32[144,128]{1,0:T(8,128)S(1)} %pack_kernel.1.own_ref), custom_call_target="tpu_custom_call" | custom-call | flops 400000000 | bytes 65536 | tf_op jit(solution)/shard_map/final_kernel/pallas_call | solution.py:365
  (5 shorter events, 0.1 us)
Async XLA Ops:
  0.6 4.6 %copy-start = (s32[1,6,6,26]{3,0,2,1:T(1,128)S(1)}, s32[1,6,6,26]{3,0,2,1:T(1,128)}, u32[]{:S(2)}) copy-start(s32[1,6,6,26]{3,0,2,1:T(1,128)} %param.9) | copy-start | bytes 11236
  1.6 7.9 %collective-permute-start = (f32[144,128]{1,0:T(8,128)S(1)}, f32[144,128]{1,0:T(8,128)S(1)}, u32[]{:S(2)}, u32[]{:S(2)}) collective-permute-start(f32[144,128]{1,0:T(8,128)S(1)} %pack_kernel.1.own_ref), channel_id=1, source_target_pairs={{0,128},{128,0},{1,129},{129,1},{2,130},{130,2},{3,131},{131,3},{4... | collective-permute-start | bytes 221192 | tf_op jit(solution)/shard_map/ppermute | solution.py:336
  9.5 5.9 %collective-permute-start.1 = (f32[48,128]{1,0:T(8,128)S(1)}, f32[48,128]{1,0:T(8,128)S(1)}, u32[]{:S(2)}, u32[]{:S(2)}) collective-permute-start(f32[48,128]{1,0:T(8,128)S(1)} %get-tuple-element.18), channel_id=1, source_target_pairs={{0,16},{16,0},{1,17},{17,1},{2,18},{18,2},{3,19},{19,3},{4,20},{20... | collective-permute-start | bytes 73736 | tf_op jit(solution)/shard_map/ppermute | solution.py:349
  10.8 5.1 %collective-permute-start.2 = (f32[48,128]{1,0:T(8,128)S(1)}, f32[48,128]{1,0:T(8,128)S(1)}, u32[]{:S(2)}, u32[]{:S(2)}) collective-permute-start(f32[48,128]{1,0:T(8,128)S(1)} %get-tuple-element.19), channel_id=1, source_target_pairs={{16,32},{32,16},{48,64},{64,48},{80,96},{96,80},{17,33},{33,17},{4... | collective-permute-start | bytes 73736 | tf_op jit(solution)/shard_map/ppermute | solution.py:348
  15.9 4.5 %collective-permute-start.3 = (f32[64,128]{1,0:T(8,128)S(1)}, f32[64,128]{1,0:T(8,128)S(1)}, u32[]{:S(2)}, u32[]{:S(2)}) collective-permute-start(f32[64,128]{1,0:T(8,128)S(1)} %get-tuple-element.20), channel_id=1, source_target_pairs={{0,1},{1,0},{2,3},{3,2},{4,5},{5,4},{6,7},{7,6},{8,9},{9,8},{10,11... | collective-permute-start | bytes 98312 | tf_op jit(solution)/shard_map/ppermute | solution.py:355
  16.1 4.3 %collective-permute-start.4 = (f32[64,128]{1,0:T(8,128)S(1)}, f32[64,128]{1,0:T(8,128)S(1)}, u32[]{:S(2)}, u32[]{:S(2)}) collective-permute-start(f32[64,128]{1,0:T(8,128)S(1)} %get-tuple-element.21), channel_id=1, source_target_pairs={{1,2},{2,1},{3,4},{4,3},{5,6},{6,5},{7,8},{8,7},{9,10},{10,9},{11,... | collective-permute-start | bytes 98312 | tf_op jit(solution)/shard_map/ppermute | solution.py:354
  20.4 31.2 %copy-start.1 = (f32[1,6,6,128]{3,0,2,1:T(1,128)S(1)}, f32[1,6,6,128]{3,0,2,1:T(1,128)}, u32[]{:S(2)}) copy-start(f32[1,6,6,128]{3,0,2,1:T(1,128)} %param.7) | copy-start | bytes 55300
  21.7 1.3 %collective-permute-start.5 = (f32[8,128]{1,0:T(8,128)S(1)}, f32[8,128]{1,0:T(8,128)S(1)}, u32[]{:S(2)}, u32[]{:S(2)}) collective-permute-start(f32[8,128]{1,0:T(8,128)S(1)} %get-tuple-element.30), channel_id=1, source_target_pairs={{0,16},{16,0},{1,17},{17,1},{2,18},{18,2},{3,19},{19,3},{4,20},{20... | collective-permute-start | bytes 12296 | tf_op jit(solution)/shard_map/ppermute | solution.py:363

commit v5 on v4

--- a/solution.py
+++ b/solution.py
@@ -21,7 +21,7 @@
 
 def pieces_of(v, count):
     out = []
-    for n in range(count):
+    for _ in range(count):
         high = v.astype(BF16).astype(F32)
         out.append(high)
         v = v - high
@@ -306,7 +306,6 @@
         scratch_shapes=[pltpu.VMEM(s, d) for s, d in scratch] + list(extra),
         compiler_params=pltpu.CompilerParams(vmem_limit_bytes=16 << 20),
         cost_estimate=pl.CostEstimate(flops=us * 400_000_000, bytes_accessed=1 << 16, transcendentals=0),
-        name=kernel.__name__,
     )
 
 
@@ -360,8 +359,7 @@
         ynear, yfar, bcent, flags, own, acc
     )
 
-    top = jnp.maximum(top, lax.ppermute(top, "core", swap))
-    tops = lax.all_to_all(jnp.broadcast_to(top[:1], (128, PTS)), ("ply", "y", "z", "xlo"), 0, 0, tiled=True)
+    tops = lax.all_to_all(jnp.broadcast_to(top[:1], (256, PTS)), AXES, 0, 0, tiled=True)
     new, damage = call(final_kernel, [((NB, 1, PTS), F32)] * 2, 4)(tops, averaged, kappa_old.reshape(NB, 1, PTS), own)
     return (new.reshape(1, BX, BY, PTS), damage.reshape(1, BX, BY, PTS))
 
@@ -376,6 +374,7 @@
         P("ply", gx, gy),
         P("ply", gx, gy, None),
     )
+
     return jax.shard_map(
         on_device,
         mesh=fine,

time: 52.6 us -> 52.7 us (level)
  blocking collectives: 28.6 us -> 29.9 us
  waiting for transfers between devices: 1.7 us -> 0.55 us
    all_to_all x1, blocking collectives: 28.6 us -> 29.9 us  [on_device(): lax.all_to_all(jnp.broadcast_to(top[:1], (256, PTS)), AXES, 0, 0, tiled=T...]
    ppermute x1 -> x0, waiting for transfers between devices: 1.15 us -> none  [on_device(): top = jnp.maximum(top, lax.ppermute(top, 'core', swap))]
  transfers between devices with their start and end apart: 6 -> 5, of which waited for: 2 -> 1; matrix products, arithmetic and copies ran while one was open for 0% -> 0% of each run, Pallas kernels for 18% -> 18%
where the time goes in v5:
time: 52.7 us; the launch traced here: 52.5 us
  blocking collectives  29.9 us (57%)
  Pallas kernels  12.6 us (24%)
  starting transfers between devices  8.59 us (16%)
  between operations  0.73 us (1%)
  waiting for transfers between devices  0.55 us (1%)
    all_to_all x1, blocking collectives, on_device(): lax.all_to_all(jnp.broadcast_to(top[:1], (256, PTS)), AXES, 0, 0, tiled=T...  29.9 us
    pallas_call x1, Pallas kernels, on_device(): call(own_kernel, [SUMS, ((NB, PTS, K), BF16), ((NB * FLAGS, PTS), F32)] +...  4.26 us
    pallas_call x1, Pallas kernels, on_device(): call(x_kernel, [SUMS], 9, feature_scratch(4 * BY), 4)  3.66 us
    ppermute x1, starting transfers between devices, on_device(): other = lax.ppermute(own, 'ply', swap)  3.65 us
    ppermute x1, starting transfers between devices, on_device(): far = lax.ppermute(far, ('y', 'core'), beside(8))  2.85 us
    pallas_call x1, Pallas kernels, on_device(): call(other_kernel, [SUMS] + tile[1:], 4, tile[:1], 3)  1.73 us
    ppermute x1, starting transfers between devices, on_device(): core = lax.ppermute(core, 'core', swap)  1.29 us
    pallas_call x1, Pallas kernels, on_device(): call(y_kernel, [((NB, PTS), F32), ((8, PTS), F32)], 6, feature_scratch(4...  1.28 us
  transfers between devices with their start and end apart: 5, of which 1 were waited for; matrix products, arithmetic and copies ran while one was open for 0% of the time, Pallas kernels for 18%

profile of v5, /device:TPU:1, one launch (start us, length us, event | category | flops | bytes accessed | tf_op | source)
XLA Modules:
  0.0 52.5 jit_solution(15643218190032528953)
XLA Ops:
  0.6 0.0 copy-start
  0.6 0.9 %shard_map.68.own_ref = f32[144,128]{1,0:T(8,128)S(1)} custom-call(s32[6,1,6]{2,1,0:T(1,128)} %bitcast.15, f32[108,1,128]{2,1,0:T(1,128)} %bitcast.13, f32[36,1,128]{2,1,0:T(1,128)} %bitcast.14), custom_call_target="tpu_custom_call" | custom-call | flops 400000000 | bytes 65536 | tf_op jit(solution)/shard_map/pallas_call | solution.py:321
  1.6 3.6 %collective-permute-start = (f32[144,128]{1,0:T(8,128)S(1)}, f32[144,128]{1,0:T(8,128)S(1)}, u32[]{:S(2)}, u32[]{:S(2)}) collective-permute-start(f32[144,128]{1,0:T(8,128)S(1)} %shard_map.68.own_ref), channel_id=1, source_target_pairs={{0,128},{128,0},{1,129},{129,1},{2,130},{130,2},{3,131},{131,3},{4... | collective-permute-start | bytes 221192 | tf_op jit(solution)/shard_map/ppermute | solution.py:335
  5.2 0.0 copy-done
  5.2 4.3 %shard_map.71 = (f32[72,128]{1,0:T(8,128)S(1)}, bf16[36,128,16]{2,1,0:T(8,128)(2,1)S(1)}, f32[1152,128]{1,0:T(8,128)S(1)}, f32[36,128]{1,0:T(8,128)S(1)}, bf16[36,16,128]{2,1,0:T(8,128)(2,1)S(1)}) custom-call(s32[36,1,26]{2,1,0:T(1,128)S(1)} %bitcast.11, f32[144,128]{1,0:T(8,128)S(1)} %shard_map.68.own_ref), custom_call_target="tpu_custom_call" | custom-call | flops 2400000000 | bytes 65536 | tf_op jit(solution)/shard_map/pallas_call | solution.py:337
  9.5 0.0 collective-permute-done.other_ref
  9.5 1.3 %collective-permute-start.1 = (f32[48,128]{1,0:T(8,128)S(1)}, f32[48,128]{1,0:T(8,128)S(1)}, u32[]{:S(2)}, u32[]{:S(2)}) collective-permute-start(f32[48,128]{1,0:T(8,128)S(1)} %get-tuple-element.18), channel_id=1, source_target_pairs={{0,16},{16,0},{1,17},{17,1},{2,18},{18,2},{3,19},{19,3},{4,20},{20... | collective-permute-start | bytes 73736 | tf_op jit(solution)/shard_map/ppermute | solution.py:348
  10.8 2.9 %collective-permute-start.2 = (f32[48,128]{1,0:T(8,128)S(1)}, f32[48,128]{1,0:T(8,128)S(1)}, u32[]{:S(2)}, u32[]{:S(2)}) collective-permute-start(f32[48,128]{1,0:T(8,128)S(1)} %get-tuple-element.19), channel_id=1, source_target_pairs={{16,32},{32,16},{48,64},{64,48},{80,96},{96,80},{17,33},{33,17},{4... | collective-permute-start | bytes 73736 | tf_op jit(solution)/shard_map/ppermute | solution.py:347
  13.6 1.7 %shard_map.72 = (f32[72,128]{1,0:T(8,128)S(1)}, f32[36,128]{1,0:T(8,128)S(1)}, bf16[36,16,128]{2,1,0:T(8,128)(2,1)S(1)}) custom-call(f32[144,128]{1,0:T(8,128)S(1)} %collective-permute-done.other_ref, bf16[36,128,16]{2,1,0:T(8,128)(2,1)S(1)} %get-tuple-element.22.bcent, f32[1152,128]{1,0:T(8,128)S(1)} %get-tuple-element.23.flags, ...), custom_call_target="tpu_custom_call" | custom-call | flops 1200000000 | bytes 65536 | tf_op jit(solution)/shard_map/pallas_call | solution.py:349
  15.4 0.0 collective-permute-done.1.core_ref
  15.4 0.5 %collective-permute-done.2.far_ref = f32[48,128]{1,0:T(8,128)S(1)} collective-permute-done((f32[48,128]{1,0:T(8,128)S(1)}, f32[48,128]{1,0:T(8,128)S(1)}, u32[]{:S(2)}, u32[]{:S(2)}) %collective-permute-start.2) | collective-permute-done | bytes 24608 | tf_op jit(solution)/shard_map/ppermute | solution.py:347
  15.9 0.2 collective-permute-start.3
  16.1 0.7 %collective-permute-start.4 = (f32[64,128]{1,0:T(8,128)S(1)}, f32[64,128]{1,0:T(8,128)S(1)}, u32[]{:S(2)}, u32[]{:S(2)}) collective-permute-start(f32[64,128]{1,0:T(8,128)S(1)} %get-tuple-element.21), channel_id=1, source_target_pairs={{1,2},{2,1},{3,4},{4,3},{5,6},{6,5},{7,8},{8,7},{9,10},{10,9},{11,... | collective-permute-start | bytes 98312 | tf_op jit(solution)/shard_map/ppermute | solution.py:353
  16.8 3.7 %shard_map.73.before = f32[72,128]{1,0:T(8,128)S(1)} custom-call(f32[48,128]{1,0:T(8,128)S(1)} %collective-permute-done.1.core_ref, f32[48,128]{1,0:T(8,128)S(1)} %collective-permute-done.2.far_ref, bf16[36,128,16]{2,1,0:T(8,128)(2,1)S(1)} %get-tuple-element.22.bcent, f32[1152,128]{1,0:T(8,128)S(1)} %get-tuple-element.23.flags, ...), custom_call_target="tpu_custom_call" | custom-call | flops 1600000000 | bytes 65536 | tf_op jit(solution)/shard_map/pallas_call | solution.py:355
  20.4 0.0 copy-start.1
  20.4 0.0 collective-permute-done.3.near_ref
  20.4 0.0 collective-permute-done.4.far_ref
  20.5 1.3 %shard_map.74 = (f32[36,128]{1,0:T(8,128)S(1)}, f32[8,128]{1,0:T(8,128)S(1)}) custom-call(f32[64,128]{1,0:T(8,128)S(1)} %collective-permute-done.3.near_ref, f32[64,128]{1,0:T(8,128)S(1)} %collective-permute-done.4.far_ref, bf16[36,128,16]{2,1,0:T(8,128)(2,1)S(1)} %get-tuple-element.22.bcent, f32[1152,128]{1,0:T(8,128)S(1)} %get-tuple-element.23.flags, ...), custom_call_target="tpu_custom_call" | custom-call | flops 800000000 | bytes 65536 | tf_op jit(solution)/shard_map/pallas_call | solution.py:358
  21.7 0.1 broadcast_in_dim.2
  21.8 29.9 %all_to_all.8 = f32[256,1,128]{2,1,0:T(1,128)S(1)} all-to-all(f32[256,1,128]{2,1,0:T(1,128)S(1)} %broadcast_in_dim.2), channel_id=1, replica_groups=mesh['ply'=2,'y'=4,'core'=2,'z'=8,'xlo'=2] {'ply','y','core','z','xlo'}, dimensions={0} | all-to-all | bytes 262144 | tf_op jit(solution)/shard_map/all_to_all | solution.py:362
  51.7 0.0 copy-done.1
  51.7 0.8 %shard_map.75 = (f32[36,1,128]{2,1,0:T(1,128)}, f32[36,1,128]{2,1,0:T(1,128)}) custom-call(f32[256,128]{1,0:T(8,128)S(1)} %bitcast.10, f32[36,128]{1,0:T(8,128)S(1)} %get-tuple-element.31.avg_ref, f32[36,1,128]{2,1,0:T(1,128)S(1)} %bitcast.12, f32[144,128]{1,0:T(8,128)S(1)} %shard_map.68.own_ref), custom_call_target="tpu_custom_call" | custom-call | flops 400000000 | bytes 65536 | tf_op jit(solution)/shard_map/pallas_call | solution.py:363
  (3 shorter events, 0.0 us)
Async XLA Ops:
  0.6 4.6 %copy-start = (s32[1,6,6,26]{3,0,2,1:T(1,128)S(1)}, s32[1,6,6,26]{3,0,2,1:T(1,128)}, u32[]{:S(2)}) copy-start(s32[1,6,6,26]{3,0,2,1:T(1,128)} %param.9) | copy-start | bytes 11236
  1.6 7.9 %collective-permute-start = (f32[144,128]{1,0:T(8,128)S(1)}, f32[144,128]{1,0:T(8,128)S(1)}, u32[]{:S(2)}, u32[]{:S(2)}) collective-permute-start(f32[144,128]{1,0:T(8,128)S(1)} %shard_map.68.own_ref), channel_id=1, source_target_pairs={{0,128},{128,0},{1,129},{129,1},{2,130},{130,2},{3,131},{131,3},{4... | collective-permute-start | bytes 221192 | tf_op jit(solution)/shard_map/ppermute | solution.py:335
  9.5 5.9 %collective-permute-start.1 = (f32[48,128]{1,0:T(8,128)S(1)}, f32[48,128]{1,0:T(8,128)S(1)}, u32[]{:S(2)}, u32[]{:S(2)}) collective-permute-start(f32[48,128]{1,0:T(8,128)S(1)} %get-tuple-element.18), channel_id=1, source_target_pairs={{0,16},{16,0},{1,17},{17,1},{2,18},{18,2},{3,19},{19,3},{4,20},{20... | collective-permute-start | bytes 73736 | tf_op jit(solution)/shard_map/ppermute | solution.py:348
  10.8 5.1 %collective-permute-start.2 = (f32[48,128]{1,0:T(8,128)S(1)}, f32[48,128]{1,0:T(8,128)S(1)}, u32[]{:S(2)}, u32[]{:S(2)}) collective-permute-start(f32[48,128]{1,0:T(8,128)S(1)} %get-tuple-element.19), channel_id=1, source_target_pairs={{16,32},{32,16},{48,64},{64,48},{80,96},{96,80},{17,33},{33,17},{4... | collective-permute-start | bytes 73736 | tf_op jit(solution)/shard_map/ppermute | solution.py:347
  15.9 4.5 %collective-permute-start.3 = (f32[64,128]{1,0:T(8,128)S(1)}, f32[64,128]{1,0:T(8,128)S(1)}, u32[]{:S(2)}, u32[]{:S(2)}) collective-permute-start(f32[64,128]{1,0:T(8,128)S(1)} %get-tuple-element.20), channel_id=1, source_target_pairs={{0,1},{1,0},{2,3},{3,2},{4,5},{5,4},{6,7},{7,6},{8,9},{9,8},{10,11... | collective-permute-start | bytes 98312 | tf_op jit(solution)/shard_map/ppermute | solution.py:354
  16.1 4.3 %collective-permute-start.4 = (f32[64,128]{1,0:T(8,128)S(1)}, f32[64,128]{1,0:T(8,128)S(1)}, u32[]{:S(2)}, u32[]{:S(2)}) collective-permute-start(f32[64,128]{1,0:T(8,128)S(1)} %get-tuple-element.21), channel_id=1, source_target_pairs={{1,2},{2,1},{3,4},{4,3},{5,6},{6,5},{7,8},{8,7},{9,10},{10,9},{11,... | collective-permute-start | bytes 98312 | tf_op jit(solution)/shard_map/ppermute | solution.py:353
  20.4 31.3 %copy-start.1 = (f32[1,6,6,128]{3,0,2,1:T(1,128)S(1)}, f32[1,6,6,128]{3,0,2,1:T(1,128)}, u32[]{:S(2)}) copy-start(f32[1,6,6,128]{3,0,2,1:T(1,128)} %param.7) | copy-start | bytes 55300

commit v6 on v5

--- a/solution.py
+++ b/solution.py
@@ -12,6 +12,7 @@
 WX = BX + 2
 PTS = 128
 K = 16
+MID = NB - 2 * BY
 FLAGS = 32
 AXES = ("ply", "y", "core", "z", "xlo")
 F32 = jnp.float32
@@ -164,9 +165,13 @@
     acc[pl.ds(2 * (BX - 2) * BY, 2 * BY), :] = jnp.zeros((2 * BY, PTS), F32)
 
 
-def other_kernel(other_ref, bcent, flags, before, acc, rows, bfeat, feat):
+def other_kernel(edge_ref, mid_ref, bcent, flags, before, acc, rows, bfeat, feat):
     for x in range(BX):
-        highs, lows, norm, strain = positions(other_ref, x * BY, BY, 1, NB, float(x - BX // 2), y_in(), other_shift())
+        if x in (0, BX - 1):
+            place = (edge_ref, min(x, 1) * BY, BY, 1, 2 * BY)
+        else:
+            place = (mid_ref, (x - 1) * BY, BY, 1, MID)
+        highs, lows, norm, strain = positions(*place, float(x - BX // 2), y_in(), other_shift())
         put_neighbour(feat, rows, x * BY, highs, lows, norm, strain)
     round_tiles(feat, bfeat, NB, 6)
     acc[...] = before[...]
@@ -247,7 +252,7 @@
     top_ref[...] = jnp.broadcast_to(jnp.max(top, axis=0, keepdims=True), (8, PTS))
 
 
-def pack_kernel(counts_hbm, coords_hbm, strain_hbm, own_ref, counts_ref, coords_ref, strain_ref, sems):
+def pack_kernel(counts_hbm, coords_hbm, strain_hbm, own_ref, edge_ref, mid_ref, counts_ref, coords_ref, strain_ref, sems):
     copies = [
         pltpu.make_async_copy(source, target, sems.at[n])
         for n, (source, target) in enumerate(
@@ -264,25 +269,31 @@
     for b in range(NB):
         live = slots < counts_ref[b // BY, 0, b % BY]
         own_ref[pl.ds(3 * NB + b, 1), :] = jnp.where(live, strain_ref[b], 0.0)
-
-
-def strips_kernel(own_ref, other_ref, core_ref, far_ref):
+    for c in range(4):
+        edge_ref[pl.ds(c * 2 * BY, BY), :] = own_ref[pl.ds(c * NB, BY), :]
+        edge_ref[pl.ds(c * 2 * BY + BY, BY), :] = own_ref[pl.ds(c * NB + NB - BY, BY), :]
+        mid_ref[pl.ds(c * MID, MID), :] = own_ref[pl.ds(c * NB + BY, MID), :]
+
+
+def strips_kernel(own_edge_ref, other_edge_ref, core_ref, far_ref):
     core = lax.axis_index("core")
     for slot, out in enumerate((core_ref, far_ref)):
         above = (1 - core) if slot == 0 else core
-        for layer, ref in enumerate((own_ref, other_ref)):
+        for layer, ref in enumerate((own_edge_ref, other_edge_ref)):
             for c in range(4):
-                out[pl.ds((layer * 4 + c) * BY, BY), :] = ref[pl.ds(c * NB + above * (BX - 1) * BY, BY), :]
-
-
-def columns_kernel(own_ref, other_ref, core_ref, far_ref, near_out, far_out):
+                out[pl.ds((layer * 4 + c) * BY, BY), :] = ref[pl.ds((c * 2 + above) * BY, BY), :]
+
+
+def columns_kernel(own_edge_ref, own_mid_ref, other_edge_ref, other_mid_ref, core_ref, far_ref, near_out, far_out):
     core, xlo = lax.axis_index("core"), lax.axis_index("xlo")
     for slot, out in enumerate((near_out, far_out)):
         y = ((1 - xlo) if slot == 0 else xlo) * (BY - 1)
-        for layer, ref in enumerate((own_ref, other_ref)):
+        for layer, (edge, mid) in enumerate(((own_edge_ref, own_mid_ref), (other_edge_ref, other_mid_ref))):
             for c in range(4):
                 row, halo = (layer * 4 + c) * WX, (layer * 4 + c) * BY
-                out[pl.ds(row + 1, BX), :] = ref[pl.ds(c * NB + y, BX, stride=BY), :]
+                out[pl.ds(row + 1, 1), :] = edge[pl.ds(c * 2 * BY + y, 1), :]
+                out[pl.ds(row + 2, BX - 2), :] = mid[pl.ds(c * MID + y, BX - 2, stride=BY), :]
+                out[pl.ds(row + BX, 1), :] = edge[pl.ds(c * 2 * BY + BY + y, 1), :]
                 out[pl.ds(row + (1 - core) * (WX - 1), 1), :] = core_ref[pl.ds(halo + y, 1), :]
                 out[pl.ds(row + core * (WX - 1), 1), :] = far_ref[pl.ds(halo + y, 1), :]
 
@@ -318,9 +329,9 @@
 
 def on_device(coords, strain, kappa_old, counts, pair_mask):
     raw = (counts.reshape(BX, 1, BY), coords.reshape(3 * NB, 1, PTS), strain.reshape(NB, 1, PTS))
-    (own,) = call(
+    own, own_edge, own_mid = call(
         pack_kernel,
-        [((4 * NB, PTS), F32)],
+        [((4 * NB, PTS), F32), ((8 * BY, PTS), F32), ((4 * MID, PTS), F32)],
         3,
         space=pl.BlockSpec(memory_space=pltpu.HBM),
         extra=[
@@ -332,7 +343,8 @@
     )(*(pltpu.with_memory_space_constraint(v, pltpu.HBM) for v in raw))
     swap = [(0, 1), (1, 0)]
     beside = lambda n: [p for i in range(1, n - 1, 2) for p in ((i, i + 1), (i + 1, i))]
-    other = lax.ppermute(own, "ply", swap)
+    other_edge = lax.ppermute(own_edge, "ply", swap)
+    other_mid = lax.ppermute(own_mid, "ply", swap)
     tile = feature_scratch(NB)
     acc, bcent, flags, own_rows, own_bfeat = call(
         own_kernel,
@@ -343,13 +355,13 @@
     )(pair_mask.reshape(NB, 1, 26), own)
 
     strip = ((8 * BY, PTS), F32)
-    core, far = call(strips_kernel, [strip, strip], 2)(own, other)
+    core, far = call(strips_kernel, [strip, strip], 2)(own_edge, other_edge)
     far = lax.ppermute(far, ("y", "core"), beside(8))
     core = lax.ppermute(core, "core", swap)
-    acc, rows, bfeat = call(other_kernel, [SUMS] + tile[1:], 4, tile[:1], 3)(other, bcent, flags, acc)
+    acc, rows, bfeat = call(other_kernel, [SUMS] + tile[1:], 5, tile[:1], 3)(other_edge, other_mid, bcent, flags, acc)
 
     column = ((8 * WX, PTS), F32)
-    ynear, yfar = call(columns_kernel, [column, column], 4)(own, other, core, far)
+    ynear, yfar = call(columns_kernel, [column, column], 6)(own_edge, own_mid, other_edge, other_mid, core, far)
     yfar = lax.ppermute(yfar, ("z", "xlo"), beside(16))
     ynear = lax.ppermute(ynear, "xlo", swap)
     (acc,) = call(x_kernel, [SUMS], 9, feature_scratch(4 * BY), 4)(

time: 52.7 us -> 54.9 us (1.042)
  starting transfers between devices: 8.59 us -> 11.1 us
  blocking collectives: 29.9 us -> 28.9 us
  waiting for transfers between devices: 0.55 us -> 1.13 us
    ppermute x1, starting transfers between devices: 1.29 us -> 4.1 us  [on_device(): core = lax.ppermute(core, 'core', swap)]
    ppermute x1 -> x2, waiting for transfers between devices: 0.01 us -> 1.12 us  [the longest x1 1.12 us: on_device(): other_edge = lax.ppermute(own_edge, 'ply', swap)]
    all_to_all x1, blocking collectives: 29.9 us -> 28.9 us  [on_device(): lax.all_to_all(jnp.broadcast_to(top[:1], (256, PTS)), AXES, 0, 0, tiled=T...]
    ppermute x1, starting transfers between devices: 2.85 us -> 1.91 us  [on_device(): far = lax.ppermute(far, ('y', 'core'), beside(8))]
    ppermute x1 -> x2, starting transfers between devices: 3.65 us -> 3.75 us  [the longest x1 3.65 us: on_device(): other_edge = lax.ppermute(own_edge, 'ply', swap)]
  transfers between devices with their start and end apart: 5 -> 6, of which waited for: 1 -> 1; matrix products, arithmetic and copies ran while one was open for 0% -> 0% of each run, Pallas kernels for 18% -> 18%
where the time goes in v6:
time: 54.9 us; the launch traced here: 54.7 us
  blocking collectives  28.9 us (53%)
  Pallas kernels  12.7 us (23%)
  starting transfers between devices  11.1 us (20%)
  waiting for transfers between devices  1.13 us (2%)
  between operations  0.75 us (1%)
    all_to_all x1, blocking collectives, on_device(): lax.all_to_all(jnp.broadcast_to(top[:1], (256, PTS)), AXES, 0, 0, tiled=T...  28.9 us
    pallas_call x1, Pallas kernels, on_device(): call(own_kernel, [SUMS, ((NB, PTS, K), BF16), ((NB * FLAGS, PTS), F32)] +...  4.26 us
    ppermute x1, starting transfers between devices, on_device(): core = lax.ppermute(core, 'core', swap)  4.1 us
    pallas_call x1, Pallas kernels, on_device(): call(x_kernel, [SUMS], 9, feature_scratch(4 * BY), 4)  3.69 us
    ppermute x1, starting transfers between devices, on_device(): other_edge = lax.ppermute(own_edge, 'ply', swap)  3.65 us
    ppermute x1, starting transfers between devices, on_device(): far = lax.ppermute(far, ('y', 'core'), beside(8))  1.91 us
    pallas_call x1, Pallas kernels, on_device(): call(other_kernel, [SUMS] + tile[1:], 5, tile[:1], 3)  1.75 us
    pallas_call x1, Pallas kernels, on_device(): call(y_kernel, [((NB, PTS), F32), ((8, PTS), F32)], 6, feature_scratch(4...  1.28 us
  transfers between devices with their start and end apart: 6, of which 1 were waited for; matrix products, arithmetic and copies ran while one was open for 0% of the time, Pallas kernels for 18%

profile of v6, /device:TPU:1, one launch (start us, length us, event | category | flops | bytes accessed | tf_op | source)
XLA Modules:
  0.0 54.7 jit_solution(18261620332158653228)
XLA Ops:
  0.6 0.0 copy-start
  0.6 0.9 %shard_map.68 = (f32[144,128]{1,0:T(8,128)S(1)}, f32[48,128]{1,0:T(8,128)S(1)}, f32[96,128]{1,0:T(8,128)S(1)}) custom-call(s32[6,1,6]{2,1,0:T(1,128)} %bitcast.15, f32[108,1,128]{2,1,0:T(1,128)} %bitcast.13, f32[36,1,128]{2,1,0:T(1,128)} %bitcast.14), custom_call_target="tpu_custom_call" | custom-call | flops 400000000 | bytes 65536 | tf_op jit(solution)/shard_map/pallas_call | solution.py:332
  1.6 3.6 %collective-permute-start = (f32[48,128]{1,0:T(8,128)S(1)}, f32[48,128]{1,0:T(8,128)S(1)}, u32[]{:S(2)}, u32[]{:S(2)}) collective-permute-start(f32[48,128]{1,0:T(8,128)S(1)} %get-tuple-element.21.own_edge_ref), channel_id=1, source_target_pairs={{0,128},{128,0},{1,129},{129,1},{2,130},{130,2},{3,131},{131,3},{4... | collective-permute-start | bytes 73736 | tf_op jit(solution)/shard_map/ppermute | solution.py:346
  5.2 0.1 collective-permute-start.1
  5.3 1.1 %collective-permute-done.other_edge_ref.edge_ref = f32[48,128]{1,0:T(8,128)S(1)} collective-permute-done((f32[48,128]{1,0:T(8,128)S(1)}, f32[48,128]{1,0:T(8,128)S(1)}, u32[]{:S(2)}, u32[]{:S(2)}) %collective-permute-start) | collective-permute-done | bytes 24608 | tf_op jit(solution)/shard_map/ppermute | solution.py:346
  6.4 4.1 %collective-permute-start.2 = (f32[48,128]{1,0:T(8,128)S(1)}, f32[48,128]{1,0:T(8,128)S(1)}, u32[]{:S(2)}, u32[]{:S(2)}) collective-permute-start(f32[48,128]{1,0:T(8,128)S(1)} %get-tuple-element.23), channel_id=1, source_target_pairs={{0,16},{16,0},{1,17},{17,1},{2,18},{18,2},{3,19},{19,3},{4,20},{20... | collective-permute-start | bytes 73736 | tf_op jit(solution)/shard_map/ppermute | solution.py:360
  10.5 1.9 %collective-permute-start.3 = (f32[48,128]{1,0:T(8,128)S(1)}, f32[48,128]{1,0:T(8,128)S(1)}, u32[]{:S(2)}, u32[]{:S(2)}) collective-permute-start(f32[48,128]{1,0:T(8,128)S(1)} %get-tuple-element.24), channel_id=1, source_target_pairs={{16,32},{32,16},{48,64},{64,48},{80,96},{96,80},{17,33},{33,17},{4... | collective-permute-start | bytes 73736 | tf_op jit(solution)/shard_map/ppermute | solution.py:359
  12.5 0.0 copy-done
  12.5 4.3 %shard_map.71 = (f32[72,128]{1,0:T(8,128)S(1)}, bf16[36,128,16]{2,1,0:T(8,128)(2,1)S(1)}, f32[1152,128]{1,0:T(8,128)S(1)}, f32[36,128]{1,0:T(8,128)S(1)}, bf16[36,16,128]{2,1,0:T(8,128)(2,1)S(1)}) custom-call(s32[36,1,26]{2,1,0:T(1,128)S(1)} %bitcast.11, f32[144,128]{1,0:T(8,128)S(1)} %get-tuple-element.27.own_ref), custom_call_target="tpu_custom_call" | custom-call | flops 2400000000 | bytes 65536 | tf_op jit(solution)/shard_map/pallas_call | solution.py:349
  16.7 0.0 collective-permute-done.2.core_ref
  16.7 0.0 collective-permute-done.3.far_ref
  16.7 0.0 collective-permute-done.1.other_mid_ref.mid_ref
  16.8 0.5 collective-permute-start.4
  17.3 0.8 %collective-permute-start.5 = (f32[64,128]{1,0:T(8,128)S(1)}, f32[64,128]{1,0:T(8,128)S(1)}, u32[]{:S(2)}, u32[]{:S(2)}) collective-permute-start(f32[64,128]{1,0:T(8,128)S(1)} %get-tuple-element.26), channel_id=1, source_target_pairs={{1,2},{2,1},{3,4},{4,3},{5,6},{6,5},{7,8},{8,7},{9,10},{10,9},{11,... | collective-permute-start | bytes 98312 | tf_op jit(solution)/shard_map/ppermute | solution.py:365
  18.2 1.7 %shard_map.72 = (f32[72,128]{1,0:T(8,128)S(1)}, f32[36,128]{1,0:T(8,128)S(1)}, bf16[36,16,128]{2,1,0:T(8,128)(2,1)S(1)}) custom-call(f32[48,128]{1,0:T(8,128)S(1)} %collective-permute-done.other_edge_ref.edge_ref, f32[96,128]{1,0:T(8,128)S(1)} %collective-permute-done.1.other_mid_ref.mid_ref, bf16[36,128,16]{2,1,0:T(8,128)(2,1)S(1)} %get-tuple-element.28.bcent, ...), custom_call_target="tpu_custom_call" | custom-call | flops 1200000000 | bytes 65536 | tf_op jit(solution)/shard_map/pallas_call | solution.py:361
  19.9 3.7 %shard_map.73.before = f32[72,128]{1,0:T(8,128)S(1)} custom-call(f32[48,128]{1,0:T(8,128)S(1)} %collective-permute-done.2.core_ref, f32[48,128]{1,0:T(8,128)S(1)} %collective-permute-done.3.far_ref, bf16[36,128,16]{2,1,0:T(8,128)(2,1)S(1)} %get-tuple-element.28.bcent, f32[1152,128]{1,0:T(8,128)S(1)} %get-tuple-element.29.flags, ...), custom_call_target="tpu_custom_call" | custom-call | flops 1600000000 | bytes 65536 | tf_op jit(solution)/shard_map/pallas_call | solution.py:367
  23.6 0.0 copy-start.1
  23.6 0.0 collective-permute-done.4.near_ref
  23.6 0.0 collective-permute-done.5.far_ref
  23.6 1.3 %shard_map.74 = (f32[36,128]{1,0:T(8,128)S(1)}, f32[8,128]{1,0:T(8,128)S(1)}) custom-call(f32[64,128]{1,0:T(8,128)S(1)} %collective-permute-done.4.near_ref, f32[64,128]{1,0:T(8,128)S(1)} %collective-permute-done.5.far_ref, bf16[36,128,16]{2,1,0:T(8,128)(2,1)S(1)} %get-tuple-element.28.bcent, f32[1152,128]{1,0:T(8,128)S(1)} %get-tuple-element.29.flags, ...), custom_call_target="tpu_custom_call" | custom-call | flops 800000000 | bytes 65536 | tf_op jit(solution)/shard_map/pallas_call | solution.py:370
  24.9 0.1 broadcast_in_dim.2
  25.0 28.9 %all_to_all.8 = f32[256,1,128]{2,1,0:T(1,128)S(1)} all-to-all(f32[256,1,128]{2,1,0:T(1,128)S(1)} %broadcast_in_dim.2), channel_id=1, replica_groups=mesh['ply'=2,'y'=4,'core'=2,'z'=8,'xlo'=2] {'ply','y','core','z','xlo'}, dimensions={0} | all-to-all | bytes 262144 | tf_op jit(solution)/shard_map/all_to_all | solution.py:374
  53.9 0.0 copy-done.1
  53.9 0.8 %shard_map.75 = (f32[36,1,128]{2,1,0:T(1,128)}, f32[36,1,128]{2,1,0:T(1,128)}) custom-call(f32[256,128]{1,0:T(8,128)S(1)} %bitcast.10, f32[36,128]{1,0:T(8,128)S(1)} %get-tuple-element.37.avg_ref, f32[36,1,128]{2,1,0:T(1,128)S(1)} %bitcast.12, f32[144,128]{1,0:T(8,128)S(1)} %get-tuple-element.27.own_ref), custom_call_target="tpu_custom_call" | custom-call | flops 400000000 | bytes 65536 | tf_op jit(solution)/shard_map/pallas_call | solution.py:375
  (3 shorter events, 0.1 us)
Async XLA Ops:
  0.6 11.8 %copy-start = (s32[1,6,6,26]{3,0,2,1:T(1,128)S(1)}, s32[1,6,6,26]{3,0,2,1:T(1,128)}, u32[]{:S(2)}) copy-start(s32[1,6,6,26]{3,0,2,1:T(1,128)} %param.9) | copy-start | bytes 11236
  1.6 4.9 %collective-permute-start = (f32[48,128]{1,0:T(8,128)S(1)}, f32[48,128]{1,0:T(8,128)S(1)}, u32[]{:S(2)}, u32[]{:S(2)}) collective-permute-start(f32[48,128]{1,0:T(8,128)S(1)} %get-tuple-element.21.own_edge_ref), channel_id=1, source_target_pairs={{0,128},{128,0},{1,129},{129,1},{2,130},{130,2},{3,131},{131,3},{4... | collective-permute-start | bytes 73736 | tf_op jit(solution)/shard_map/ppermute | solution.py:346
  5.2 11.5 %collective-permute-start.1 = (f32[96,128]{1,0:T(8,128)S(1)}, f32[96,128]{1,0:T(8,128)S(1)}, u32[]{:S(2)}, u32[]{:S(2)}) collective-permute-start(f32[96,128]{1,0:T(8,128)S(1)} %get-tuple-element.22.own_mid_ref), channel_id=1, source_target_pairs={{0,128},{128,0},{1,129},{129,1},{2,130},{130,2},{3,131},{131,3},{4... | collective-permute-start | bytes 147464 | tf_op jit(solution)/shard_map/ppermute | solution.py:347
  6.4 10.3 %collective-permute-start.2 = (f32[48,128]{1,0:T(8,128)S(1)}, f32[48,128]{1,0:T(8,128)S(1)}, u32[]{:S(2)}, u32[]{:S(2)}) collective-permute-start(f32[48,128]{1,0:T(8,128)S(1)} %get-tuple-element.23), channel_id=1, source_target_pairs={{0,16},{16,0},{1,17},{17,1},{2,18},{18,2},{3,19},{19,3},{4,20},{20... | collective-permute-start | bytes 73736 | tf_op jit(solution)/shard_map/ppermute | solution.py:360
  10.5 6.2 %collective-permute-start.3 = (f32[48,128]{1,0:T(8,128)S(1)}, f32[48,128]{1,0:T(8,128)S(1)}, u32[]{:S(2)}, u32[]{:S(2)}) collective-permute-start(f32[48,128]{1,0:T(8,128)S(1)} %get-tuple-element.24), channel_id=1, source_target_pairs={{16,32},{32,16},{48,64},{64,48},{80,96},{96,80},{17,33},{33,17},{4... | collective-permute-start | bytes 73736 | tf_op jit(solution)/shard_map/ppermute | solution.py:359
  16.8 6.8 %collective-permute-start.4 = (f32[64,128]{1,0:T(8,128)S(1)}, f32[64,128]{1,0:T(8,128)S(1)}, u32[]{:S(2)}, u32[]{:S(2)}) collective-permute-start(f32[64,128]{1,0:T(8,128)S(1)} %get-tuple-element.25), channel_id=1, source_target_pairs={{0,1},{1,0},{2,3},{3,2},{4,5},{5,4},{6,7},{7,6},{8,9},{9,8},{10,11... | collective-permute-start | bytes 98312 | tf_op jit(solution)/shard_map/ppermute | solution.py:366
  17.3 6.3 %collective-permute-start.5 = (f32[64,128]{1,0:T(8,128)S(1)}, f32[64,128]{1,0:T(8,128)S(1)}, u32[]{:S(2)}, u32[]{:S(2)}) collective-permute-start(f32[64,128]{1,0:T(8,128)S(1)} %get-tuple-element.26), channel_id=1, source_target_pairs={{1,2},{2,1},{3,4},{4,3},{5,6},{6,5},{7,8},{8,7},{9,10},{10,9},{11,... | collective-permute-start | bytes 98312 | tf_op jit(solution)/shard_map/ppermute | solution.py:365
  23.6 30.3 %copy-start.1 = (f32[1,6,6,128]{3,0,2,1:T(1,128)S(1)}, f32[1,6,6,128]{3,0,2,1:T(1,128)}, u32[]{:S(2)}) copy-start(f32[1,6,6,128]{3,0,2,1:T(1,128)} %param.7) | copy-start | bytes 55300

commit v7 on v5

--- a/solution.py
+++ b/solution.py
@@ -145,7 +145,7 @@
     return (1 - 2 * lax.axis_index("ply")).astype(F32)
 
 
-def own_kernel(mask_ref, own_ref, acc, bcent, flags, rows, bfeat, turned, cent, feat):
+def own_kernel(mask_ref, own_ref, acc, bcent, flags, turned, cent, feat, rows, bfeat):
     fill_flags(mask_ref, turned, flags)
     for x in range(BX):
         highs, lows, norm, strain = positions(own_ref, x * BY, BY, 1, NB, float(x - BX // 2), y_in(), 0.0)
@@ -160,8 +160,7 @@
     lax.fori_loop(0, NB, turn, 0, unroll=6)
     refs = (bcent, bfeat, rows, flags, acc)
     edges(0, False, *refs)
-    middles(0, 1, BX - 2, False, 3, *refs)
-    acc[pl.ds(2 * (BX - 2) * BY, 2 * BY), :] = jnp.zeros((2 * BY, PTS), F32)
+    middles(0, 1, BX - 1, False, 2, *refs)
 
 
 def other_kernel(other_ref, bcent, flags, before, acc, rows, bfeat, feat):
@@ -176,7 +175,7 @@
 
 
 def x_kernel(
-    core_ref, far_ref, bcent, flags, own_rows, own_bfeat, other_rows, other_bfeat, before, acc, feat, rows, bfeat
+    core_ref, far_ref, bcent, flags, other_rows, other_bfeat, before, acc, feat, rows, bfeat
 ):
     core = lax.axis_index("core")
     for slot, ref in enumerate((core_ref, far_ref)):
@@ -205,7 +204,6 @@
         return carry
 
     lax.fori_loop(0, 2, side, 0, unroll=2)
-    middles(0, BX - 2, BX - 1, True, 1, bcent, own_bfeat, own_rows, flags, acc)
     middles(1, 2, BX - 1, True, 3, bcent, other_bfeat, other_rows, flags, acc)
 
 
@@ -334,11 +332,11 @@
     beside = lambda n: [p for i in range(1, n - 1, 2) for p in ((i, i + 1), (i + 1, i))]
     other = lax.ppermute(own, "ply", swap)
     tile = feature_scratch(NB)
-    acc, bcent, flags, own_rows, own_bfeat = call(
+    acc, bcent, flags = call(
         own_kernel,
-        [SUMS, ((NB, PTS, K), BF16), ((NB * FLAGS, PTS), F32)] + tile[1:],
+        [SUMS, ((NB, PTS, K), BF16), ((NB * FLAGS, PTS), F32)],
         2,
-        [((PTS, PTS), F32), ((NB * K, PTS), F32)] + tile[:1],
+        [((PTS, PTS), F32), ((NB * K, PTS), F32)] + tile,
         6,
     )(pair_mask.reshape(NB, 1, 26), own)
 
@@ -352,9 +350,7 @@
     ynear, yfar = call(columns_kernel, [column, column], 4)(own, other, core, far)
     yfar = lax.ppermute(yfar, ("z", "xlo"), beside(16))
     ynear = lax.ppermute(ynear, "xlo", swap)
-    (acc,) = call(x_kernel, [SUMS], 9, feature_scratch(4 * BY), 4)(
-        core, far, bcent, flags, own_rows, own_bfeat, rows, bfeat, acc
-    )
+    (acc,) = call(x_kernel, [SUMS], 7, feature_scratch(4 * BY), 4)(core, far, bcent, flags, rows, bfeat, acc)
     averaged, top = call(y_kernel, [((NB, PTS), F32), ((8, PTS), F32)], 6, feature_scratch(4 * WX) + [SUMS], 2)(
         ynear, yfar, bcent, flags, own, acc
     )

time: 52.7 us -> 53.6 us (1.017)
  transfers between devices with their start and end apart: 5 -> 5, of which waited for: 1 -> 1; matrix products, arithmetic and copies ran while one was open for 0% -> 0% of each run, Pallas kernels for 18% -> 19%
where the time goes in v7:
time: 53.6 us; the launch traced here: 53.4 us
  blocking collectives  30.4 us (57%)
  Pallas kernels  13.1 us (24%)
  starting transfers between devices  8.85 us (17%)
  between operations  0.73 us (1%)
    all_to_all x1, blocking collectives, on_device(): lax.all_to_all(jnp.broadcast_to(top[:1], (256, PTS)), AXES, 0, 0, tiled=T...  30.4 us
    pallas_call x1, Pallas kernels, on_device(): call(own_kernel, [SUMS, ((NB, PTS, K), BF16), ((NB * FLAGS, PTS), F32)],...  5.3 us
    ppermute x1, starting transfers between devices, on_device(): other = lax.ppermute(own, 'ply', swap)  3.65 us
    ppermute x1, starting transfers between devices, on_device(): far = lax.ppermute(far, ('y', 'core'), beside(8))  3.11 us
    pallas_call x1, Pallas kernels, on_device(): call(x_kernel, [SUMS], 7, feature_scratch(4 * BY), 4)  3.04 us
    pallas_call x1, Pallas kernels, on_device(): call(other_kernel, [SUMS] + tile[1:], 4, tile[:1], 3)  1.76 us
    pallas_call x1, Pallas kernels, on_device(): call(y_kernel, [((NB, PTS), F32), ((8, PTS), F32)], 6, feature_scratch(4...  1.3 us
  transfers between devices with their start and end apart: 5, of which 1 were waited for; matrix products, arithmetic and copies ran while one was open for 0% of the time, Pallas kernels for 19%

profile of v7, /device:TPU:1, one launch (start us, length us, event | category | flops | bytes accessed | tf_op | source)
XLA Modules:
  0.0 53.4 jit_solution(2090642872523234565)
XLA Ops:
  0.6 0.0 copy-start
  0.6 0.9 %shard_map.68.own_ref = f32[144,128]{1,0:T(8,128)S(1)} custom-call(s32[6,1,6]{2,1,0:T(1,128)} %bitcast.15, f32[108,1,128]{2,1,0:T(1,128)} %bitcast.13, f32[36,1,128]{2,1,0:T(1,128)} %bitcast.14), custom_call_target="tpu_custom_call" | custom-call | flops 400000000 | bytes 65536 | tf_op jit(solution)/shard_map/pallas_call | solution.py:319
  1.6 3.6 %collective-permute-start = (f32[144,128]{1,0:T(8,128)S(1)}, f32[144,128]{1,0:T(8,128)S(1)}, u32[]{:S(2)}, u32[]{:S(2)}) collective-permute-start(f32[144,128]{1,0:T(8,128)S(1)} %shard_map.68.own_ref), channel_id=1, source_target_pairs={{0,128},{128,0},{1,129},{129,1},{2,130},{130,2},{3,131},{131,3},{4... | collective-permute-start | bytes 221192 | tf_op jit(solution)/shard_map/ppermute | solution.py:333
  5.2 0.0 copy-done
  5.2 5.3 %shard_map.71 = (f32[72,128]{1,0:T(8,128)S(1)}, bf16[36,128,16]{2,1,0:T(8,128)(2,1)S(1)}, f32[1152,128]{1,0:T(8,128)S(1)}) custom-call(s32[36,1,26]{2,1,0:T(1,128)S(1)} %bitcast.11, f32[144,128]{1,0:T(8,128)S(1)} %shard_map.68.own_ref), custom_call_target="tpu_custom_call" | custom-call | flops 2400000000 | bytes 65536 | tf_op jit(solution)/shard_map/pallas_call | solution.py:335
  10.5 0.0 collective-permute-done.other_ref
  10.5 1.0 %collective-permute-start.1 = (f32[48,128]{1,0:T(8,128)S(1)}, f32[48,128]{1,0:T(8,128)S(1)}, u32[]{:S(2)}, u32[]{:S(2)}) collective-permute-start(f32[48,128]{1,0:T(8,128)S(1)} %get-tuple-element.16), channel_id=1, source_target_pairs={{0,16},{16,0},{1,17},{17,1},{2,18},{18,2},{3,19},{19,3},{4,20},{20... | collective-permute-start | bytes 73736 | tf_op jit(solution)/shard_map/ppermute | solution.py:346
  11.6 3.1 %collective-permute-start.2 = (f32[48,128]{1,0:T(8,128)S(1)}, f32[48,128]{1,0:T(8,128)S(1)}, u32[]{:S(2)}, u32[]{:S(2)}) collective-permute-start(f32[48,128]{1,0:T(8,128)S(1)} %get-tuple-element.17), channel_id=1, source_target_pairs={{16,32},{32,16},{48,64},{64,48},{80,96},{96,80},{17,33},{33,17},{4... | collective-permute-start | bytes 73736 | tf_op jit(solution)/shard_map/ppermute | solution.py:345
  14.7 1.8 %shard_map.72 = (f32[72,128]{1,0:T(8,128)S(1)}, f32[36,128]{1,0:T(8,128)S(1)}, bf16[36,16,128]{2,1,0:T(8,128)(2,1)S(1)}) custom-call(f32[144,128]{1,0:T(8,128)S(1)} %collective-permute-done.other_ref, bf16[36,128,16]{2,1,0:T(8,128)(2,1)S(1)} %get-tuple-element.20.bcent, f32[1152,128]{1,0:T(8,128)S(1)} %get-tuple-element.21.flags, ...), custom_call_target="tpu_custom_call" | custom-call | flops 1200000000 | bytes 65536 | tf_op jit(solution)/shard_map/pallas_call | solution.py:347
  16.4 0.0 collective-permute-done.1.core_ref
  16.4 0.2 collective-permute-done.2.far_ref
  16.7 0.4 collective-permute-start.3
  17.1 0.7 %collective-permute-start.4 = (f32[64,128]{1,0:T(8,128)S(1)}, f32[64,128]{1,0:T(8,128)S(1)}, u32[]{:S(2)}, u32[]{:S(2)}) collective-permute-start(f32[64,128]{1,0:T(8,128)S(1)} %get-tuple-element.19), channel_id=1, source_target_pairs={{1,2},{2,1},{3,4},{4,3},{5,6},{6,5},{7,8},{8,7},{9,10},{10,9},{11,... | collective-permute-start | bytes 98312 | tf_op jit(solution)/shard_map/ppermute | solution.py:351
  17.8 3.0 %shard_map.73.before = f32[72,128]{1,0:T(8,128)S(1)} custom-call(f32[48,128]{1,0:T(8,128)S(1)} %collective-permute-done.1.core_ref, f32[48,128]{1,0:T(8,128)S(1)} %collective-permute-done.2.far_ref, bf16[36,128,16]{2,1,0:T(8,128)(2,1)S(1)} %get-tuple-element.20.bcent, f32[1152,128]{1,0:T(8,128)S(1)} %get-tuple-element.21.flags, ...), custom_call_target="tpu_custom_call" | custom-call | flops 1600000000 | bytes 65536 | tf_op jit(solution)/shard_map/pallas_call | solution.py:353
  20.8 0.0 copy-start.1
  20.8 0.0 collective-permute-done.3.near_ref
  20.9 0.0 collective-permute-done.4.far_ref
  20.9 1.3 %shard_map.74 = (f32[36,128]{1,0:T(8,128)S(1)}, f32[8,128]{1,0:T(8,128)S(1)}) custom-call(f32[64,128]{1,0:T(8,128)S(1)} %collective-permute-done.3.near_ref, f32[64,128]{1,0:T(8,128)S(1)} %collective-permute-done.4.far_ref, bf16[36,128,16]{2,1,0:T(8,128)(2,1)S(1)} %get-tuple-element.20.bcent, f32[1152,128]{1,0:T(8,128)S(1)} %get-tuple-element.21.flags, ...), custom_call_target="tpu_custom_call" | custom-call | flops 800000000 | bytes 65536 | tf_op jit(solution)/shard_map/pallas_call | solution.py:354
  22.2 0.1 broadcast_in_dim.2
  22.3 30.4 %all_to_all.8 = f32[256,1,128]{2,1,0:T(1,128)S(1)} all-to-all(f32[256,1,128]{2,1,0:T(1,128)S(1)} %broadcast_in_dim.2), channel_id=1, replica_groups=mesh['ply'=2,'y'=4,'core'=2,'z'=8,'xlo'=2] {'ply','y','core','z','xlo'}, dimensions={0} | all-to-all | bytes 262144 | tf_op jit(solution)/shard_map/all_to_all | solution.py:358
  52.6 0.0 copy-done.1
  52.6 0.8 %shard_map.75 = (f32[36,1,128]{2,1,0:T(1,128)}, f32[36,1,128]{2,1,0:T(1,128)}) custom-call(f32[256,128]{1,0:T(8,128)S(1)} %bitcast.10, f32[36,128]{1,0:T(8,128)S(1)} %get-tuple-element.27.avg_ref, f32[36,1,128]{2,1,0:T(1,128)S(1)} %bitcast.12, f32[144,128]{1,0:T(8,128)S(1)} %shard_map.68.own_ref), custom_call_target="tpu_custom_call" | custom-call | flops 400000000 | bytes 65536 | tf_op jit(solution)/shard_map/pallas_call | solution.py:359
  (3 shorter events, 0.0 us)
Async XLA Ops:
  0.6 4.6 %copy-start = (s32[1,6,6,26]{3,0,2,1:T(1,128)S(1)}, s32[1,6,6,26]{3,0,2,1:T(1,128)}, u32[]{:S(2)}) copy-start(s32[1,6,6,26]{3,0,2,1:T(1,128)} %param.9) | copy-start | bytes 11236
  1.6 9.0 %collective-permute-start = (f32[144,128]{1,0:T(8,128)S(1)}, f32[144,128]{1,0:T(8,128)S(1)}, u32[]{:S(2)}, u32[]{:S(2)}) collective-permute-start(f32[144,128]{1,0:T(8,128)S(1)} %shard_map.68.own_ref), channel_id=1, source_target_pairs={{0,128},{128,0},{1,129},{129,1},{2,130},{130,2},{3,131},{131,3},{4... | collective-permute-start | bytes 221192 | tf_op jit(solution)/shard_map/ppermute | solution.py:333
  10.5 5.9 %collective-permute-start.1 = (f32[48,128]{1,0:T(8,128)S(1)}, f32[48,128]{1,0:T(8,128)S(1)}, u32[]{:S(2)}, u32[]{:S(2)}) collective-permute-start(f32[48,128]{1,0:T(8,128)S(1)} %get-tuple-element.16), channel_id=1, source_target_pairs={{0,16},{16,0},{1,17},{17,1},{2,18},{18,2},{3,19},{19,3},{4,20},{20... | collective-permute-start | bytes 73736 | tf_op jit(solution)/shard_map/ppermute | solution.py:346
  11.6 5.1 %collective-permute-start.2 = (f32[48,128]{1,0:T(8,128)S(1)}, f32[48,128]{1,0:T(8,128)S(1)}, u32[]{:S(2)}, u32[]{:S(2)}) collective-permute-start(f32[48,128]{1,0:T(8,128)S(1)} %get-tuple-element.17), channel_id=1, source_target_pairs={{16,32},{32,16},{48,64},{64,48},{80,96},{96,80},{17,33},{33,17},{4... | collective-permute-start | bytes 73736 | tf_op jit(solution)/shard_map/ppermute | solution.py:345
  16.7 4.1 %collective-permute-start.3 = (f32[64,128]{1,0:T(8,128)S(1)}, f32[64,128]{1,0:T(8,128)S(1)}, u32[]{:S(2)}, u32[]{:S(2)}) collective-permute-start(f32[64,128]{1,0:T(8,128)S(1)} %get-tuple-element.18), channel_id=1, source_target_pairs={{0,1},{1,0},{2,3},{3,2},{4,5},{5,4},{6,7},{7,6},{8,9},{9,8},{10,11... | collective-permute-start | bytes 98312 | tf_op jit(solution)/shard_map/ppermute | solution.py:352
  17.1 3.7 %collective-permute-start.4 = (f32[64,128]{1,0:T(8,128)S(1)}, f32[64,128]{1,0:T(8,128)S(1)}, u32[]{:S(2)}, u32[]{:S(2)}) collective-permute-start(f32[64,128]{1,0:T(8,128)S(1)} %get-tuple-element.19), channel_id=1, source_target_pairs={{1,2},{2,1},{3,4},{4,3},{5,6},{6,5},{7,8},{8,7},{9,10},{10,9},{11,... | collective-permute-start | bytes 98312 | tf_op jit(solution)/shard_map/ppermute | solution.py:351
  20.8 31.8 %copy-start.1 = (f32[1,6,6,128]{3,0,2,1:T(1,128)S(1)}, f32[1,6,6,128]{3,0,2,1:T(1,128)}, u32[]{:S(2)}) copy-start(f32[1,6,6,128]{3,0,2,1:T(1,128)} %param.7) | copy-start | bytes 55300

commit v8 on v7

--- a/solution.py
+++ b/solution.py
@@ -151,27 +151,27 @@
         highs, lows, norm, strain = positions(own_ref, x * BY, BY, 1, NB, float(x - BX // 2), y_in(), 0.0)
         put_neighbour(feat, rows, x * BY, highs, lows, norm, strain)
         put_center(cent, x * BY, highs, lows, norm)
-    round_tiles(feat, bfeat, NB, 6)
+    round_tiles(feat, bfeat, NB, 12)
 
     def turn(a, carry):
         bcent[a] = cent[pl.ds(pl.multiple_of(a * K, K), K), :].T.astype(BF16)
         return carry
 
-    lax.fori_loop(0, NB, turn, 0, unroll=6)
+    lax.fori_loop(0, NB, turn, 0, unroll=NB)
     refs = (bcent, bfeat, rows, flags, acc)
     edges(0, False, *refs)
-    middles(0, 1, BX - 1, False, 2, *refs)
+    middles(0, 1, BX - 1, False, 4, *refs)
 
 
 def other_kernel(other_ref, bcent, flags, before, acc, rows, bfeat, feat):
     for x in range(BX):
         highs, lows, norm, strain = positions(other_ref, x * BY, BY, 1, NB, float(x - BX // 2), y_in(), other_shift())
         put_neighbour(feat, rows, x * BY, highs, lows, norm, strain)
-    round_tiles(feat, bfeat, NB, 6)
+    round_tiles(feat, bfeat, NB, 12)
     acc[...] = before[...]
     refs = (bcent, bfeat, rows, flags, acc)
     edges(1, True, *refs)
-    middles(1, 1, 2, True, 1, *refs)
+    middles(1, 1, 3, True, 2, *refs)
 
 
 def x_kernel(
@@ -204,7 +204,7 @@
         return carry
 
     lax.fori_loop(0, 2, side, 0, unroll=2)
-    middles(1, 2, BX - 1, True, 3, bcent, other_bfeat, other_rows, flags, acc)
+    middles(1, 3, BX - 1, True, 2, bcent, other_bfeat, other_rows, flags, acc)
 
 
 def y_kernel(near_ref, far_ref, bcent, flags, own_ref, before, avg_ref, top_ref, feat, rows, bfeat, acc):

time: 53.6 us -> 52.9 us (0.987)
  Pallas kernels: 13.1 us -> 12.4 us
    pallas_call x1, Pallas kernels: 5.3 us -> 4.58 us  [on_device(): call(own_kernel, [SUMS, ((NB, PTS, K), BF16), ((NB * FLAGS, PTS), F32)],...]
    pallas_call x1, Pallas kernels: 3.04 us -> 2.38 us  [on_device(): call(x_kernel, [SUMS], 7, feature_scratch(4 * BY), 4)]
    pallas_call x1, Pallas kernels: 1.76 us -> 2.39 us  [on_device(): call(other_kernel, [SUMS] + tile[1:], 4, tile[:1], 3)]
  transfers between devices with their start and end apart: 5 -> 5, of which waited for: 1 -> 0; matrix products, arithmetic and copies ran while one was open for 0% -> 0% of each run, Pallas kernels for 19% -> 18%
where the time goes in v8:
time: 52.9 us; the launch traced here: 52.7 us
  blocking collectives  30.6 us (58%)
  Pallas kernels  12.4 us (23%)
  starting transfers between devices  8.85 us (17%)
  between operations  0.75 us (1%)
    all_to_all x1, blocking collectives, on_device(): lax.all_to_all(jnp.broadcast_to(top[:1], (256, PTS)), AXES, 0, 0, tiled=T...  30.6 us
    pallas_call x1, Pallas kernels, on_device(): call(own_kernel, [SUMS, ((NB, PTS, K), BF16), ((NB * FLAGS, PTS), F32)],...  4.58 us
    ppermute x1, starting transfers between devices, on_device(): other = lax.ppermute(own, 'ply', swap)  3.65 us
    ppermute x1, starting transfers between devices, on_device(): far = lax.ppermute(far, ('y', 'core'), beside(8))  3.11 us
    pallas_call x1, Pallas kernels, on_device(): call(other_kernel, [SUMS] + tile[1:], 4, tile[:1], 3)  2.39 us
    pallas_call x1, Pallas kernels, on_device(): call(x_kernel, [SUMS], 7, feature_scratch(4 * BY), 4)  2.38 us
    pallas_call x1, Pallas kernels, on_device(): call(y_kernel, [((NB, PTS), F32), ((8, PTS), F32)], 6, feature_scratch(4...  1.29 us
  transfers between devices with their start and end apart: 5, of which 0 were waited for; matrix products, arithmetic and copies ran while one was open for 0% of the time, Pallas kernels for 18%

profile of v8, /device:TPU:1, one launch (start us, length us, event | category | flops | bytes accessed | tf_op | source)
XLA Modules:
  0.0 52.7 jit_solution(14882265410538473671)
XLA Ops:
  0.6 0.0 copy-start
  0.6 0.9 %shard_map.68.own_ref = f32[144,128]{1,0:T(8,128)S(1)} custom-call(s32[6,1,6]{2,1,0:T(1,128)} %bitcast.15, f32[108,1,128]{2,1,0:T(1,128)} %bitcast.13, f32[36,1,128]{2,1,0:T(1,128)} %bitcast.14), custom_call_target="tpu_custom_call" | custom-call | flops 400000000 | bytes 65536 | tf_op jit(solution)/shard_map/pallas_call | solution.py:319
  1.6 3.6 %collective-permute-start = (f32[144,128]{1,0:T(8,128)S(1)}, f32[144,128]{1,0:T(8,128)S(1)}, u32[]{:S(2)}, u32[]{:S(2)}) collective-permute-start(f32[144,128]{1,0:T(8,128)S(1)} %shard_map.68.own_ref), channel_id=1, source_target_pairs={{0,128},{128,0},{1,129},{129,1},{2,130},{130,2},{3,131},{131,3},{4... | collective-permute-start | bytes 221192 | tf_op jit(solution)/shard_map/ppermute | solution.py:333
  5.2 0.0 copy-done
  5.2 4.6 %shard_map.71 = (f32[72,128]{1,0:T(8,128)S(1)}, bf16[36,128,16]{2,1,0:T(8,128)(2,1)S(1)}, f32[1152,128]{1,0:T(8,128)S(1)}) custom-call(s32[36,1,26]{2,1,0:T(1,128)S(1)} %bitcast.11, f32[144,128]{1,0:T(8,128)S(1)} %shard_map.68.own_ref), custom_call_target="tpu_custom_call" | custom-call | flops 2400000000 | bytes 65536 | tf_op jit(solution)/shard_map/pallas_call | solution.py:335
  9.8 0.0 collective-permute-done.other_ref
  9.8 1.0 %collective-permute-start.1 = (f32[48,128]{1,0:T(8,128)S(1)}, f32[48,128]{1,0:T(8,128)S(1)}, u32[]{:S(2)}, u32[]{:S(2)}) collective-permute-start(f32[48,128]{1,0:T(8,128)S(1)} %get-tuple-element.16), channel_id=1, source_target_pairs={{0,16},{16,0},{1,17},{17,1},{2,18},{18,2},{3,19},{19,3},{4,20},{20... | collective-permute-start | bytes 73736 | tf_op jit(solution)/shard_map/ppermute | solution.py:346
  10.9 3.1 %collective-permute-start.2 = (f32[48,128]{1,0:T(8,128)S(1)}, f32[48,128]{1,0:T(8,128)S(1)}, u32[]{:S(2)}, u32[]{:S(2)}) collective-permute-start(f32[48,128]{1,0:T(8,128)S(1)} %get-tuple-element.17), channel_id=1, source_target_pairs={{16,32},{32,16},{48,64},{64,48},{80,96},{96,80},{17,33},{33,17},{4... | collective-permute-start | bytes 73736 | tf_op jit(solution)/shard_map/ppermute | solution.py:345
  14.0 2.4 %shard_map.72 = (f32[72,128]{1,0:T(8,128)S(1)}, f32[36,128]{1,0:T(8,128)S(1)}, bf16[36,16,128]{2,1,0:T(8,128)(2,1)S(1)}) custom-call(f32[144,128]{1,0:T(8,128)S(1)} %collective-permute-done.other_ref, bf16[36,128,16]{2,1,0:T(8,128)(2,1)S(1)} %get-tuple-element.20.bcent, f32[1152,128]{1,0:T(8,128)S(1)} %get-tuple-element.21.flags, ...), custom_call_target="tpu_custom_call" | custom-call | flops 1200000000 | bytes 65536 | tf_op jit(solution)/shard_map/pallas_call | solution.py:347
  16.4 0.0 collective-permute-done.1.core_ref
  16.4 0.0 collective-permute-done.2.far_ref
  16.4 0.4 collective-permute-start.3
  16.8 0.7 %collective-permute-start.4 = (f32[64,128]{1,0:T(8,128)S(1)}, f32[64,128]{1,0:T(8,128)S(1)}, u32[]{:S(2)}, u32[]{:S(2)}) collective-permute-start(f32[64,128]{1,0:T(8,128)S(1)} %get-tuple-element.19), channel_id=1, source_target_pairs={{1,2},{2,1},{3,4},{4,3},{5,6},{6,5},{7,8},{8,7},{9,10},{10,9},{11,... | collective-permute-start | bytes 98312 | tf_op jit(solution)/shard_map/ppermute | solution.py:351
  17.5 2.4 %shard_map.73.before = f32[72,128]{1,0:T(8,128)S(1)} custom-call(f32[48,128]{1,0:T(8,128)S(1)} %collective-permute-done.1.core_ref, f32[48,128]{1,0:T(8,128)S(1)} %collective-permute-done.2.far_ref, bf16[36,128,16]{2,1,0:T(8,128)(2,1)S(1)} %get-tuple-element.20.bcent, f32[1152,128]{1,0:T(8,128)S(1)} %get-tuple-element.21.flags, ...), custom_call_target="tpu_custom_call" | custom-call | flops 1600000000 | bytes 65536 | tf_op jit(solution)/shard_map/pallas_call | solution.py:353
  19.9 0.0 copy-start.1
  19.9 0.0 collective-permute-done.3.near_ref
  19.9 0.0 collective-permute-done.4.far_ref
  19.9 1.3 %shard_map.74 = (f32[36,128]{1,0:T(8,128)S(1)}, f32[8,128]{1,0:T(8,128)S(1)}) custom-call(f32[64,128]{1,0:T(8,128)S(1)} %collective-permute-done.3.near_ref, f32[64,128]{1,0:T(8,128)S(1)} %collective-permute-done.4.far_ref, bf16[36,128,16]{2,1,0:T(8,128)(2,1)S(1)} %get-tuple-element.20.bcent, f32[1152,128]{1,0:T(8,128)S(1)} %get-tuple-element.21.flags, ...), custom_call_target="tpu_custom_call" | custom-call | flops 800000000 | bytes 65536 | tf_op jit(solution)/shard_map/pallas_call | solution.py:354
  21.2 0.1 broadcast_in_dim.2
  21.3 30.6 %all_to_all.8 = f32[256,1,128]{2,1,0:T(1,128)S(1)} all-to-all(f32[256,1,128]{2,1,0:T(1,128)S(1)} %broadcast_in_dim.2), channel_id=1, replica_groups=mesh['ply'=2,'y'=4,'core'=2,'z'=8,'xlo'=2] {'ply','y','core','z','xlo'}, dimensions={0} | all-to-all | bytes 262144 | tf_op jit(solution)/shard_map/all_to_all | solution.py:358
  51.9 0.0 copy-done.1
  51.9 0.8 %shard_map.75 = (f32[36,1,128]{2,1,0:T(1,128)}, f32[36,1,128]{2,1,0:T(1,128)}) custom-call(f32[256,128]{1,0:T(8,128)S(1)} %bitcast.10, f32[36,128]{1,0:T(8,128)S(1)} %get-tuple-element.27.avg_ref, f32[36,1,128]{2,1,0:T(1,128)S(1)} %bitcast.12, f32[144,128]{1,0:T(8,128)S(1)} %shard_map.68.own_ref), custom_call_target="tpu_custom_call" | custom-call | flops 400000000 | bytes 65536 | tf_op jit(solution)/shard_map/pallas_call | solution.py:359
  (3 shorter events, 0.1 us)
Async XLA Ops:
  0.6 4.6 %copy-start = (s32[1,6,6,26]{3,0,2,1:T(1,128)S(1)}, s32[1,6,6,26]{3,0,2,1:T(1,128)}, u32[]{:S(2)}) copy-start(s32[1,6,6,26]{3,0,2,1:T(1,128)} %param.9) | copy-start | bytes 11236
  1.6 8.2 %collective-permute-start = (f32[144,128]{1,0:T(8,128)S(1)}, f32[144,128]{1,0:T(8,128)S(1)}, u32[]{:S(2)}, u32[]{:S(2)}) collective-permute-start(f32[144,128]{1,0:T(8,128)S(1)} %shard_map.68.own_ref), channel_id=1, source_target_pairs={{0,128},{128,0},{1,129},{129,1},{2,130},{130,2},{3,131},{131,3},{4... | collective-permute-start | bytes 221192 | tf_op jit(solution)/shard_map/ppermute | solution.py:333
  9.8 6.6 %collective-permute-start.1 = (f32[48,128]{1,0:T(8,128)S(1)}, f32[48,128]{1,0:T(8,128)S(1)}, u32[]{:S(2)}, u32[]{:S(2)}) collective-permute-start(f32[48,128]{1,0:T(8,128)S(1)} %get-tuple-element.16), channel_id=1, source_target_pairs={{0,16},{16,0},{1,17},{17,1},{2,18},{18,2},{3,19},{19,3},{4,20},{20... | collective-permute-start | bytes 73736 | tf_op jit(solution)/shard_map/ppermute | solution.py:346
  10.9 5.5 %collective-permute-start.2 = (f32[48,128]{1,0:T(8,128)S(1)}, f32[48,128]{1,0:T(8,128)S(1)}, u32[]{:S(2)}, u32[]{:S(2)}) collective-permute-start(f32[48,128]{1,0:T(8,128)S(1)} %get-tuple-element.17), channel_id=1, source_target_pairs={{16,32},{32,16},{48,64},{64,48},{80,96},{96,80},{17,33},{33,17},{4... | collective-permute-start | bytes 73736 | tf_op jit(solution)/shard_map/ppermute | solution.py:345
  16.4 3.4 %collective-permute-start.3 = (f32[64,128]{1,0:T(8,128)S(1)}, f32[64,128]{1,0:T(8,128)S(1)}, u32[]{:S(2)}, u32[]{:S(2)}) collective-permute-start(f32[64,128]{1,0:T(8,128)S(1)} %get-tuple-element.18), channel_id=1, source_target_pairs={{0,1},{1,0},{2,3},{3,2},{4,5},{5,4},{6,7},{7,6},{8,9},{9,8},{10,11... | collective-permute-start | bytes 98312 | tf_op jit(solution)/shard_map/ppermute | solution.py:352
  16.8 3.1 %collective-permute-start.4 = (f32[64,128]{1,0:T(8,128)S(1)}, f32[64,128]{1,0:T(8,128)S(1)}, u32[]{:S(2)}, u32[]{:S(2)}) collective-permute-start(f32[64,128]{1,0:T(8,128)S(1)} %get-tuple-element.19), channel_id=1, source_target_pairs={{1,2},{2,1},{3,4},{4,3},{5,6},{6,5},{7,8},{8,7},{9,10},{10,9},{11,... | collective-permute-start | bytes 98312 | tf_op jit(solution)/shard_map/ppermute | solution.py:351
  19.9 32.1 %copy-start.1 = (f32[1,6,6,128]{3,0,2,1:T(1,128)S(1)}, f32[1,6,6,128]{3,0,2,1:T(1,128)}, u32[]{:S(2)}) copy-start(f32[1,6,6,128]{3,0,2,1:T(1,128)} %param.7) | copy-start | bytes 55300
